TPU v7x, 32 devices: a whole 2x2x4 slice. The times are simulated.
32 devices in a mesh: grp: 8 (over z, y), chan: 4 (over x, core).
Axes of the slice: x: 2, y: 2, z: 4, core: 2. Of those that a mesh axis runs over, the one named last changes fastest.
Arguments:
- grad_out: bfloat16 [64, 8, 16, 128], P('grp', 'chan'), may hold values from -6 to 6
- feat_full: bfloat16 [64, 8, 16, 128], P('grp', 'chan'), may hold values from -6 to 6
- filters_full: bfloat16 [3, 3, 3, 128, 128], replicated, may hold values from -0.109375 to 0.109375
- upsample_weight: bfloat16 [2, 2, 2, 512, 128], replicated, may hold values from -0.1875 to 0.1875
- filters_half: bfloat16 [3, 3, 3, 512, 512], P(None, None, None, None, 'chan'), may hold values from -0.0546875 to 0.0546875
Outputs:
- grad_half: bfloat16 [4, 32, 8, 512], P('chan', 'grp')
- taps_grad: float32 [3, 3, 3, 128, 128], P(None, None, None, 'grp', 'chan')
All inputs are finite; a program needn't handle non-finite values.
Results may differ from a plain program's by a relative error of at most 0.0058.
Values may be sent and summed in bfloat16 or wider, within the bound.
No kernel may reach another device: no remote copies, remote signals or barrier semaphores. Data moves between devices by JAX's collectives and lax.ppermute only.
A program may use at most 64 MiB of HBM per device.

v0:
```python
import jax
import jax.numpy as jnp
from jax import lax
from jax.experimental import pallas as pl
from jax.experimental.pallas import tpu as pltpu
from jax.sharding import PartitionSpec as P


F32 = jnp.float32
BF16 = jnp.bfloat16
LIMIT = 20 * 2**20
HALO = 3
NT = (((1,), (1,)), ((), ()))
NN = (((1,), (0,)), ((), ()))


def dot(a, b, dims):
    return lax.dot_general(a, b, dims, preferred_element_type=F32)


def swap(value, axis, k):
    n = lax.axis_size(axis)
    return lax.ppermute(value, axis, [(i, i ^ k) for i in range(n)])


def shift(value, axis, step):
    n = lax.axis_size(axis)
    return lax.ppermute(value, axis, [(i, (i + step) % n) for i in range(n)])


def pair(k):
    return jnp.bitwise_xor(lax.axis_index("chan"), k)


def fetch_kernel(*refs):
    count = len(refs) // 2
    arrived = refs[2 * count]
    copies = []
    for k in range(count):
        source, target = refs[k], refs[count + k]
        if source.shape != target.shape:
            width = target.shape[3]
            start = pl.multiple_of(lax.axis_index("chan") * width, width)
            source = source.at[:, :, :, pl.ds(start, width), :]
        copies.append(pltpu.make_async_copy(source, target, arrived.at[k]))
    for copy in copies:
        copy.start()
    for copy in copies:
        copy.wait()


def main_kernel(n, m, *refs):
    bricks, rims, (full_ref, up_ref, half_ref) = (
        refs[:n],
        refs[n : 2 * n],
        refs[2 * n : 2 * n + 3],
    )
    outs, (stage, spread, padded, result, held, arrived) = (
        refs[2 * n + 3 : 3 * n + 3],
        refs[3 * n + 3 :],
    )
    load = pltpu.make_async_copy(half_ref, held, arrived)
    load.start()
    nx, ny, nz, ch = bricks[0].shape
    nx = nx // 2
    halo = rims[0].shape[0] // 2
    rows, half_x, half_z = n * ny, nx // 2, nz // 2
    deep = nx + 2 * halo
    pairs = deep // 2
    half_y = rows // 2
    width = up_ref.shape[3]
    spread[:, :, 0] = jnp.zeros((4, pairs, nz, ch), BF16)
    spread[:, :, rows + 1] = jnp.zeros((4, pairs, nz, ch), BF16)
    level = lax.broadcasted_iota(jnp.int32, (deep * ny, half_z, ch), 1)
    for k in range(n):
        stage[: halo * ny] = rims[k][:halo].astype(F32).reshape(halo * ny, nz, ch)
        stage[halo * ny : (halo + nx) * ny] = bricks[k][:nx].astype(F32).reshape(nx * ny, nz, ch)
        stage[(halo + nx) * ny :] = rims[k][halo:].astype(F32).reshape(halo * ny, nz, ch)
        even = stage[:, pl.ds(0, half_z, stride=2), :]
        odd = stage[:, pl.ds(1, half_z, stride=2), :]
        after = jnp.where(level == half_z - 1, 0.0, pltpu.roll(even, half_z - 1, 1))
        before = jnp.where(level == 0, 0.0, pltpu.roll(odd, 1, 1))
        first = pair(k) * ny + 1
        for which, value in enumerate((even, after, odd, before)):
            value = value.reshape(pairs, 2, ny, half_z, ch)
            for b in range(ny):
                packed = jnp.concatenate([value[:, 0, b], value[:, 1, b]], axis=1)
                spread[which, :, first + b] = packed.astype(BF16)
    taps = jnp.concatenate(
        [
            jnp.concatenate([full_ref[p, q, r] for q in range(3) for r in range(3)], axis=1)
            for p in range(3)
        ],
        axis=0,
    )
    grads = []
    for order in ((2, 0, 3), (1, 2, 0)):
        window = jnp.concatenate(
            [
                spread[which, :, 2 - q : 2 - q + rows].reshape(pairs * rows * nz, ch)
                for q in range(3)
                for which in order
            ],
            axis=1,
        )
        product = dot(window, taps, NT).reshape(pairs, rows, 2, half_z, 3 * ch)
        planes = {}
        for u in range(-2, nx + 2):
            total = None
            for p in range(3):
                x = u - p + 1 + halo
                term = product[x // 2, :, x % 2, :, p * ch : (p + 1) * ch]
                total = term if total is None else total + term
            planes[u] = total.reshape(half_y, 2, half_z, ch)
        grads.append(planes)
    columns = []
    for a in range(2):
        for b in range(2):
            for c in range(2):
                pieces = [
                    grads[c][2 * i + a][:, b].reshape(half_y * half_z, ch)
                    for i in range(-1, half_x + 1)
                ]
                columns.append(jnp.concatenate(pieces, axis=0).astype(BF16))
    up = jnp.concatenate(
        [up_ref[a, b, c] for a in range(2) for b in range(2) for c in range(2)], axis=1
    )
    wide_x = half_x + 2
    coarse = dot(jnp.concatenate(columns, axis=1), up, NT).reshape(wide_x, half_y, half_z, width)
    g = lax.axis_index("grp")
    low = jnp.where(g > 0, 1.0, 0.0)
    high = jnp.where(g < m - 1, 1.0, 0.0)
    padded[:, 0] = jnp.zeros((3, wide_x, half_z, width), F32)
    padded[:, half_y + 1] = jnp.zeros((3, wide_x, half_z, width), F32)
    level = lax.broadcasted_iota(jnp.int32, (half_y, half_z, width), 1)
    for i in range(wide_x):
        plane = coarse[i]
        if i == 0:
            plane = plane * low
        if i == wide_x - 1:
            plane = plane * high
        plane = plane.astype(BF16).astype(F32)
        padded[0, 1 : half_y + 1, i] = jnp.where(
            level == half_z - 1, 0.0, pltpu.roll(plane, half_z - 1, 1)
        )
        padded[1, 1 : half_y + 1, i] = plane
        padded[2, 1 : half_y + 1, i] = jnp.where(level == 0, 0.0, pltpu.roll(plane, 1, 1))
    cells = half_y * half_x * half_z
    total = None
    load.wait()
    for p in range(3):
        windows = [
            padded[r, 2 - q : 2 - q + half_y, 2 - p : 2 - p + half_x]
            .reshape(cells, width)
            .astype(BF16)
            for q in range(3)
            for r in range(3)
        ]
        kernels = [held[p, q, r] for q in range(3) for r in range(3)]
        if width % 128 == 0:
            windows = [jnp.concatenate(windows, axis=1)]
            kernels = [jnp.concatenate(kernels, axis=1)]
        for window, kernel in zip(windows, kernels):
            product = dot(window, kernel, NT)
            total = product if total is None else total + product
    result[...] = total.reshape(result.shape)
    for k in range(n):
        outs[k][...] = result[pair(k)].astype(outs[k].dtype)


def taps_kernel(n, m, *refs):
    bricks, rims, (keep_ref, send_ref, spread, table) = (
        refs[:n],
        refs[n : 2 * n],
        refs[2 * n :],
    )
    nx, ny, nz, ch = bricks[0].shape
    nx = nx // 2
    halo = rims[0].shape[0] // 2
    rows = n * ny
    part = ch // n
    block = ch // m
    spread[:, 0] = jnp.zeros((nx + 2, nz, ch), BF16)
    spread[:, rows + 1] = jnp.zeros((nx + 2, nz, ch), BF16)
    start = lax.axis_index("chan") * part
    source = lax.broadcasted_iota(jnp.int32, (ch, ch), 0)
    target = lax.broadcasted_iota(jnp.int32, (ch, ch), 1)
    copies = (lax.rem(target, part) + start == source) & (target < 3 * part)
    pick = jnp.where(copies, 1.0, 0.0).astype(BF16)
    bits = m.bit_length() - 1
    owner = target // block
    turned = jnp.zeros_like(owner)
    for bit in range(bits):
        turned = turned + (owner // 2**bit % 2) * 2 ** (bits - 1 - bit)
    order = jnp.where(turned * block + lax.rem(target, block) == source, 1.0, 0.0).astype(BF16)
    turned_feats = []
    for k in range(n):
        cells = jnp.concatenate(
            [rims[k][halo - 1 : halo], bricks[k][:nx], rims[k][halo : halo + 1]], axis=0
        )
        cells = cells.reshape((nx + 2) * ny * nz, ch)
        chosen = dot(cells, pick, NN)
        level = lax.rem(lax.broadcasted_iota(jnp.int32, chosen.shape, 0), nz)
        lane = lax.broadcasted_iota(jnp.int32, chosen.shape, 1)
        count = chosen.shape[0]
        above = jnp.where(level == nz - 1, 0.0, pltpu.roll(chosen, count - 1, 0))
        below = jnp.where(level == 0, 0.0, pltpu.roll(chosen, 1, 0))
        mixed = jnp.where(lane < part, above, jnp.where(lane < 2 * part, chosen, below))
        mixed = mixed.astype(BF16).reshape(nx + 2, ny, nz, ch)
        first = pair(k) * ny + 1
        for b in range(ny):
            spread[:, first + b] = mixed[:, b]
        feat = bricks[k][nx:].reshape(nx * ny * nz, ch)
        turned_feats.append(dot(order, feat, NT).astype(BF16))
    for p in range(3):
        total = None
        for k in range(n):
            first = pair(k) * ny
            window = jnp.concatenate(
                [
                    spread[2 - p : 2 - p + nx, pl.ds(first + 2 - q, ny)].reshape(
                        nx * ny * nz, ch
                    )
                    for q in range(3)
                ],
                axis=1,
            )
            product = dot(turned_feats[k], window, NN)
            total = product if total is None else total + product
        table[:, 3 * p * ch : (3 * p + 3) * ch] = total
    half = ch // 2
    bit = lax.rem(lax.axis_index("grp"), 2)
    keep_ref[...] = table[pl.ds(pl.multiple_of(bit * half, half), half), :]
    send_ref[...] = table[pl.ds(pl.multiple_of((1 - bit) * half, half), half), :].astype(BF16)


def load_kernel(grad_ref, feat_ref, own_ref, first_ref, last_ref, arrived):
    nx = grad_ref.shape[0]
    halo = first_ref.shape[0]
    copies = [
        pltpu.make_async_copy(grad_ref.at[pl.ds(nx - halo, halo)], last_ref, arrived.at[0]),
        pltpu.make_async_copy(grad_ref.at[pl.ds(0, halo)], first_ref, arrived.at[1]),
        pltpu.make_async_copy(grad_ref, own_ref.at[pl.ds(0, nx)], arrived.at[2]),
        pltpu.make_async_copy(feat_ref, own_ref.at[pl.ds(nx, nx)], arrived.at[3]),
    ]
    for copy in copies:
        copy.start()
    for copy in copies:
        copy.wait()


def rims_kernel(m, left_ref, right_ref, out_ref):
    g = lax.axis_index("grp")
    halo = left_ref.shape[0]
    left = left_ref[...]
    right = right_ref[...]
    out_ref[:halo] = jnp.where(g > 0, left, jnp.zeros_like(left))
    out_ref[halo:] = jnp.where(g < m - 1, right, jnp.zeros_like(right))


def fold_kernel(bit, keep_ref, got_ref, held_ref, send_ref):
    total = keep_ref[...] + got_ref[...].astype(F32)
    half = held_ref.shape[0]
    upper = lax.rem(lax.axis_index("grp") // 2**bit, 2) == 1
    held_ref[...] = jnp.where(upper, total[half:], total[:half])
    send_ref[...] = jnp.where(upper, total[:half], total[half:]).astype(BF16)


def finish_kernel(keep_ref, got_ref, out_ref):
    part = out_ref.shape[4]
    ch = keep_ref.shape[1] // 9
    total = keep_ref[...] + got_ref[...].astype(F32)
    for p in range(3):
        for q in range(3):
            for r in range(3):
                at = (3 * p + q) * ch + r * part
                out_ref[p, q, r] = total[:, at : at + part]


def sum_kernel(*refs):
    inputs, out_ref = refs[:-1], refs[-1]
    total = inputs[0][...]
    for ref in inputs[1:]:
        total = total + ref[...].astype(F32)
    out_ref[...] = total.astype(BF16)


def call(kernel, outs, scratch, inputs, placed=True, far=0):
    spaces = [pltpu.VMEM] * (len(inputs) - far) + [pltpu.HBM] * far
    return pl.pallas_call(
        kernel,
        out_shape=[pltpu.VMEM(v.shape, v.dtype) if placed else v for v in outs],
        in_specs=[pl.BlockSpec(memory_space=space) for space in spaces],
        out_specs=[pl.BlockSpec(memory_space=pltpu.VMEM)] * len(outs),
        scratch_shapes=scratch,
        compiler_params=pltpu.CompilerParams(vmem_limit_bytes=LIMIT),
    )(*[pltpu.with_memory_space_constraint(v, space) for v, space in zip(inputs, spaces)])


def fetch(weights, shapes):
    count = len(weights)
    return pl.pallas_call(
        fetch_kernel,
        out_shape=[pltpu.VMEM(shape, BF16) for shape in shapes],
        in_specs=[pl.BlockSpec(memory_space=pltpu.HBM)] * count,
        out_specs=[pl.BlockSpec(memory_space=pltpu.VMEM)] * count,
        scratch_shapes=[pltpu.SemaphoreType.DMA((count,))],
        compiler_params=pltpu.CompilerParams(vmem_limit_bytes=LIMIT),
    )(*[pltpu.with_memory_space_constraint(v, pltpu.HBM) for v in weights])


def gather(value):
    held = {0: value}
    k = lax.axis_size("chan") // 2
    while k:
        for j in list(held):
            held[j ^ k] = swap(held[j], "chan", k)
        k //= 2
    return [held[j] for j in sorted(held)]


def work(grad_out, feat_full, filters_full, upsample_weight, filters_half):
    n, m = lax.axis_size("chan"), lax.axis_size("grp")
    nx, ny, nz, ch = grad_out.shape
    half_x, half_y, half_z = nx // 2, n * ny // 2, nz // 2
    width = filters_half.shape[4]
    shape = jax.ShapeDtypeStruct
    edge = shape((HALO, ny, nz, ch), BF16)
    own, first, last = call(
        load_kernel,
        [shape((2 * nx, ny, nz, ch), BF16), edge, edge],
        [pltpu.SemaphoreType.DMA((4,))],
        (grad_out, feat_full),
        far=2,
    )
    from_left = shift(last, "grp", 1)
    from_right = shift(first, "grp", -1)
    bricks = gather(own)
    (rim,) = call(
        lambda *refs: rims_kernel(m, *refs),
        [shape((2 * HALO, ny, nz, ch), BF16)],
        [],
        (from_left, from_right),
    )
    rims = gather(rim)
    up = upsample_weight.shape[:3] + (width, ch)
    full, up = fetch((filters_full, upsample_weight), (filters_full.shape, up))
    keep, send = call(
        lambda *refs: taps_kernel(n, m, *refs),
        [shape((ch // 2, 9 * ch), F32), shape((ch // 2, 9 * ch), BF16)],
        [
            pltpu.VMEM((nx + 2, n * ny + 2, nz, ch), BF16),
            pltpu.VMEM((ch, 9 * ch), F32),
        ],
        (*bricks, *rims),
    )
    got = swap(send, "grp", 1)
    chunk = (half_y // n, half_x, half_z, filters_half.shape[3])
    deep = nx + 2 * HALO
    chunks = call(
        lambda *refs: main_kernel(n, m, *refs),
        [shape(chunk, F32)] + [shape(chunk, BF16)] * (n - 1),
        [
            pltpu.VMEM((deep * ny, nz, ch), F32),
            pltpu.VMEM((4, deep // 2, n * ny + 2, nz, ch), BF16),
            pltpu.VMEM((3, half_y + 2, half_x + 2, half_z, width), F32),
            pltpu.VMEM((n,) + chunk, F32),
            pltpu.VMEM(filters_half.shape, BF16),
            pltpu.SemaphoreType.DMA,
        ],
        (*bricks, *rims, full, up, filters_half),
        far=1,
    )
    parts = [chunks[0]]
    for k in range(1, n):
        parts.append(swap(chunks[k], "chan", k))
    (grad_half,) = call(sum_kernel, [shape(chunk, BF16)], [], parts, False)
    for bit in range(1, m.bit_length() - 1):
        rows = keep.shape[0] // 2
        keep, send = call(
            lambda *refs: fold_kernel(bit, *refs),
            [shape((rows, 9 * ch), F32), shape((rows, 9 * ch), BF16)],
            [],
            (keep, got),
        )
        got = swap(send, "grp", 2**bit)
    (taps_grad,) = call(
        finish_kernel, [shape((3, 3, 3, ch // m, ch // n), F32)], [], (keep, got), False
    )
    return (grad_half, taps_grad)


def solution(mesh):
    in_specs = (
        P("grp", "chan", None, None),
        P("grp", "chan", None, None),
        P(),
        P(),
        P(None, None, None, None, "chan"),
    )
    out_specs = (P("chan", "grp", None, None), P(None, None, None, "grp", "chan"))
    return jax.shard_map(work, mesh=mesh, in_specs=in_specs, out_specs=out_specs, check_vma=False)
```

profile of v0, /device:TPU:0, one launch (start us, length us, event | category | flops | bytes accessed | tf_op | source)
XLA Modules:
  0.0 45.9 jit_solution(6318853476648878792)
XLA Ops:
  0.6 1.0 %shard_map.68 = (bf16[16,2,16,128]{3,2,1,0:T(8,128)(2,1)S(1)}, bf16[3,2,16,128]{3,2,1,0:T(8,128)(2,1)S(1)}, bf16[3,2,16,128]{3,2,1,0:T(8,128)(2,1)S(1)}) custom-call(bf16[8,2,16,128]{3,2,1,0:T(8,128)(2,1)} %grad_ref.1, bf16[8,2,16,128]{3,2,1,0:T(8,128)(2,1)} %feat_ref.1), custom_call_target="tpu_custom_call" | custom-call | tf_op jit(solution)/shard_map/pallas_call | solution.py:290
  1.6 3.0 %collective-permute-start.1 = (bf16[16,2,16,128]{3,2,1,0:T(8,128)(2,1)S(1)}, bf16[16,2,16,128]{3,2,1,0:T(8,128)(2,1)S(1)}, u32[]{:S(2)}, u32[]{:S(2)}) collective-permute-start(bf16[16,2,16,128]{3,2,1,0:T(8,128)(2,1)S(1)} %get-tuple-element.17.refs_0_), channel_id=1, source_target_pairs={{0,2},{1,3},{2,0},{3,1},{4,6},{5,7},{6,4},{7,5},{8,10},{9,11},{10,... | collective-permute-start | bytes 393224 | tf_op jit(solution)/shard_map/ppermute | solution.py:23
  4.6 0.0 collective-permute-start
  4.6 3.5 %collective-permute-done.1.refs_2_ = bf16[16,2,16,128]{3,2,1,0:T(8,128)(2,1)S(1)} collective-permute-done((bf16[16,2,16,128]{3,2,1,0:T(8,128)(2,1)S(1)}, bf16[16,2,16,128]{3,2,1,0:T(8,128)(2,1)S(1)}, u32[]{:S(2)}, u32[]{:S(2)}) %collective-permute-start.1) | collective-permute-done | bytes 131104 | tf_op jit(solution)/shard_map/ppermute | solution.py:23
  8.1 0.0 collective-permute-start.2
  8.1 1.8 %collective-permute-start.3 = (bf16[3,2,16,128]{3,2,1,0:T(8,128)(2,1)S(1)}, bf16[3,2,16,128]{3,2,1,0:T(8,128)(2,1)S(1)}, u32[]{:S(2)}, u32[]{:S(2)}) collective-permute-start(bf16[3,2,16,128]{3,2,1,0:T(8,128)(2,1)S(1)} %get-tuple-element.18), channel_id=1, source_target_pairs={{0,4},{4,8},{8,12},{12,16},{16,20},{20,24},{24,28},{28,0},{1,5},{5... | collective-permute-start | bytes 73736 | tf_op jit(solution)/shard_map/ppermute | solution.py:28
  9.9 3.0 %collective-permute-start.4 = (bf16[3,2,16,128]{3,2,1,0:T(8,128)(2,1)S(1)}, bf16[3,2,16,128]{3,2,1,0:T(8,128)(2,1)S(1)}, u32[]{:S(2)}, u32[]{:S(2)}) collective-permute-start(bf16[3,2,16,128]{3,2,1,0:T(8,128)(2,1)S(1)} %get-tuple-element.19), channel_id=1, source_target_pairs={{0,28},{4,0},{8,4},{12,8},{16,12},{20,16},{24,20},{28,24},{1,29},{... | collective-permute-start | bytes 73736 | tf_op jit(solution)/shard_map/ppermute | solution.py:28
  12.9 1.9 %collective-permute-done.3.refs_0_ = bf16[3,2,16,128]{3,2,1,0:T(8,128)(2,1)S(1)} collective-permute-done((bf16[3,2,16,128]{3,2,1,0:T(8,128)(2,1)S(1)}, bf16[3,2,16,128]{3,2,1,0:T(8,128)(2,1)S(1)}, u32[]{:S(2)}, u32[]{:S(2)}) %collective-permute-start.3) | collective-permute-done | bytes 24608 | tf_op jit(solution)/shard_map/ppermute | solution.py:28
  14.8 0.0 collective-permute-done.4.refs_1_
  14.8 1.6 %collective-permute-start.6 = (bf16[6,2,16,128]{3,2,1,0:T(8,128)(2,1)S(1)}, bf16[6,2,16,128]{3,2,1,0:T(8,128)(2,1)S(1)}, u32[]{:S(2)}, u32[]{:S(2)}) collective-permute-start(bf16[6,2,16,128]{3,2,1,0:T(8,128)(2,1)S(1)} %shard_map.69.refs_4_), channel_id=1, source_target_pairs={{0,2},{1,3},{2,0},{3,1},{4,6},{5,7},{6,4},{7,5},{8,10},{9,11},{10,... | collective-permute-start | bytes 147464 | tf_op jit(solution)/shard_map/ppermute | solution.py:23
  16.5 0.0 collective-permute-start.5
  16.5 2.5 %collective-permute-done.6.refs_6_ = bf16[6,2,16,128]{3,2,1,0:T(8,128)(2,1)S(1)} collective-permute-done((bf16[6,2,16,128]{3,2,1,0:T(8,128)(2,1)S(1)}, bf16[6,2,16,128]{3,2,1,0:T(8,128)(2,1)S(1)}, u32[]{:S(2)}, u32[]{:S(2)}) %collective-permute-start.6) | collective-permute-done | bytes 49184 | tf_op jit(solution)/shard_map/ppermute | solution.py:23
  19.0 0.0 collective-permute-start.7
  19.0 0.0 collective-permute-done.5.refs_5_
  19.0 1.2 %collective-permute-done.7.refs_7_ = bf16[6,2,16,128]{3,2,1,0:T(8,128)(2,1)S(1)} collective-permute-done((bf16[6,2,16,128]{3,2,1,0:T(8,128)(2,1)S(1)}, bf16[6,2,16,128]{3,2,1,0:T(8,128)(2,1)S(1)}, u32[]{:S(2)}, u32[]{:S(2)}) %collective-permute-start.7) | collective-permute-done | bytes 49184 | tf_op jit(solution)/shard_map/ppermute | solution.py:23
  20.2 0.0 collective-permute-done.refs_1_
  20.2 0.0 collective-permute-done.2.refs_3_
  20.2 1.0 %shard_map.73 = (f32[64,1152]{1,0:T(8,128)S(1)}, bf16[64,1152]{1,0:T(8,128)(2,1)S(1)}) custom-call(bf16[16,2,16,128]{3,2,1,0:T(8,128)(2,1)S(1)} %get-tuple-element.17.refs_0_, bf16[16,2,16,128]{3,2,1,0:T(8,128)(2,1)S(1)} %collective-permute-done.refs_1_, bf16[16,2,16,128]{3,2,1,0:T(8,128)(2,1)S(1)} %collective-permute-done.1.refs_2_, ...), custom_call_target="tpu_custom_call" | custom-call | tf_op jit(solution)/shard_map/pallas_call | solution.py:290
  21.3 1.4 %collective-permute-start.11 = (bf16[64,1152]{1,0:T(8,128)(2,1)S(1)}, bf16[64,1152]{1,0:T(8,128)(2,1)S(1)}, u32[]{:S(2)}, u32[]{:S(2)}) collective-permute-start(bf16[64,1152]{1,0:T(8,128)(2,1)S(1)} %get-tuple-element.27), channel_id=1, source_target_pairs={{0,4},{4,0},{8,12},{12,8},{16,20},{20,16},{24,28},{28,24},{1,5},{5... | collective-permute-start | bytes 442376 | tf_op jit(solution)/shard_map/ppermute | solution.py:23
  22.7 4.6 %collective-permute-done.11.refs_1_ = bf16[64,1152]{1,0:T(8,128)(2,1)S(1)} collective-permute-done((bf16[64,1152]{1,0:T(8,128)(2,1)S(1)}, bf16[64,1152]{1,0:T(8,128)(2,1)S(1)}, u32[]{:S(2)}, u32[]{:S(2)}) %collective-permute-start.11) | collective-permute-done | bytes 147488 | tf_op jit(solution)/shard_map/ppermute | solution.py:23
  27.3 1.2 %collective-permute-start.12 = (bf16[32,1152]{1,0:T(8,128)(2,1)S(1)}, bf16[32,1152]{1,0:T(8,128)(2,1)S(1)}, u32[]{:S(2)}, u32[]{:S(2)}) collective-permute-start(bf16[32,1152]{1,0:T(8,128)(2,1)S(1)} %get-tuple-element.29), channel_id=1, source_target_pairs={{0,8},{4,12},{8,0},{12,4},{16,24},{20,28},{24,16},{28,20},{1,9},{5... | collective-permute-start | bytes 221192 | tf_op jit(solution)/shard_map/ppermute | solution.py:23
  28.5 3.2 %collective-permute-done.12.refs_1_ = bf16[32,1152]{1,0:T(8,128)(2,1)S(1)} collective-permute-done((bf16[32,1152]{1,0:T(8,128)(2,1)S(1)}, bf16[32,1152]{1,0:T(8,128)(2,1)S(1)}, u32[]{:S(2)}, u32[]{:S(2)}) %collective-permute-start.12) | collective-permute-done | bytes 73760 | tf_op jit(solution)/shard_map/ppermute | solution.py:23
  31.8 2.2 %collective-permute-start.13 = (bf16[16,1152]{1,0:T(8,128)(2,1)S(1)}, bf16[16,1152]{1,0:T(8,128)(2,1)S(1)}, u32[]{:S(2)}, u32[]{:S(2)}) collective-permute-start(bf16[16,1152]{1,0:T(8,128)(2,1)S(1)} %get-tuple-element.31), channel_id=1, source_target_pairs={{0,16},{4,20},{8,24},{12,28},{16,0},{20,4},{24,8},{28,12},{1,17},{... | collective-permute-start | bytes 110600 | tf_op jit(solution)/shard_map/ppermute | solution.py:23
  34.0 1.2 %shard_map.70 = (bf16[3,3,3,128,128]{4,3,2,1,0:T(8,128)(2,1)S(1)}, bf16[2,2,2,128,128]{4,3,2,1,0:T(8,128)(2,1)S(1)}) custom-call(bf16[3,3,3,128,128]{4,3,2,1,0:T(8,128)(2,1)} %refs_0_.1, bf16[2,2,2,512,128]{4,3,2,1,0:T(8,128)(2,1)} %refs_1_.1), custom_call_target="tpu_custom_call" | custom-call | tf_op jit(solution)/shard_map/pallas_call | solution.py:302
  35.2 4.3 %shard_map.71 = (f32[1,4,8,512]{3,2,1,0:T(8,128)S(1)}, bf16[1,4,8,512]{3,2,1,0:T(8,128)(2,1)S(1)}, bf16[1,4,8,512]{3,2,1,0:T(8,128)(2,1)S(1)}, bf16[1,4,8,512]{3,2,1,0:T(8,128)(2,1)S(1)}) custom-call(bf16[16,2,16,128]{3,2,1,0:T(8,128)(2,1)S(1)} %get-tuple-element.17.refs_0_, bf16[16,2,16,128]{3,2,1,0:T(8,128)(2,1)S(1)} %collective-permute-done.refs_1_, ...), custom_call_target="tpu_custom_call" | custom-call | tf_op jit(solution)/shard_map/pallas_call | solution.py:290
  39.5 0.1 collective-permute-start.8
  39.6 1.5 %collective-permute-start.9 = (bf16[1,4,8,512]{3,2,1,0:T(8,128)(2,1)S(1)}, bf16[1,4,8,512]{3,2,1,0:T(8,128)(2,1)S(1)}, u32[]{:S(2)}, u32[]{:S(2)}) collective-permute-start(bf16[1,4,8,512]{3,2,1,0:T(8,128)(2,1)S(1)} %get-tuple-element.24), channel_id=1, source_target_pairs={{0,2},{1,3},{2,0},{3,1},{4,6},{5,7},{6,4},{7,5},{8,10},{9,11},{10,... | collective-permute-start | bytes 98312 | tf_op jit(solution)/shard_map/ppermute | solution.py:23
  41.1 0.3 collective-permute-start.10
  41.4 0.0 collective-permute-done.8.refs_1_
  41.4 2.1 %collective-permute-done.9.refs_2_ = bf16[1,4,8,512]{3,2,1,0:T(8,128)(2,1)S(1)} collective-permute-done((bf16[1,4,8,512]{3,2,1,0:T(8,128)(2,1)S(1)}, bf16[1,4,8,512]{3,2,1,0:T(8,128)(2,1)S(1)}, u32[]{:S(2)}, u32[]{:S(2)}) %collective-permute-start.9) | collective-permute-done | bytes 32800 | tf_op jit(solution)/shard_map/ppermute | solution.py:23
  43.6 0.9 %collective-permute-done.10.refs_3_ = bf16[1,4,8,512]{3,2,1,0:T(8,128)(2,1)S(1)} collective-permute-done((bf16[1,4,8,512]{3,2,1,0:T(8,128)(2,1)S(1)}, bf16[1,4,8,512]{3,2,1,0:T(8,128)(2,1)S(1)}, u32[]{:S(2)}, u32[]{:S(2)}) %collective-permute-start.10) | collective-permute-done | bytes 32800 | tf_op jit(solution)/shard_map/ppermute | solution.py:23
  44.5 0.6 %shard_map.72 = bf16[1,4,8,512]{3,2,1,0:T(8,128)(2,1)} custom-call(f32[1,4,8,512]{3,2,1,0:T(8,128)S(1)} %get-tuple-element.22.refs_0_, bf16[1,4,8,512]{3,2,1,0:T(8,128)(2,1)S(1)} %collective-permute-done.8.refs_1_, bf16[1,4,8,512]{3,2,1,0:T(8,128)(2,1)S(1)} %collective-permute-done.9.refs_2_, bf16[1,4,8,512]{3,2,1,0:T(8,128)(2,1)S(1)} %collective-permute-done.10.refs_3_), custom_call_target="tpu_custom_call" | custom-call | tf_op jit(solution)/shard_map/pallas_call | solution.py:290
  45.1 0.0 collective-permute-done.13.got_ref
  45.1 0.8 %shard_map.76 = f32[3,3,3,16,32]{4,3,2,1,0:T(8,128)} custom-call(f32[16,1152]{1,0:T(8,128)S(1)} %get-tuple-element.30.keep_ref, bf16[16,1152]{1,0:T(8,128)(2,1)S(1)} %collective-permute-done.13.got_ref), custom_call_target="tpu_custom_call" | custom-call | tf_op jit(solution)/shard_map/pallas_call | solution.py:290
  (3 shorter events, 0.1 us)
Async XLA Ops:
  1.6 6.5 %collective-permute-start.1 = (bf16[16,2,16,128]{3,2,1,0:T(8,128)(2,1)S(1)}, bf16[16,2,16,128]{3,2,1,0:T(8,128)(2,1)S(1)}, u32[]{:S(2)}, u32[]{:S(2)}) collective-permute-start(bf16[16,2,16,128]{3,2,1,0:T(8,128)(2,1)S(1)} %get-tuple-element.17.refs_0_), channel_id=1, source_target_pairs={{0,2},{1,3},{2,0},{3,1},{4,6},{5,7},{6,4},{7,5},{8,10},{9,11},{10,... | collective-permute-start | bytes 393224 | tf_op jit(solution)/shard_map/ppermute | solution.py:23
  4.6 15.6 %collective-permute-start = (bf16[16,2,16,128]{3,2,1,0:T(8,128)(2,1)S(1)}, bf16[16,2,16,128]{3,2,1,0:T(8,128)(2,1)S(1)}, u32[]{:S(2)}, u32[]{:S(2)}) collective-permute-start(bf16[16,2,16,128]{3,2,1,0:T(8,128)(2,1)S(1)} %get-tuple-element.17.refs_0_), channel_id=1, source_target_pairs={{0,1},{1,0},{2,3},{3,2},{4,5},{5,4},{6,7},{7,6},{8,9},{9,8},{10,11... | collective-permute-start | bytes 393224 | tf_op jit(solution)/shard_map/ppermute | solution.py:23
  8.1 12.1 %collective-permute-start.2 = (bf16[16,2,16,128]{3,2,1,0:T(8,128)(2,1)S(1)}, bf16[16,2,16,128]{3,2,1,0:T(8,128)(2,1)S(1)}, u32[]{:S(2)}, u32[]{:S(2)}) collective-permute-start(bf16[16,2,16,128]{3,2,1,0:T(8,128)(2,1)S(1)} %collective-permute-done.1.refs_2_), channel_id=1, source_target_pairs={{0,1},{1,0},{2,3},{3,2},{4,5},{5,4},{6,7},{7,6},{8,9},{9,8},{10,11... | collective-permute-start | bytes 393224 | tf_op jit(solution)/shard_map/ppermute | solution.py:23
  8.1 6.7 %collective-permute-start.3 = (bf16[3,2,16,128]{3,2,1,0:T(8,128)(2,1)S(1)}, bf16[3,2,16,128]{3,2,1,0:T(8,128)(2,1)S(1)}, u32[]{:S(2)}, u32[]{:S(2)}) collective-permute-start(bf16[3,2,16,128]{3,2,1,0:T(8,128)(2,1)S(1)} %get-tuple-element.18), channel_id=1, source_target_pairs={{0,4},{4,8},{8,12},{12,16},{16,20},{20,24},{24,28},{28,0},{1,5},{5... | collective-permute-start | bytes 73736 | tf_op jit(solution)/shard_map/ppermute | solution.py:28
  9.9 4.9 %collective-permute-start.4 = (bf16[3,2,16,128]{3,2,1,0:T(8,128)(2,1)S(1)}, bf16[3,2,16,128]{3,2,1,0:T(8,128)(2,1)S(1)}, u32[]{:S(2)}, u32[]{:S(2)}) collective-permute-start(bf16[3,2,16,128]{3,2,1,0:T(8,128)(2,1)S(1)} %get-tuple-element.19), channel_id=1, source_target_pairs={{0,28},{4,0},{8,4},{12,8},{16,12},{20,16},{24,20},{28,24},{1,29},{... | collective-permute-start | bytes 73736 | tf_op jit(solution)/shard_map/ppermute | solution.py:28
  14.8 4.2 %collective-permute-start.6 = (bf16[6,2,16,128]{3,2,1,0:T(8,128)(2,1)S(1)}, bf16[6,2,16,128]{3,2,1,0:T(8,128)(2,1)S(1)}, u32[]{:S(2)}, u32[]{:S(2)}) collective-permute-start(bf16[6,2,16,128]{3,2,1,0:T(8,128)(2,1)S(1)} %shard_map.69.refs_4_), channel_id=1, source_target_pairs={{0,2},{1,3},{2,0},{3,1},{4,6},{5,7},{6,4},{7,5},{8,10},{9,11},{10,... | collective-permute-start | bytes 147464 | tf_op jit(solution)/shard_map/ppermute | solution.py:23
  16.5 2.5 %collective-permute-start.5 = (bf16[6,2,16,128]{3,2,1,0:T(8,128)(2,1)S(1)}, bf16[6,2,16,128]{3,2,1,0:T(8,128)(2,1)S(1)}, u32[]{:S(2)}, u32[]{:S(2)}) collective-permute-start(bf16[6,2,16,128]{3,2,1,0:T(8,128)(2,1)S(1)} %shard_map.69.refs_4_), channel_id=1, source_target_pairs={{0,1},{1,0},{2,3},{3,2},{4,5},{5,4},{6,7},{7,6},{8,9},{9,8},{10,11... | collective-permute-start | bytes 147464 | tf_op jit(solution)/shard_map/ppermute | solution.py:23
  19.0 1.2 %collective-permute-start.7 = (bf16[6,2,16,128]{3,2,1,0:T(8,128)(2,1)S(1)}, bf16[6,2,16,128]{3,2,1,0:T(8,128)(2,1)S(1)}, u32[]{:S(2)}, u32[]{:S(2)}) collective-permute-start(bf16[6,2,16,128]{3,2,1,0:T(8,128)(2,1)S(1)} %collective-permute-done.6.refs_6_), channel_id=1, source_target_pairs={{0,1},{1,0},{2,3},{3,2},{4,5},{5,4},{6,7},{7,6},{8,9},{9,8},{10,11... | collective-permute-start | bytes 147464 | tf_op jit(solution)/shard_map/ppermute | solution.py:23
  21.3 6.0 %collective-permute-start.11 = (bf16[64,1152]{1,0:T(8,128)(2,1)S(1)}, bf16[64,1152]{1,0:T(8,128)(2,1)S(1)}, u32[]{:S(2)}, u32[]{:S(2)}) collective-permute-start(bf16[64,1152]{1,0:T(8,128)(2,1)S(1)} %get-tuple-element.27), channel_id=1, source_target_pairs={{0,4},{4,0},{8,12},{12,8},{16,20},{20,16},{24,28},{28,24},{1,5},{5... | collective-permute-start | bytes 442376 | tf_op jit(solution)/shard_map/ppermute | solution.py:23
  27.3 4.4 %collective-permute-start.12 = (bf16[32,1152]{1,0:T(8,128)(2,1)S(1)}, bf16[32,1152]{1,0:T(8,128)(2,1)S(1)}, u32[]{:S(2)}, u32[]{:S(2)}) collective-permute-start(bf16[32,1152]{1,0:T(8,128)(2,1)S(1)} %get-tuple-element.29), channel_id=1, source_target_pairs={{0,8},{4,12},{8,0},{12,4},{16,24},{20,28},{24,16},{28,20},{1,9},{5... | collective-permute-start | bytes 221192 | tf_op jit(solution)/shard_map/ppermute | solution.py:23
  31.8 13.4 %collective-permute-start.13 = (bf16[16,1152]{1,0:T(8,128)(2,1)S(1)}, bf16[16,1152]{1,0:T(8,128)(2,1)S(1)}, u32[]{:S(2)}, u32[]{:S(2)}) collective-permute-start(bf16[16,1152]{1,0:T(8,128)(2,1)S(1)} %get-tuple-element.31), channel_id=1, source_target_pairs={{0,16},{4,20},{8,24},{12,28},{16,0},{20,4},{24,8},{28,12},{1,17},{... | collective-permute-start | bytes 110600 | tf_op jit(solution)/shard_map/ppermute | solution.py:23
  39.5 1.9 %collective-permute-start.8 = (bf16[1,4,8,512]{3,2,1,0:T(8,128)(2,1)S(1)}, bf16[1,4,8,512]{3,2,1,0:T(8,128)(2,1)S(1)}, u32[]{:S(2)}, u32[]{:S(2)}) collective-permute-start(bf16[1,4,8,512]{3,2,1,0:T(8,128)(2,1)S(1)} %get-tuple-element.23), channel_id=1, source_target_pairs={{0,1},{1,0},{2,3},{3,2},{4,5},{5,4},{6,7},{7,6},{8,9},{9,8},{10,11... | collective-permute-start | bytes 98312 | tf_op jit(solution)/shard_map/ppermute | solution.py:23
  39.6 4.0 %collective-permute-start.9 = (bf16[1,4,8,512]{3,2,1,0:T(8,128)(2,1)S(1)}, bf16[1,4,8,512]{3,2,1,0:T(8,128)(2,1)S(1)}, u32[]{:S(2)}, u32[]{:S(2)}) collective-permute-start(bf16[1,4,8,512]{3,2,1,0:T(8,128)(2,1)S(1)} %get-tuple-element.24), channel_id=1, source_target_pairs={{0,2},{1,3},{2,0},{3,1},{4,6},{5,7},{6,4},{7,5},{8,10},{9,11},{10,... | collective-permute-start | bytes 98312 | tf_op jit(solution)/shard_map/ppermute | solution.py:23
  41.1 3.4 %collective-permute-start.10 = (bf16[1,4,8,512]{3,2,1,0:T(8,128)(2,1)S(1)}, bf16[1,4,8,512]{3,2,1,0:T(8,128)(2,1)S(1)}, u32[]{:S(2)}, u32[]{:S(2)}) collective-permute-start(bf16[1,4,8,512]{3,2,1,0:T(8,128)(2,1)S(1)} %get-tuple-element.25), channel_id=1, source_target_pairs={{0,3},{1,2},{2,1},{3,0},{4,7},{5,6},{6,5},{7,4},{8,11},{9,10},{10,... | collective-permute-start | bytes 98312 | tf_op jit(solution)/shard_map/ppermute | solution.py:23
where the time goes:
time: 46.1 us; the launch traced here: 45.9 us
  waiting for transfers between devices  20 us (43%)
  starting transfers between devices  16.2 us (35%)
  Pallas kernels  9.01 us (20%)
  between operations  0.7 us (2%)
    ppermute x12, waiting for transfers between devices, swap(): return lax.ppermute(value, axis, [(i, i ^ k) for i in range(n)])  18.1 us
    ppermute x12, starting transfers between devices, swap(): return lax.ppermute(value, axis, [(i, i ^ k) for i in range(n)])  11.4 us
    pallas_call x8, Pallas kernels, call(): pl.pallas_call(kernel, out_shape=[pltpu.VMEM(v.shape, v.dtype) if placed...  7.77 us
    ppermute x2, starting transfers between devices, shift(): return lax.ppermute(value, axis, [(i, (i + step) % n) for i in range(n)])  4.81 us
    ppermute x2, waiting for transfers between devices, shift(): return lax.ppermute(value, axis, [(i, (i + step) % n) for i in range(n)])  1.88 us
    pallas_call x1, Pallas kernels, fetch(): pl.pallas_call(fetch_kernel, out_shape=[pltpu.VMEM(shape, BF16) for shape...  1.23 us
  transfers between devices with their start and end apart: 14, of which 8 were waited for; matrix products, arithmetic and copies ran while one was open for 0% of the time, Pallas kernels for 13%

commit v1 on v0

--- a/solution.py
+++ b/solution.py
@@ -212,6 +212,7 @@
             spread[:, first + b] = mixed[:, b]
         feat = bricks[k][nx:].reshape(nx * ny * nz, ch)
         turned_feats.append(dot(order, feat, NT).astype(BF16))
+    totals = []
     for p in range(3):
         total = None
         for k in range(n):
@@ -227,7 +228,8 @@
             )
             product = dot(turned_feats[k], window, NN)
             total = product if total is None else total + product
-        table[:, 3 * p * ch : (3 * p + 3) * ch] = total
+        totals += [total[:, q * ch : q * ch + 3 * part] for q in range(3)]
+    table[...] = jnp.concatenate(totals, axis=1)
     half = ch // 2
     bit = lax.rem(lax.axis_index("grp"), 2)
     keep_ref[...] = table[pl.ds(pl.multiple_of(bit * half, half), half), :]
@@ -268,12 +270,11 @@
 
 def finish_kernel(keep_ref, got_ref, out_ref):
     part = out_ref.shape[4]
-    ch = keep_ref.shape[1] // 9
     total = keep_ref[...] + got_ref[...].astype(F32)
     for p in range(3):
         for q in range(3):
             for r in range(3):
-                at = (3 * p + q) * ch + r * part
+                at = (9 * p + 3 * q + r) * part
                 out_ref[p, q, r] = total[:, at : at + part]
 
 
@@ -324,6 +325,7 @@
     nx, ny, nz, ch = grad_out.shape
     half_x, half_y, half_z = nx // 2, n * ny // 2, nz // 2
     width = filters_half.shape[4]
+    lanes = 27 * (ch // n)
     shape = jax.ShapeDtypeStruct
     edge = shape((HALO, ny, nz, ch), BF16)
     own, first, last = call(
@@ -347,10 +349,10 @@
     full, up = fetch((filters_full, upsample_weight), (filters_full.shape, up))
     keep, send = call(
         lambda *refs: taps_kernel(n, m, *refs),
-        [shape((ch // 2, 9 * ch), F32), shape((ch // 2, 9 * ch), BF16)],
+        [shape((ch // 2, lanes), F32), shape((ch // 2, lanes), BF16)],
         [
             pltpu.VMEM((nx + 2, n * ny + 2, nz, ch), BF16),
-            pltpu.VMEM((ch, 9 * ch), F32),
+            pltpu.VMEM((ch, lanes), F32),
         ],
         (*bricks, *rims),
     )
@@ -379,7 +381,7 @@
         rows = keep.shape[0] // 2
         keep, send = call(
             lambda *refs: fold_kernel(bit, *refs),
-            [shape((rows, 9 * ch), F32), shape((rows, 9 * ch), BF16)],
+            [shape((rows, lanes), F32), shape((rows, lanes), BF16)],
             [],
             (keep, got),
         )

time: 46.1 us -> 41.6 us (0.902)
  waiting for transfers between devices: 20 us -> 14.8 us
  starting transfers between devices: 16.2 us -> 16.9 us
    ppermute x12, waiting for transfers between devices: 18.1 us -> 12.9 us  [swap(): return lax.ppermute(value, axis, [(i, i ^ k) for i in range(n)])]
    ppermute x12, starting transfers between devices: 11.4 us -> 12.1 us  [swap(): return lax.ppermute(value, axis, [(i, i ^ k) for i in range(n)])]
  transfers between devices with their start and end apart: 14 -> 14, of which waited for: 8 -> 7; matrix products, arithmetic and copies ran while one was open for 0% -> 0% of each run, Pallas kernels for 13% -> 15%
where the time goes in v1:
time: 41.6 us; the launch traced here: 41.5 us
  starting transfers between devices  16.9 us (41%)
  waiting for transfers between devices  14.8 us (36%)
  Pallas kernels  8.99 us (22%)
  between operations  0.7 us (2%)
    ppermute x12, waiting for transfers between devices, swap(): return lax.ppermute(value, axis, [(i, i ^ k) for i in range(n)])  12.9 us
    ppermute x12, starting transfers between devices, swap(): return lax.ppermute(value, axis, [(i, i ^ k) for i in range(n)])  12.1 us
    pallas_call x8, Pallas kernels, call(): pl.pallas_call(kernel, out_shape=[pltpu.VMEM(v.shape, v.dtype) if placed...  7.76 us
    ppermute x2, starting transfers between devices, shift(): return lax.ppermute(value, axis, [(i, (i + step) % n) for i in range(n)])  4.81 us
    ppermute x2, waiting for transfers between devices, shift(): return lax.ppermute(value, axis, [(i, (i + step) % n) for i in range(n)])  1.88 us
    pallas_call x1, Pallas kernels, fetch(): pl.pallas_call(fetch_kernel, out_shape=[pltpu.VMEM(shape, BF16) for shape...  1.23 us
  transfers between devices with their start and end apart: 14, of which 7 were waited for; matrix products, arithmetic and copies ran while one was open for 0% of the time, Pallas kernels for 15%

profile of v1, /device:TPU:0, one launch (start us, length us, event | category | flops | bytes accessed | tf_op | source)
XLA Modules:
  0.0 41.5 jit_solution(17565435929215337642)
XLA Ops:
  0.6 1.0 %shard_map.68 = (bf16[16,2,16,128]{3,2,1,0:T(8,128)(2,1)S(1)}, bf16[3,2,16,128]{3,2,1,0:T(8,128)(2,1)S(1)}, bf16[3,2,16,128]{3,2,1,0:T(8,128)(2,1)S(1)}) custom-call(bf16[8,2,16,128]{3,2,1,0:T(8,128)(2,1)} %grad_ref.1, bf16[8,2,16,128]{3,2,1,0:T(8,128)(2,1)} %feat_ref.1), custom_call_target="tpu_custom_call" | custom-call | tf_op jit(solution)/shard_map/pallas_call | solution.py:291
  1.6 3.0 %collective-permute-start.1 = (bf16[16,2,16,128]{3,2,1,0:T(8,128)(2,1)S(1)}, bf16[16,2,16,128]{3,2,1,0:T(8,128)(2,1)S(1)}, u32[]{:S(2)}, u32[]{:S(2)}) collective-permute-start(bf16[16,2,16,128]{3,2,1,0:T(8,128)(2,1)S(1)} %get-tuple-element.17.refs_0_), channel_id=1, source_target_pairs={{0,2},{1,3},{2,0},{3,1},{4,6},{5,7},{6,4},{7,5},{8,10},{9,11},{10,... | collective-permute-start | bytes 393224 | tf_op jit(solution)/shard_map/ppermute | solution.py:23
  4.6 0.0 collective-permute-start
  4.6 3.5 %collective-permute-done.1.refs_2_ = bf16[16,2,16,128]{3,2,1,0:T(8,128)(2,1)S(1)} collective-permute-done((bf16[16,2,16,128]{3,2,1,0:T(8,128)(2,1)S(1)}, bf16[16,2,16,128]{3,2,1,0:T(8,128)(2,1)S(1)}, u32[]{:S(2)}, u32[]{:S(2)}) %collective-permute-start.1) | collective-permute-done | bytes 131104 | tf_op jit(solution)/shard_map/ppermute | solution.py:23
  8.1 0.0 collective-permute-start.2
  8.1 1.8 %collective-permute-start.3 = (bf16[3,2,16,128]{3,2,1,0:T(8,128)(2,1)S(1)}, bf16[3,2,16,128]{3,2,1,0:T(8,128)(2,1)S(1)}, u32[]{:S(2)}, u32[]{:S(2)}) collective-permute-start(bf16[3,2,16,128]{3,2,1,0:T(8,128)(2,1)S(1)} %get-tuple-element.18), channel_id=1, source_target_pairs={{0,4},{4,8},{8,12},{12,16},{16,20},{20,24},{24,28},{28,0},{1,5},{5... | collective-permute-start | bytes 73736 | tf_op jit(solution)/shard_map/ppermute | solution.py:28
  9.9 3.0 %collective-permute-start.4 = (bf16[3,2,16,128]{3,2,1,0:T(8,128)(2,1)S(1)}, bf16[3,2,16,128]{3,2,1,0:T(8,128)(2,1)S(1)}, u32[]{:S(2)}, u32[]{:S(2)}) collective-permute-start(bf16[3,2,16,128]{3,2,1,0:T(8,128)(2,1)S(1)} %get-tuple-element.19), channel_id=1, source_target_pairs={{0,28},{4,0},{8,4},{12,8},{16,12},{20,16},{24,20},{28,24},{1,29},{... | collective-permute-start | bytes 73736 | tf_op jit(solution)/shard_map/ppermute | solution.py:28
  12.9 1.9 %collective-permute-done.3.refs_0_ = bf16[3,2,16,128]{3,2,1,0:T(8,128)(2,1)S(1)} collective-permute-done((bf16[3,2,16,128]{3,2,1,0:T(8,128)(2,1)S(1)}, bf16[3,2,16,128]{3,2,1,0:T(8,128)(2,1)S(1)}, u32[]{:S(2)}, u32[]{:S(2)}) %collective-permute-start.3) | collective-permute-done | bytes 24608 | tf_op jit(solution)/shard_map/ppermute | solution.py:28
  14.8 0.0 collective-permute-done.4.refs_1_
  14.8 1.6 %collective-permute-start.6 = (bf16[6,2,16,128]{3,2,1,0:T(8,128)(2,1)S(1)}, bf16[6,2,16,128]{3,2,1,0:T(8,128)(2,1)S(1)}, u32[]{:S(2)}, u32[]{:S(2)}) collective-permute-start(bf16[6,2,16,128]{3,2,1,0:T(8,128)(2,1)S(1)} %shard_map.69.refs_4_), channel_id=1, source_target_pairs={{0,2},{1,3},{2,0},{3,1},{4,6},{5,7},{6,4},{7,5},{8,10},{9,11},{10,... | collective-permute-start | bytes 147464 | tf_op jit(solution)/shard_map/ppermute | solution.py:23
  16.5 0.0 collective-permute-start.5
  16.5 2.5 %collective-permute-done.6.refs_6_ = bf16[6,2,16,128]{3,2,1,0:T(8,128)(2,1)S(1)} collective-permute-done((bf16[6,2,16,128]{3,2,1,0:T(8,128)(2,1)S(1)}, bf16[6,2,16,128]{3,2,1,0:T(8,128)(2,1)S(1)}, u32[]{:S(2)}, u32[]{:S(2)}) %collective-permute-start.6) | collective-permute-done | bytes 49184 | tf_op jit(solution)/shard_map/ppermute | solution.py:23
  19.0 0.0 collective-permute-start.7
  19.0 0.0 collective-permute-done.5.refs_5_
  19.0 1.2 %collective-permute-done.7.refs_7_ = bf16[6,2,16,128]{3,2,1,0:T(8,128)(2,1)S(1)} collective-permute-done((bf16[6,2,16,128]{3,2,1,0:T(8,128)(2,1)S(1)}, bf16[6,2,16,128]{3,2,1,0:T(8,128)(2,1)S(1)}, u32[]{:S(2)}, u32[]{:S(2)}) %collective-permute-start.7) | collective-permute-done | bytes 49184 | tf_op jit(solution)/shard_map/ppermute | solution.py:23
  20.2 0.0 collective-permute-done.refs_1_
  20.2 0.0 collective-permute-done.2.refs_3_
  20.2 1.0 %shard_map.73 = (f32[64,864]{1,0:T(8,128)S(1)}, bf16[64,864]{1,0:T(8,128)(2,1)S(1)}) custom-call(bf16[16,2,16,128]{3,2,1,0:T(8,128)(2,1)S(1)} %get-tuple-element.17.refs_0_, bf16[16,2,16,128]{3,2,1,0:T(8,128)(2,1)S(1)} %collective-permute-done.refs_1_, bf16[16,2,16,128]{3,2,1,0:T(8,128)(2,1)S(1)} %collective-permute-done.1.refs_2_, ...), custom_call_target="tpu_custom_call" | custom-call | tf_op jit(solution)/shard_map/pallas_call | solution.py:291
  21.3 1.4 %collective-permute-start.11 = (bf16[64,864]{1,0:T(8,128)(2,1)S(1)}, bf16[64,864]{1,0:T(8,128)(2,1)S(1)}, u32[]{:S(2)}, u32[]{:S(2)}) collective-permute-start(bf16[64,864]{1,0:T(8,128)(2,1)S(1)} %get-tuple-element.27), channel_id=1, source_target_pairs={{0,4},{4,0},{8,12},{12,8},{16,20},{20,16},{24,28},{28,24},{1,5},{5... | collective-permute-start | bytes 331784 | tf_op jit(solution)/shard_map/ppermute | solution.py:23
  22.7 3.9 %collective-permute-done.11.refs_1_ = bf16[64,864]{1,0:T(8,128)(2,1)S(1)} collective-permute-done((bf16[64,864]{1,0:T(8,128)(2,1)S(1)}, bf16[64,864]{1,0:T(8,128)(2,1)S(1)}, u32[]{:S(2)}, u32[]{:S(2)}) %collective-permute-start.11) | collective-permute-done | bytes 110624 | tf_op jit(solution)/shard_map/ppermute | solution.py:23
  26.6 1.2 %collective-permute-start.12 = (bf16[32,864]{1,0:T(8,128)(2,1)S(1)}, bf16[32,864]{1,0:T(8,128)(2,1)S(1)}, u32[]{:S(2)}, u32[]{:S(2)}) collective-permute-start(bf16[32,864]{1,0:T(8,128)(2,1)S(1)} %get-tuple-element.29), channel_id=1, source_target_pairs={{0,8},{4,12},{8,0},{12,4},{16,24},{20,28},{24,16},{28,20},{1,9},{5... | collective-permute-start | bytes 165896 | tf_op jit(solution)/shard_map/ppermute | solution.py:23
  27.8 1.2 %shard_map.70 = (bf16[3,3,3,128,128]{4,3,2,1,0:T(8,128)(2,1)S(1)}, bf16[2,2,2,128,128]{4,3,2,1,0:T(8,128)(2,1)S(1)}) custom-call(bf16[3,3,3,128,128]{4,3,2,1,0:T(8,128)(2,1)} %refs_0_.1, bf16[2,2,2,512,128]{4,3,2,1,0:T(8,128)(2,1)} %refs_1_.1), custom_call_target="tpu_custom_call" | custom-call | tf_op jit(solution)/shard_map/pallas_call | solution.py:303
  29.1 4.3 %shard_map.71 = (f32[1,4,8,512]{3,2,1,0:T(8,128)S(1)}, bf16[1,4,8,512]{3,2,1,0:T(8,128)(2,1)S(1)}, bf16[1,4,8,512]{3,2,1,0:T(8,128)(2,1)S(1)}, bf16[1,4,8,512]{3,2,1,0:T(8,128)(2,1)S(1)}) custom-call(bf16[16,2,16,128]{3,2,1,0:T(8,128)(2,1)S(1)} %get-tuple-element.17.refs_0_, bf16[16,2,16,128]{3,2,1,0:T(8,128)(2,1)S(1)} %collective-permute-done.refs_1_, ...), custom_call_target="tpu_custom_call" | custom-call | tf_op jit(solution)/shard_map/pallas_call | solution.py:291
  33.3 0.1 collective-permute-start.8
  33.4 1.6 %collective-permute-start.9 = (bf16[1,4,8,512]{3,2,1,0:T(8,128)(2,1)S(1)}, bf16[1,4,8,512]{3,2,1,0:T(8,128)(2,1)S(1)}, u32[]{:S(2)}, u32[]{:S(2)}) collective-permute-start(bf16[1,4,8,512]{3,2,1,0:T(8,128)(2,1)S(1)} %get-tuple-element.24), channel_id=1, source_target_pairs={{0,2},{1,3},{2,0},{3,1},{4,6},{5,7},{6,4},{7,5},{8,10},{9,11},{10,... | collective-permute-start | bytes 98312 | tf_op jit(solution)/shard_map/ppermute | solution.py:23
  35.0 0.3 collective-permute-start.10
  35.2 0.0 collective-permute-done.12.refs_1_
  35.3 2.9 %collective-permute-start.13 = (bf16[16,864]{1,0:T(8,128)(2,1)S(1)}, bf16[16,864]{1,0:T(8,128)(2,1)S(1)}, u32[]{:S(2)}, u32[]{:S(2)}) collective-permute-start(bf16[16,864]{1,0:T(8,128)(2,1)S(1)} %get-tuple-element.31), channel_id=1, source_target_pairs={{0,16},{4,20},{8,24},{12,28},{16,0},{20,4},{24,8},{28,12},{1,17},{... | collective-permute-start | bytes 82952 | tf_op jit(solution)/shard_map/ppermute | solution.py:23
  38.2 0.0 collective-permute-done.8.refs_1_
  38.2 0.0 collective-permute-done.9.refs_2_
  38.2 0.1 collective-permute-done.10.refs_3_
  38.3 0.6 %shard_map.72 = bf16[1,4,8,512]{3,2,1,0:T(8,128)(2,1)} custom-call(f32[1,4,8,512]{3,2,1,0:T(8,128)S(1)} %get-tuple-element.22.refs_0_, bf16[1,4,8,512]{3,2,1,0:T(8,128)(2,1)S(1)} %collective-permute-done.8.refs_1_, bf16[1,4,8,512]{3,2,1,0:T(8,128)(2,1)S(1)} %collective-permute-done.9.refs_2_, bf16[1,4,8,512]{3,2,1,0:T(8,128)(2,1)S(1)} %collective-permute-done.10.refs_3_), custom_call_target="tpu_custom_call" | custom-call | tf_op jit(solution)/shard_map/pallas_call | solution.py:291
  38.9 1.7 %collective-permute-done.13.got_ref = bf16[16,864]{1,0:T(8,128)(2,1)S(1)} collective-permute-done((bf16[16,864]{1,0:T(8,128)(2,1)S(1)}, bf16[16,864]{1,0:T(8,128)(2,1)S(1)}, u32[]{:S(2)}, u32[]{:S(2)}) %collective-permute-start.13) | collective-permute-done | bytes 27680 | tf_op jit(solution)/shard_map/ppermute | solution.py:23
  40.7 0.8 %shard_map.76 = f32[3,3,3,16,32]{4,3,2,1,0:T(8,128)} custom-call(f32[16,864]{1,0:T(8,128)S(1)} %get-tuple-element.30.keep_ref, bf16[16,864]{1,0:T(8,128)(2,1)S(1)} %collective-permute-done.13.got_ref), custom_call_target="tpu_custom_call" | custom-call | tf_op jit(solution)/shard_map/pallas_call | solution.py:291
  (3 shorter events, 0.1 us)
Async XLA Ops:
  1.6 6.5 %collective-permute-start.1 = (bf16[16,2,16,128]{3,2,1,0:T(8,128)(2,1)S(1)}, bf16[16,2,16,128]{3,2,1,0:T(8,128)(2,1)S(1)}, u32[]{:S(2)}, u32[]{:S(2)}) collective-permute-start(bf16[16,2,16,128]{3,2,1,0:T(8,128)(2,1)S(1)} %get-tuple-element.17.refs_0_), channel_id=1, source_target_pairs={{0,2},{1,3},{2,0},{3,1},{4,6},{5,7},{6,4},{7,5},{8,10},{9,11},{10,... | collective-permute-start | bytes 393224 | tf_op jit(solution)/shard_map/ppermute | solution.py:23
  4.6 15.6 %collective-permute-start = (bf16[16,2,16,128]{3,2,1,0:T(8,128)(2,1)S(1)}, bf16[16,2,16,128]{3,2,1,0:T(8,128)(2,1)S(1)}, u32[]{:S(2)}, u32[]{:S(2)}) collective-permute-start(bf16[16,2,16,128]{3,2,1,0:T(8,128)(2,1)S(1)} %get-tuple-element.17.refs_0_), channel_id=1, source_target_pairs={{0,1},{1,0},{2,3},{3,2},{4,5},{5,4},{6,7},{7,6},{8,9},{9,8},{10,11... | collective-permute-start | bytes 393224 | tf_op jit(solution)/shard_map/ppermute | solution.py:23
  8.1 12.1 %collective-permute-start.2 = (bf16[16,2,16,128]{3,2,1,0:T(8,128)(2,1)S(1)}, bf16[16,2,16,128]{3,2,1,0:T(8,128)(2,1)S(1)}, u32[]{:S(2)}, u32[]{:S(2)}) collective-permute-start(bf16[16,2,16,128]{3,2,1,0:T(8,128)(2,1)S(1)} %collective-permute-done.1.refs_2_), channel_id=1, source_target_pairs={{0,1},{1,0},{2,3},{3,2},{4,5},{5,4},{6,7},{7,6},{8,9},{9,8},{10,11... | collective-permute-start | bytes 393224 | tf_op jit(solution)/shard_map/ppermute | solution.py:23
  8.1 6.7 %collective-permute-start.3 = (bf16[3,2,16,128]{3,2,1,0:T(8,128)(2,1)S(1)}, bf16[3,2,16,128]{3,2,1,0:T(8,128)(2,1)S(1)}, u32[]{:S(2)}, u32[]{:S(2)}) collective-permute-start(bf16[3,2,16,128]{3,2,1,0:T(8,128)(2,1)S(1)} %get-tuple-element.18), channel_id=1, source_target_pairs={{0,4},{4,8},{8,12},{12,16},{16,20},{20,24},{24,28},{28,0},{1,5},{5... | collective-permute-start | bytes 73736 | tf_op jit(solution)/shard_map/ppermute | solution.py:28
  9.9 4.9 %collective-permute-start.4 = (bf16[3,2,16,128]{3,2,1,0:T(8,128)(2,1)S(1)}, bf16[3,2,16,128]{3,2,1,0:T(8,128)(2,1)S(1)}, u32[]{:S(2)}, u32[]{:S(2)}) collective-permute-start(bf16[3,2,16,128]{3,2,1,0:T(8,128)(2,1)S(1)} %get-tuple-element.19), channel_id=1, source_target_pairs={{0,28},{4,0},{8,4},{12,8},{16,12},{20,16},{24,20},{28,24},{1,29},{... | collective-permute-start | bytes 73736 | tf_op jit(solution)/shard_map/ppermute | solution.py:28
  14.8 4.2 %collective-permute-start.6 = (bf16[6,2,16,128]{3,2,1,0:T(8,128)(2,1)S(1)}, bf16[6,2,16,128]{3,2,1,0:T(8,128)(2,1)S(1)}, u32[]{:S(2)}, u32[]{:S(2)}) collective-permute-start(bf16[6,2,16,128]{3,2,1,0:T(8,128)(2,1)S(1)} %shard_map.69.refs_4_), channel_id=1, source_target_pairs={{0,2},{1,3},{2,0},{3,1},{4,6},{5,7},{6,4},{7,5},{8,10},{9,11},{10,... | collective-permute-start | bytes 147464 | tf_op jit(solution)/shard_map/ppermute | solution.py:23
  16.5 2.5 %collective-permute-start.5 = (bf16[6,2,16,128]{3,2,1,0:T(8,128)(2,1)S(1)}, bf16[6,2,16,128]{3,2,1,0:T(8,128)(2,1)S(1)}, u32[]{:S(2)}, u32[]{:S(2)}) collective-permute-start(bf16[6,2,16,128]{3,2,1,0:T(8,128)(2,1)S(1)} %shard_map.69.refs_4_), channel_id=1, source_target_pairs={{0,1},{1,0},{2,3},{3,2},{4,5},{5,4},{6,7},{7,6},{8,9},{9,8},{10,11... | collective-permute-start | bytes 147464 | tf_op jit(solution)/shard_map/ppermute | solution.py:23
  19.0 1.2 %collective-permute-start.7 = (bf16[6,2,16,128]{3,2,1,0:T(8,128)(2,1)S(1)}, bf16[6,2,16,128]{3,2,1,0:T(8,128)(2,1)S(1)}, u32[]{:S(2)}, u32[]{:S(2)}) collective-permute-start(bf16[6,2,16,128]{3,2,1,0:T(8,128)(2,1)S(1)} %collective-permute-done.6.refs_6_), channel_id=1, source_target_pairs={{0,1},{1,0},{2,3},{3,2},{4,5},{5,4},{6,7},{7,6},{8,9},{9,8},{10,11... | collective-permute-start | bytes 147464 | tf_op jit(solution)/shard_map/ppermute | solution.py:23
  21.3 5.3 %collective-permute-start.11 = (bf16[64,864]{1,0:T(8,128)(2,1)S(1)}, bf16[64,864]{1,0:T(8,128)(2,1)S(1)}, u32[]{:S(2)}, u32[]{:S(2)}) collective-permute-start(bf16[64,864]{1,0:T(8,128)(2,1)S(1)} %get-tuple-element.27), channel_id=1, source_target_pairs={{0,4},{4,0},{8,12},{12,8},{16,20},{20,16},{24,28},{28,24},{1,5},{5... | collective-permute-start | bytes 331784 | tf_op jit(solution)/shard_map/ppermute | solution.py:23
  26.6 8.7 %collective-permute-start.12 = (bf16[32,864]{1,0:T(8,128)(2,1)S(1)}, bf16[32,864]{1,0:T(8,128)(2,1)S(1)}, u32[]{:S(2)}, u32[]{:S(2)}) collective-permute-start(bf16[32,864]{1,0:T(8,128)(2,1)S(1)} %get-tuple-element.29), channel_id=1, source_target_pairs={{0,8},{4,12},{8,0},{12,4},{16,24},{20,28},{24,16},{28,20},{1,9},{5... | collective-permute-start | bytes 165896 | tf_op jit(solution)/shard_map/ppermute | solution.py:23
  33.3 4.9 %collective-permute-start.8 = (bf16[1,4,8,512]{3,2,1,0:T(8,128)(2,1)S(1)}, bf16[1,4,8,512]{3,2,1,0:T(8,128)(2,1)S(1)}, u32[]{:S(2)}, u32[]{:S(2)}) collective-permute-start(bf16[1,4,8,512]{3,2,1,0:T(8,128)(2,1)S(1)} %get-tuple-element.23), channel_id=1, source_target_pairs={{0,1},{1,0},{2,3},{3,2},{4,5},{5,4},{6,7},{7,6},{8,9},{9,8},{10,11... | collective-permute-start | bytes 98312 | tf_op jit(solution)/shard_map/ppermute | solution.py:23
  33.4 4.8 %collective-permute-start.9 = (bf16[1,4,8,512]{3,2,1,0:T(8,128)(2,1)S(1)}, bf16[1,4,8,512]{3,2,1,0:T(8,128)(2,1)S(1)}, u32[]{:S(2)}, u32[]{:S(2)}) collective-permute-start(bf16[1,4,8,512]{3,2,1,0:T(8,128)(2,1)S(1)} %get-tuple-element.24), channel_id=1, source_target_pairs={{0,2},{1,3},{2,0},{3,1},{4,6},{5,7},{6,4},{7,5},{8,10},{9,11},{10,... | collective-permute-start | bytes 98312 | tf_op jit(solution)/shard_map/ppermute | solution.py:23
  35.0 3.4 %collective-permute-start.10 = (bf16[1,4,8,512]{3,2,1,0:T(8,128)(2,1)S(1)}, bf16[1,4,8,512]{3,2,1,0:T(8,128)(2,1)S(1)}, u32[]{:S(2)}, u32[]{:S(2)}) collective-permute-start(bf16[1,4,8,512]{3,2,1,0:T(8,128)(2,1)S(1)} %get-tuple-element.25), channel_id=1, source_target_pairs={{0,3},{1,2},{2,1},{3,0},{4,7},{5,6},{6,5},{7,4},{8,11},{9,10},{10,... | collective-permute-start | bytes 98312 | tf_op jit(solution)/shard_map/ppermute | solution.py:23
  35.3 5.4 %collective-permute-start.13 = (bf16[16,864]{1,0:T(8,128)(2,1)S(1)}, bf16[16,864]{1,0:T(8,128)(2,1)S(1)}, u32[]{:S(2)}, u32[]{:S(2)}) collective-permute-start(bf16[16,864]{1,0:T(8,128)(2,1)S(1)} %get-tuple-element.31), channel_id=1, source_target_pairs={{0,16},{4,20},{8,24},{12,28},{16,0},{20,4},{24,8},{28,12},{1,17},{... | collective-permute-start | bytes 82952 | tf_op jit(solution)/shard_map/ppermute | solution.py:23

commit v2 on v1

--- a/solution.py
+++ b/solution.py
@@ -49,33 +49,20 @@
         copy.wait()
 
 
-def main_kernel(n, m, *refs):
-    bricks, rims, (full_ref, up_ref, half_ref) = (
-        refs[:n],
-        refs[n : 2 * n],
-        refs[2 * n : 2 * n + 3],
-    )
-    outs, (stage, spread, padded, result, held, arrived) = (
-        refs[2 * n + 3 : 3 * n + 3],
-        refs[3 * n + 3 :],
-    )
-    load = pltpu.make_async_copy(half_ref, held, arrived)
-    load.start()
-    nx, ny, nz, ch = bricks[0].shape
-    nx = nx // 2
-    halo = rims[0].shape[0] // 2
-    rows, half_x, half_z = n * ny, nx // 2, nz // 2
-    deep = nx + 2 * halo
-    pairs = deep // 2
-    half_y = rows // 2
-    width = up_ref.shape[3]
+def spread_out(sources, full_ref, stage, spread):
+    ny, nz, ch = sources[0][0].shape[1:]
+    count = sum(source.shape[0] for source in sources[0])
+    n, pairs, half_z = len(sources), count // 2, nz // 2
+    rows = n * ny
     spread[:, :, 0] = jnp.zeros((4, pairs, nz, ch), BF16)
     spread[:, :, rows + 1] = jnp.zeros((4, pairs, nz, ch), BF16)
-    level = lax.broadcasted_iota(jnp.int32, (deep * ny, half_z, ch), 1)
+    level = lax.broadcasted_iota(jnp.int32, (count * ny, half_z, ch), 1)
     for k in range(n):
-        stage[: halo * ny] = rims[k][:halo].astype(F32).reshape(halo * ny, nz, ch)
-        stage[halo * ny : (halo + nx) * ny] = bricks[k][:nx].astype(F32).reshape(nx * ny, nz, ch)
-        stage[(halo + nx) * ny :] = rims[k][halo:].astype(F32).reshape(halo * ny, nz, ch)
+        at = 0
+        for source in sources[k]:
+            size = source.shape[0] * ny
+            stage[at : at + size] = source.astype(F32).reshape(size, nz, ch)
+            at += size
         even = stage[:, pl.ds(0, half_z, stride=2), :]
         odd = stage[:, pl.ds(1, half_z, stride=2), :]
         after = jnp.where(level == half_z - 1, 0.0, pltpu.roll(even, half_z - 1, 1))
@@ -93,7 +80,7 @@
         ],
         axis=0,
     )
-    grads = []
+    products = []
     for order in ((2, 0, 3), (1, 2, 0)):
         window = jnp.concatenate(
             [
@@ -103,14 +90,50 @@
             ],
             axis=1,
         )
-        product = dot(window, taps, NT).reshape(pairs, rows, 2, half_z, 3 * ch)
+        products.append(dot(window, taps, NT).reshape(pairs, rows, 2, half_z, 3 * ch))
+    return products
+
+
+def inner_kernel(n, *refs):
+    bricks, (full_ref, out_ref, stage, spread) = refs[:n], refs[n:]
+    nx, ch = bricks[0].shape[0] // 2, bricks[0].shape[3]
+    products = spread_out([[brick[:nx]] for brick in bricks], full_ref, stage, spread)
+    for c, product in enumerate(products):
+        for u in range(-1, nx + 1):
+            total = None
+            for p in range(3):
+                x = u - p + 1
+                if 0 <= x < nx:
+                    term = product[x // 2, :, x % 2, :, p * ch : (p + 1) * ch]
+                    total = term if total is None else total + term
+            out_ref[c, u + 1] = total
+
+
+def main_kernel(n, m, *refs):
+    rims, (inner_ref, full_ref, up_ref, half_ref) = refs[:n], refs[n : n + 4]
+    outs, (stage, spread, padded, result, held, arrived) = (
+        refs[n + 4 : 2 * n + 4],
+        refs[2 * n + 4 :],
+    )
+    load = pltpu.make_async_copy(half_ref, held, arrived)
+    load.start()
+    halo = rims[0].shape[0] // 2 - 1
+    nx, rows, half_z, ch = inner_ref.shape[1:]
+    nx = nx - 2
+    half_x, half_y = nx // 2, rows // 2
+    width = up_ref.shape[3]
+    products = spread_out([[rim[: 2 * halo]] for rim in rims], full_ref, stage, spread)
+    grads = []
+    for c, product in enumerate(products):
         planes = {}
         for u in range(-2, nx + 2):
-            total = None
+            total = inner_ref[c, u + 1] if -1 <= u <= nx else None
             for p in range(3):
-                x = u - p + 1 + halo
-                term = product[x // 2, :, x % 2, :, p * ch : (p + 1) * ch]
-                total = term if total is None else total + term
+                x = u - p + 1
+                if not 0 <= x < nx:
+                    at = x + halo if x < 0 else x - nx + halo
+                    term = product[at // 2, :, at % 2, :, p * ch : (p + 1) * ch]
+                    total = term if total is None else total + term
             planes[u] = total.reshape(half_y, 2, half_z, ch)
         grads.append(planes)
     columns = []
@@ -168,20 +191,19 @@
         outs[k][...] = result[pair(k)].astype(outs[k].dtype)
 
 
-def taps_kernel(n, m, *refs):
-    bricks, rims, (keep_ref, send_ref, spread, table) = (
-        refs[:n],
-        refs[n : 2 * n],
-        refs[2 * n :],
-    )
-    nx, ny, nz, ch = bricks[0].shape
-    nx = nx // 2
-    halo = rims[0].shape[0] // 2
-    rows = n * ny
-    part = ch // n
-    block = ch // m
-    spread[:, 0] = jnp.zeros((nx + 2, nz, ch), BF16)
-    spread[:, rows + 1] = jnp.zeros((nx + 2, nz, ch), BF16)
+def chosen_lanes(cells, pick, part, nz):
+    chosen = dot(cells, pick, NN)
+    level = lax.rem(lax.broadcasted_iota(jnp.int32, chosen.shape, 0), nz)
+    lane = lax.broadcasted_iota(jnp.int32, chosen.shape, 1)
+    count = chosen.shape[0]
+    above = jnp.where(level == nz - 1, 0.0, pltpu.roll(chosen, count - 1, 0))
+    below = jnp.where(level == 0, 0.0, pltpu.roll(chosen, 1, 0))
+    mixed = jnp.where(lane < part, above, jnp.where(lane < 2 * part, chosen, below))
+    return mixed.astype(BF16)
+
+
+def selections(n, m, ch):
+    part, block = ch // n, ch // m
     start = lax.axis_index("chan") * part
     source = lax.broadcasted_iota(jnp.int32, (ch, ch), 0)
     target = lax.broadcasted_iota(jnp.int32, (ch, ch), 1)
@@ -192,41 +214,48 @@
     turned = jnp.zeros_like(owner)
     for bit in range(bits):
         turned = turned + (owner // 2**bit % 2) * 2 ** (bits - 1 - bit)
-    order = jnp.where(turned * block + lax.rem(target, block) == source, 1.0, 0.0).astype(BF16)
+    place = turned * block + lax.rem(target, block)
+    return pick, place, source
+
+
+def taps_kernel(n, m, *refs):
+    bricks, (keep_ref, send_ref, spread, table) = refs[:n], refs[n:]
+    nx, ny, nz, ch = bricks[0].shape
+    nx = nx // 2
+    rows = n * ny
+    part = ch // n
+    cells = nx * ny * nz
+    spread[:, 0] = jnp.zeros((nx, nz, ch), BF16)
+    spread[:, rows + 1] = jnp.zeros((nx, nz, ch), BF16)
+    pick, place, source = selections(n, m, ch)
+    order = jnp.where(place == source, 1.0, 0.0).astype(BF16)
     turned_feats = []
     for k in range(n):
-        cells = jnp.concatenate(
-            [rims[k][halo - 1 : halo], bricks[k][:nx], rims[k][halo : halo + 1]], axis=0
-        )
-        cells = cells.reshape((nx + 2) * ny * nz, ch)
-        chosen = dot(cells, pick, NN)
-        level = lax.rem(lax.broadcasted_iota(jnp.int32, chosen.shape, 0), nz)
-        lane = lax.broadcasted_iota(jnp.int32, chosen.shape, 1)
-        count = chosen.shape[0]
-        above = jnp.where(level == nz - 1, 0.0, pltpu.roll(chosen, count - 1, 0))
-        below = jnp.where(level == 0, 0.0, pltpu.roll(chosen, 1, 0))
-        mixed = jnp.where(lane < part, above, jnp.where(lane < 2 * part, chosen, below))
-        mixed = mixed.astype(BF16).reshape(nx + 2, ny, nz, ch)
+        mixed = chosen_lanes(bricks[k][:nx].reshape(cells, ch), pick, part, nz)
+        mixed = mixed.reshape(nx, ny, nz, ch)
         first = pair(k) * ny + 1
         for b in range(ny):
             spread[:, first + b] = mixed[:, b]
-        feat = bricks[k][nx:].reshape(nx * ny * nz, ch)
-        turned_feats.append(dot(order, feat, NT).astype(BF16))
+        turned_feats.append(dot(order, bricks[k][nx:].reshape(cells, ch), NT).astype(BF16))
     totals = []
+    plane = ny * nz
     for p in range(3):
         total = None
+        feat_from, grad_from = max(0, p - 1), max(0, 1 - p)
+        count = nx - abs(p - 1)
         for k in range(n):
             first = pair(k) * ny
             window = jnp.concatenate(
                 [
-                    spread[2 - p : 2 - p + nx, pl.ds(first + 2 - q, ny)].reshape(
-                        nx * ny * nz, ch
-                    )
+                    spread[
+                        grad_from : grad_from + count, pl.ds(first + 2 - q, ny)
+                    ].reshape(count * plane, ch)
                     for q in range(3)
                 ],
                 axis=1,
             )
-            product = dot(turned_feats[k], window, NN)
+            feat = turned_feats[k][:, feat_from * plane : (feat_from + count) * plane]
+            product = dot(feat, window, NN)
             total = product if total is None else total + product
         totals += [total[:, q * ch : q * ch + 3 * part] for q in range(3)]
     table[...] = jnp.concatenate(totals, axis=1)
@@ -236,12 +265,72 @@
     send_ref[...] = table[pl.ds(pl.multiple_of((1 - bit) * half, half), half), :].astype(BF16)
 
 
+def outer_kernel(n, m, *refs):
+    bricks, rims, (out_ref, spread) = refs[:n], refs[n : 2 * n], refs[2 * n :]
+    nx, ny, nz, ch = bricks[0].shape
+    nx = nx // 2
+    halo = rims[0].shape[0] // 2 - 1
+    rows = n * ny
+    part = ch // n
+    plane = ny * nz
+    half = ch // 2
+    spread[:, 0] = jnp.zeros((4, nz, ch), BF16)
+    spread[:, rows + 1] = jnp.zeros((4, nz, ch), BF16)
+    pick, place, source = selections(n, m, ch)
+    bit = lax.rem(lax.axis_index("grp"), 2)
+    order = jnp.where(place[:half] == source[:half] + bit * half, 1.0, 0.0).astype(BF16)
+    cells = []
+    for k in range(n):
+        for planes in (
+            bricks[k][0:1],
+            rims[k][halo : halo + 1],
+            rims[k][halo - 1 : halo],
+            bricks[k][nx - 1 : nx],
+        ):
+            cells.append(planes.reshape(plane, ch))
+    mixed = chosen_lanes(jnp.concatenate(cells, axis=0), pick, part, nz)
+    mixed = mixed.reshape(n, 4, ny, nz, ch)
+    for k in range(n):
+        first = pair(k) * ny + 1
+        for b in range(ny):
+            spread[:, first + b] = mixed[k, :, b]
+    for e in range(2):
+        feats, windows = [], []
+        for k in range(n):
+            if e == 0:
+                sides = (rims[k][2 * halo], bricks[k][2 * nx - 1])
+            else:
+                sides = (bricks[k][nx], rims[k][2 * halo + 1])
+            first = pair(k) * ny
+            for side, feat in enumerate(sides):
+                feats.append(feat.reshape(plane, ch))
+                windows.append(
+                    jnp.concatenate(
+                        [
+                            spread[2 * e + side, pl.ds(first + 2 - q, ny)].reshape(plane, ch)
+                            for q in range(3)
+                        ],
+                        axis=1,
+                    )
+                )
+        feat = dot(order, jnp.concatenate(feats, axis=0), NT).astype(BF16)
+        total = dot(feat, jnp.concatenate(windows, axis=0), NN)
+        out_ref[e] = jnp.concatenate(
+            [total[:, q * ch : q * ch + 3 * part] for q in range(3)], axis=1
+        )
+
+
 def load_kernel(grad_ref, feat_ref, own_ref, first_ref, last_ref, arrived):
     nx = grad_ref.shape[0]
-    halo = first_ref.shape[0]
+    halo = first_ref.shape[0] - 1
+    cut = pl.ds(0, halo)
     copies = [
-        pltpu.make_async_copy(grad_ref.at[pl.ds(nx - halo, halo)], last_ref, arrived.at[0]),
-        pltpu.make_async_copy(grad_ref.at[pl.ds(0, halo)], first_ref, arrived.at[1]),
+        pltpu.make_async_copy(
+            grad_ref.at[pl.ds(nx - halo, halo)], last_ref.at[cut], arrived.at[0]
+        ),
+        pltpu.make_async_copy(grad_ref.at[cut], first_ref.at[cut], arrived.at[1]),
+        pltpu.make_async_copy(feat_ref.at[nx - 1], last_ref.at[halo], arrived.at[4]),
+        pltpu.make_async_copy(feat_ref.at[0], first_ref.at[halo], arrived.at[5]),
         pltpu.make_async_copy(grad_ref, own_ref.at[pl.ds(0, nx)], arrived.at[2]),
         pltpu.make_async_copy(feat_ref, own_ref.at[pl.ds(nx, nx)], arrived.at[3]),
     ]
@@ -253,15 +342,30 @@
 
 def rims_kernel(m, left_ref, right_ref, out_ref):
     g = lax.axis_index("grp")
-    halo = left_ref.shape[0]
-    left = left_ref[...]
-    right = right_ref[...]
-    out_ref[:halo] = jnp.where(g > 0, left, jnp.zeros_like(left))
-    out_ref[halo:] = jnp.where(g < m - 1, right, jnp.zeros_like(right))
-
-
-def fold_kernel(bit, keep_ref, got_ref, held_ref, send_ref):
+    halo = left_ref.shape[0] - 1
+    left, right = left_ref[...], right_ref[...]
+    left = jnp.where(g > 0, left, jnp.zeros_like(left))
+    right = jnp.where(g < m - 1, right, jnp.zeros_like(right))
+    out_ref[:halo] = left[:halo]
+    out_ref[halo : 2 * halo] = right[:halo]
+    out_ref[2 * halo] = left[halo]
+    out_ref[2 * halo + 1] = right[halo]
+
+
+def fold_kernel(bit, keep_ref, got_ref, *refs):
+    extra, (held_ref, send_ref) = refs[:-2], refs[-2:]
     total = keep_ref[...] + got_ref[...].astype(F32)
+    if extra:
+        (outer_ref,) = extra
+        third = outer_ref.shape[2]
+        total = jnp.concatenate(
+            [
+                total[:, :third] + outer_ref[0],
+                total[:, third : 2 * third],
+                total[:, 2 * third :] + outer_ref[1],
+            ],
+            axis=1,
+        )
     half = held_ref.shape[0]
     upper = lax.rem(lax.axis_index("grp") // 2**bit, 2) == 1
     held_ref[...] = jnp.where(upper, total[half:], total[:half])
@@ -327,11 +431,11 @@
     width = filters_half.shape[4]
     lanes = 27 * (ch // n)
     shape = jax.ShapeDtypeStruct
-    edge = shape((HALO, ny, nz, ch), BF16)
+    edge = shape((HALO + 1, ny, nz, ch), BF16)
     own, first, last = call(
         load_kernel,
         [shape((2 * nx, ny, nz, ch), BF16), edge, edge],
-        [pltpu.SemaphoreType.DMA((4,))],
+        [pltpu.SemaphoreType.DMA((6,))],
         (grad_out, feat_full),
         far=2,
     )
@@ -340,7 +444,7 @@
     bricks = gather(own)
     (rim,) = call(
         lambda *refs: rims_kernel(m, *refs),
-        [shape((2 * HALO, ny, nz, ch), BF16)],
+        [shape((2 * HALO + 2, ny, nz, ch), BF16)],
         [],
         (from_left, from_right),
     )
@@ -350,27 +454,38 @@
     keep, send = call(
         lambda *refs: taps_kernel(n, m, *refs),
         [shape((ch // 2, lanes), F32), shape((ch // 2, lanes), BF16)],
+        [pltpu.VMEM((nx, n * ny + 2, nz, ch), BF16), pltpu.VMEM((ch, lanes), F32)],
+        tuple(bricks),
+    )
+    (outer,) = call(
+        lambda *refs: outer_kernel(n, m, *refs),
+        [shape((2, ch // 2, lanes // 3), F32)],
+        [pltpu.VMEM((4, n * ny + 2, nz, ch), BF16)],
+        (*bricks, *rims),
+    )
+    got = swap(send, "grp", 1)
+    (inner,) = call(
+        lambda *refs: inner_kernel(n, *refs),
+        [shape((2, nx + 2, n * ny, half_z, ch), F32)],
         [
-            pltpu.VMEM((nx + 2, n * ny + 2, nz, ch), BF16),
-            pltpu.VMEM((ch, lanes), F32),
+            pltpu.VMEM((nx * ny, nz, ch), F32),
+            pltpu.VMEM((4, half_x, n * ny + 2, nz, ch), BF16),
         ],
-        (*bricks, *rims),
-    )
-    got = swap(send, "grp", 1)
+        (*bricks, full),
+    )
     chunk = (half_y // n, half_x, half_z, filters_half.shape[3])
-    deep = nx + 2 * HALO
     chunks = call(
         lambda *refs: main_kernel(n, m, *refs),
         [shape(chunk, F32)] + [shape(chunk, BF16)] * (n - 1),
         [
-            pltpu.VMEM((deep * ny, nz, ch), F32),
-            pltpu.VMEM((4, deep // 2, n * ny + 2, nz, ch), BF16),
+            pltpu.VMEM((2 * HALO * ny, nz, ch), F32),
+            pltpu.VMEM((4, HALO, n * ny + 2, nz, ch), BF16),
             pltpu.VMEM((3, half_y + 2, half_x + 2, half_z, width), F32),
             pltpu.VMEM((n,) + chunk, F32),
             pltpu.VMEM(filters_half.shape, BF16),
             pltpu.SemaphoreType.DMA,
         ],
-        (*bricks, *rims, full, up, filters_half),
+        (*rims, inner, full, up, filters_half),
         far=1,
     )
     parts = [chunks[0]]
@@ -383,7 +498,7 @@
             lambda *refs: fold_kernel(bit, *refs),
             [shape((rows, lanes), F32), shape((rows, lanes), BF16)],
             [],
-            (keep, got),
+            (keep, got) if bit > 1 else (keep, got, outer),
         )
         got = swap(send, "grp", 2**bit)
     (taps_grad,) = call(

time: 41.6 us -> 38.1 us (0.916)
  waiting for transfers between devices: 14.8 us -> 10.3 us
  Pallas kernels: 8.99 us -> 10.3 us
    ppermute x12, waiting for transfers between devices: 12.9 us -> 8.2 us  [swap(): return lax.ppermute(value, axis, [(i, i ^ k) for i in range(n)])]
    pallas_call x8 -> x10, Pallas kernels: 7.76 us -> 9.06 us  [call(): pl.pallas_call(kernel, out_shape=[pltpu.VMEM(v.shape, v.dtype) if placed...]
  transfers between devices with their start and end apart: 14 -> 14, of which waited for: 7 -> 7; matrix products, arithmetic and copies ran while one was open for 0% -> 0% of each run, Pallas kernels for 15% -> 22%
where the time goes in v2:
time: 38.1 us; the launch traced here: 37.8 us
  starting transfers between devices  16.6 us (44%)
  Pallas kernels  10.3 us (27%)
  waiting for transfers between devices  10.3 us (27%)
  between operations  0.71 us (2%)
    ppermute x12, starting transfers between devices, swap(): return lax.ppermute(value, axis, [(i, i ^ k) for i in range(n)])  11.8 us
    pallas_call x10, Pallas kernels, call(): pl.pallas_call(kernel, out_shape=[pltpu.VMEM(v.shape, v.dtype) if placed...  9.06 us
    ppermute x12, waiting for transfers between devices, swap(): return lax.ppermute(value, axis, [(i, i ^ k) for i in range(n)])  8.2 us
    ppermute x2, starting transfers between devices, shift(): return lax.ppermute(value, axis, [(i, (i + step) % n) for i in range(n)])  4.81 us
    ppermute x2, waiting for transfers between devices, shift(): return lax.ppermute(value, axis, [(i, (i + step) % n) for i in range(n)])  2.06 us
    pallas_call x1, Pallas kernels, fetch(): pl.pallas_call(fetch_kernel, out_shape=[pltpu.VMEM(shape, BF16) for shape...  1.23 us
  transfers between devices with their start and end apart: 14, of which 7 were waited for; matrix products, arithmetic and copies ran while one was open for 0% of the time, Pallas kernels for 22%

profile of v2, /device:TPU:0, one launch (start us, length us, event | category | flops | bytes accessed | tf_op | source)
XLA Modules:
  0.0 37.8 jit_solution(15580012702327161408)
XLA Ops:
  0.6 1.0 %shard_map.68 = (bf16[16,2,16,128]{3,2,1,0:T(8,128)(2,1)S(1)}, bf16[4,2,16,128]{3,2,1,0:T(8,128)(2,1)S(1)}, bf16[4,2,16,128]{3,2,1,0:T(8,128)(2,1)S(1)}) custom-call(bf16[8,2,16,128]{3,2,1,0:T(8,128)(2,1)} %grad_ref.1, bf16[8,2,16,128]{3,2,1,0:T(8,128)(2,1)} %feat_ref.1), custom_call_target="tpu_custom_call" | custom-call | tf_op jit(solution)/shard_map/pallas_call | solution.py:395
  1.6 3.0 %collective-permute-start.6 = (bf16[16,2,16,128]{3,2,1,0:T(8,128)(2,1)S(1)}, bf16[16,2,16,128]{3,2,1,0:T(8,128)(2,1)S(1)}, u32[]{:S(2)}, u32[]{:S(2)}) collective-permute-start(bf16[16,2,16,128]{3,2,1,0:T(8,128)(2,1)S(1)} %get-tuple-element.19.refs_0_), channel_id=1, source_target_pairs={{0,2},{1,3},{2,0},{3,1},{4,6},{5,7},{6,4},{7,5},{8,10},{9,11},{10,... | collective-permute-start | bytes 393224 | tf_op jit(solution)/shard_map/ppermute | solution.py:23
  4.7 0.0 collective-permute-start.5
  4.7 3.5 %collective-permute-done.6.refs_2_ = bf16[16,2,16,128]{3,2,1,0:T(8,128)(2,1)S(1)} collective-permute-done((bf16[16,2,16,128]{3,2,1,0:T(8,128)(2,1)S(1)}, bf16[16,2,16,128]{3,2,1,0:T(8,128)(2,1)S(1)}, u32[]{:S(2)}, u32[]{:S(2)}) %collective-permute-start.6) | collective-permute-done | bytes 131104 | tf_op jit(solution)/shard_map/ppermute | solution.py:23
  8.2 0.0 collective-permute-start.7
  8.2 1.8 %collective-permute-start = (bf16[4,2,16,128]{3,2,1,0:T(8,128)(2,1)S(1)}, bf16[4,2,16,128]{3,2,1,0:T(8,128)(2,1)S(1)}, u32[]{:S(2)}, u32[]{:S(2)}) collective-permute-start(bf16[4,2,16,128]{3,2,1,0:T(8,128)(2,1)S(1)} %get-tuple-element.17), channel_id=1, source_target_pairs={{0,4},{4,8},{8,12},{12,16},{16,20},{20,24},{24,28},{28,0},{1,5},{5... | collective-permute-start | bytes 98312 | tf_op jit(solution)/shard_map/ppermute | solution.py:28
  9.9 3.0 %collective-permute-start.1 = (bf16[4,2,16,128]{3,2,1,0:T(8,128)(2,1)S(1)}, bf16[4,2,16,128]{3,2,1,0:T(8,128)(2,1)S(1)}, u32[]{:S(2)}, u32[]{:S(2)}) collective-permute-start(bf16[4,2,16,128]{3,2,1,0:T(8,128)(2,1)S(1)} %get-tuple-element.18), channel_id=1, source_target_pairs={{0,28},{4,0},{8,4},{12,8},{16,12},{20,16},{24,20},{28,24},{1,29},{... | collective-permute-start | bytes 98312 | tf_op jit(solution)/shard_map/ppermute | solution.py:28
  13.0 2.1 %collective-permute-done.refs_0_ = bf16[4,2,16,128]{3,2,1,0:T(8,128)(2,1)S(1)} collective-permute-done((bf16[4,2,16,128]{3,2,1,0:T(8,128)(2,1)S(1)}, bf16[4,2,16,128]{3,2,1,0:T(8,128)(2,1)S(1)}, u32[]{:S(2)}, u32[]{:S(2)}) %collective-permute-start) | collective-permute-done | bytes 32800 | tf_op jit(solution)/shard_map/ppermute | solution.py:28
  15.0 0.0 collective-permute-done.1.refs_1_
  15.1 1.6 %collective-permute-start.3 = (bf16[8,2,16,128]{3,2,1,0:T(8,128)(2,1)S(1)}, bf16[8,2,16,128]{3,2,1,0:T(8,128)(2,1)S(1)}, u32[]{:S(2)}, u32[]{:S(2)}) collective-permute-start(bf16[8,2,16,128]{3,2,1,0:T(8,128)(2,1)S(1)} %shard_map.69.refs_0_.refs_4_), channel_id=1, source_target_pairs={{0,2},{1,3},{2,0},{3,1},{4,6},{5,7},{6,4},{7,5},{8,10},{9,11},{10,... | collective-permute-start | bytes 196616 | tf_op jit(solution)/shard_map/ppermute | solution.py:23
  16.6 0.0 collective-permute-done.5.refs_1_
  16.6 0.0 collective-permute-done.7.refs_3_
  16.6 1.0 %shard_map.74 = (f32[64,864]{1,0:T(8,128)S(1)}, bf16[64,864]{1,0:T(8,128)(2,1)S(1)}) custom-call(bf16[16,2,16,128]{3,2,1,0:T(8,128)(2,1)S(1)} %get-tuple-element.19.refs_0_, bf16[16,2,16,128]{3,2,1,0:T(8,128)(2,1)S(1)} %collective-permute-done.5.refs_1_, bf16[16,2,16,128]{3,2,1,0:T(8,128)(2,1)S(1)} %collective-permute-done.6.refs_2_, ...), custom_call_target="tpu_custom_call" | custom-call | tf_op jit(solution)/shard_map/pallas_call | solution.py:395
  17.6 1.3 %collective-permute-start.11 = (bf16[64,864]{1,0:T(8,128)(2,1)S(1)}, bf16[64,864]{1,0:T(8,128)(2,1)S(1)}, u32[]{:S(2)}, u32[]{:S(2)}) collective-permute-start(bf16[64,864]{1,0:T(8,128)(2,1)S(1)} %get-tuple-element.27), channel_id=1, source_target_pairs={{0,4},{4,0},{8,12},{12,8},{16,20},{20,16},{24,28},{28,24},{1,5},{5... | collective-permute-start | bytes 331784 | tf_op jit(solution)/shard_map/ppermute | solution.py:23
  18.9 0.0 collective-permute-start.2
  18.9 0.5 %collective-permute-done.3.refs_2_.refs_6_ = bf16[8,2,16,128]{3,2,1,0:T(8,128)(2,1)S(1)} collective-permute-done((bf16[8,2,16,128]{3,2,1,0:T(8,128)(2,1)S(1)}, bf16[8,2,16,128]{3,2,1,0:T(8,128)(2,1)S(1)}, u32[]{:S(2)}, u32[]{:S(2)}) %collective-permute-start.3) | collective-permute-done | bytes 65568 | tf_op jit(solution)/shard_map/ppermute | solution.py:23
  19.4 0.0 collective-permute-start.4
  19.4 0.7 %collective-permute-done.2.refs_1_.refs_5_ = bf16[8,2,16,128]{3,2,1,0:T(8,128)(2,1)S(1)} collective-permute-done((bf16[8,2,16,128]{3,2,1,0:T(8,128)(2,1)S(1)}, bf16[8,2,16,128]{3,2,1,0:T(8,128)(2,1)S(1)}, u32[]{:S(2)}, u32[]{:S(2)}) %collective-permute-start.2) | collective-permute-done | bytes 65568 | tf_op jit(solution)/shard_map/ppermute | solution.py:23
  20.2 0.5 %collective-permute-done.4.refs_3_.refs_7_ = bf16[8,2,16,128]{3,2,1,0:T(8,128)(2,1)S(1)} collective-permute-done((bf16[8,2,16,128]{3,2,1,0:T(8,128)(2,1)S(1)}, bf16[8,2,16,128]{3,2,1,0:T(8,128)(2,1)S(1)}, u32[]{:S(2)}, u32[]{:S(2)}) %collective-permute-start.4) | collective-permute-done | bytes 65568 | tf_op jit(solution)/shard_map/ppermute | solution.py:23
  20.6 0.6 %shard_map.75.refs_2_ = f32[2,64,288]{2,1,0:T(8,128)S(1)} custom-call(bf16[16,2,16,128]{3,2,1,0:T(8,128)(2,1)S(1)} %get-tuple-element.19.refs_0_, bf16[16,2,16,128]{3,2,1,0:T(8,128)(2,1)S(1)} %collective-permute-done.5.refs_1_, bf16[16,2,16,128]{3,2,1,0:T(8,128)(2,1)S(1)} %collective-permute-done.6.refs_2_, ...), custom_call_target="tpu_custom_call" | custom-call | tf_op jit(solution)/shard_map/pallas_call | solution.py:395
  21.3 1.2 %collective-permute-done.11.refs_1_ = bf16[64,864]{1,0:T(8,128)(2,1)S(1)} collective-permute-done((bf16[64,864]{1,0:T(8,128)(2,1)S(1)}, bf16[64,864]{1,0:T(8,128)(2,1)S(1)}, u32[]{:S(2)}, u32[]{:S(2)}) %collective-permute-start.11) | collective-permute-done | bytes 110624 | tf_op jit(solution)/shard_map/ppermute | solution.py:23
  22.5 0.1 shard_map.76
  22.6 0.8 %collective-permute-start.12 = (bf16[32,864]{1,0:T(8,128)(2,1)S(1)}, bf16[32,864]{1,0:T(8,128)(2,1)S(1)}, u32[]{:S(2)}, u32[]{:S(2)}) collective-permute-start(bf16[32,864]{1,0:T(8,128)(2,1)S(1)} %get-tuple-element.29), channel_id=1, source_target_pairs={{0,8},{4,12},{8,0},{12,4},{16,24},{20,28},{24,16},{28,20},{1,9},{5... | collective-permute-start | bytes 165896 | tf_op jit(solution)/shard_map/ppermute | solution.py:23
  23.4 1.2 %shard_map.70 = (bf16[3,3,3,128,128]{4,3,2,1,0:T(8,128)(2,1)S(1)}, bf16[2,2,2,128,128]{4,3,2,1,0:T(8,128)(2,1)S(1)}) custom-call(bf16[3,3,3,128,128]{4,3,2,1,0:T(8,128)(2,1)} %refs_0_.1, bf16[2,2,2,512,128]{4,3,2,1,0:T(8,128)(2,1)} %refs_1_.1), custom_call_target="tpu_custom_call" | custom-call | tf_op jit(solution)/shard_map/pallas_call | solution.py:407
  24.7 1.6 %shard_map.71.refs_4_ = f32[2,10,8,8,128]{4,3,2,1,0:T(8,128)S(1)} custom-call(bf16[16,2,16,128]{3,2,1,0:T(8,128)(2,1)S(1)} %get-tuple-element.19.refs_0_, bf16[16,2,16,128]{3,2,1,0:T(8,128)(2,1)S(1)} %collective-permute-done.5.refs_1_, bf16[16,2,16,128]{3,2,1,0:T(8,128)(2,1)S(1)} %collective-permute-done.6.refs_2_, ...), custom_call_target="tpu_custom_call" | custom-call | tf_op jit(solution)/shard_map/pallas_call | solution.py:395
  26.2 3.3 %shard_map.72 = (f32[1,4,8,512]{3,2,1,0:T(8,128)S(1)}, bf16[1,4,8,512]{3,2,1,0:T(8,128)(2,1)S(1)}, bf16[1,4,8,512]{3,2,1,0:T(8,128)(2,1)S(1)}, bf16[1,4,8,512]{3,2,1,0:T(8,128)(2,1)S(1)}) custom-call(bf16[8,2,16,128]{3,2,1,0:T(8,128)(2,1)S(1)} %shard_map.69.refs_0_.refs_4_, bf16[8,2,16,128]{3,2,1,0:T(8,128)(2,1)S(1)} %collective-permute-done.2.refs_1_.refs_5_, ...), custom_call_target="tpu_custom_call" | custom-call | tf_op jit(solution)/shard_map/pallas_call | solution.py:395
  29.5 0.1 collective-permute-start.8
  29.6 0.6 %collective-permute-start.9 = (bf16[1,4,8,512]{3,2,1,0:T(8,128)(2,1)S(1)}, bf16[1,4,8,512]{3,2,1,0:T(8,128)(2,1)S(1)}, u32[]{:S(2)}, u32[]{:S(2)}) collective-permute-start(bf16[1,4,8,512]{3,2,1,0:T(8,128)(2,1)S(1)} %get-tuple-element.24), channel_id=1, source_target_pairs={{0,2},{1,3},{2,0},{3,1},{4,6},{5,7},{6,4},{7,5},{8,10},{9,11},{10,... | collective-permute-start | bytes 98312 | tf_op jit(solution)/shard_map/ppermute | solution.py:23
  30.2 1.2 %collective-permute-start.10 = (bf16[1,4,8,512]{3,2,1,0:T(8,128)(2,1)S(1)}, bf16[1,4,8,512]{3,2,1,0:T(8,128)(2,1)S(1)}, u32[]{:S(2)}, u32[]{:S(2)}) collective-permute-start(bf16[1,4,8,512]{3,2,1,0:T(8,128)(2,1)S(1)} %get-tuple-element.25), channel_id=1, source_target_pairs={{0,3},{1,2},{2,1},{3,0},{4,7},{5,6},{6,5},{7,4},{8,11},{9,10},{10,... | collective-permute-start | bytes 98312 | tf_op jit(solution)/shard_map/ppermute | solution.py:23
  31.5 0.0 collective-permute-done.12.refs_1_
  31.5 3.1 %collective-permute-start.13 = (bf16[16,864]{1,0:T(8,128)(2,1)S(1)}, bf16[16,864]{1,0:T(8,128)(2,1)S(1)}, u32[]{:S(2)}, u32[]{:S(2)}) collective-permute-start(bf16[16,864]{1,0:T(8,128)(2,1)S(1)} %get-tuple-element.31), channel_id=1, source_target_pairs={{0,16},{4,20},{8,24},{12,28},{16,0},{20,4},{24,8},{28,12},{1,17},{... | collective-permute-start | bytes 82952 | tf_op jit(solution)/shard_map/ppermute | solution.py:23
  34.6 0.0 collective-permute-done.8.refs_1_
  34.6 0.0 collective-permute-done.9.refs_2_
  34.6 0.0 collective-permute-done.10.refs_3_
  34.6 0.6 %shard_map.73 = bf16[1,4,8,512]{3,2,1,0:T(8,128)(2,1)} custom-call(f32[1,4,8,512]{3,2,1,0:T(8,128)S(1)} %get-tuple-element.22.refs_0_, bf16[1,4,8,512]{3,2,1,0:T(8,128)(2,1)S(1)} %collective-permute-done.8.refs_1_, bf16[1,4,8,512]{3,2,1,0:T(8,128)(2,1)S(1)} %collective-permute-done.9.refs_2_, bf16[1,4,8,512]{3,2,1,0:T(8,128)(2,1)S(1)} %collective-permute-done.10.refs_3_), custom_call_target="tpu_custom_call" | custom-call | tf_op jit(solution)/shard_map/pallas_call | solution.py:395
  35.3 1.8 %collective-permute-done.13.got_ref = bf16[16,864]{1,0:T(8,128)(2,1)S(1)} collective-permute-done((bf16[16,864]{1,0:T(8,128)(2,1)S(1)}, bf16[16,864]{1,0:T(8,128)(2,1)S(1)}, u32[]{:S(2)}, u32[]{:S(2)}) %collective-permute-start.13) | collective-permute-done | bytes 27680 | tf_op jit(solution)/shard_map/ppermute | solution.py:23
  37.0 0.8 %shard_map.78 = f32[3,3,3,16,32]{4,3,2,1,0:T(8,128)} custom-call(f32[16,864]{1,0:T(8,128)S(1)} %get-tuple-element.30.keep_ref, bf16[16,864]{1,0:T(8,128)(2,1)S(1)} %collective-permute-done.13.got_ref), custom_call_target="tpu_custom_call" | custom-call | tf_op jit(solution)/shard_map/pallas_call | solution.py:395
  (2 shorter events, 0.0 us)
Async XLA Ops:
  1.6 6.5 %collective-permute-start.6 = (bf16[16,2,16,128]{3,2,1,0:T(8,128)(2,1)S(1)}, bf16[16,2,16,128]{3,2,1,0:T(8,128)(2,1)S(1)}, u32[]{:S(2)}, u32[]{:S(2)}) collective-permute-start(bf16[16,2,16,128]{3,2,1,0:T(8,128)(2,1)S(1)} %get-tuple-element.19.refs_0_), channel_id=1, source_target_pairs={{0,2},{1,3},{2,0},{3,1},{4,6},{5,7},{6,4},{7,5},{8,10},{9,11},{10,... | collective-permute-start | bytes 393224 | tf_op jit(solution)/shard_map/ppermute | solution.py:23
  4.7 12.0 %collective-permute-start.5 = (bf16[16,2,16,128]{3,2,1,0:T(8,128)(2,1)S(1)}, bf16[16,2,16,128]{3,2,1,0:T(8,128)(2,1)S(1)}, u32[]{:S(2)}, u32[]{:S(2)}) collective-permute-start(bf16[16,2,16,128]{3,2,1,0:T(8,128)(2,1)S(1)} %get-tuple-element.19.refs_0_), channel_id=1, source_target_pairs={{0,1},{1,0},{2,3},{3,2},{4,5},{5,4},{6,7},{7,6},{8,9},{9,8},{10,11... | collective-permute-start | bytes 393224 | tf_op jit(solution)/shard_map/ppermute | solution.py:23
  8.2 8.5 %collective-permute-start.7 = (bf16[16,2,16,128]{3,2,1,0:T(8,128)(2,1)S(1)}, bf16[16,2,16,128]{3,2,1,0:T(8,128)(2,1)S(1)}, u32[]{:S(2)}, u32[]{:S(2)}) collective-permute-start(bf16[16,2,16,128]{3,2,1,0:T(8,128)(2,1)S(1)} %collective-permute-done.6.refs_2_), channel_id=1, source_target_pairs={{0,1},{1,0},{2,3},{3,2},{4,5},{5,4},{6,7},{7,6},{8,9},{9,8},{10,11... | collective-permute-start | bytes 393224 | tf_op jit(solution)/shard_map/ppermute | solution.py:23
  8.2 6.9 %collective-permute-start = (bf16[4,2,16,128]{3,2,1,0:T(8,128)(2,1)S(1)}, bf16[4,2,16,128]{3,2,1,0:T(8,128)(2,1)S(1)}, u32[]{:S(2)}, u32[]{:S(2)}) collective-permute-start(bf16[4,2,16,128]{3,2,1,0:T(8,128)(2,1)S(1)} %get-tuple-element.17), channel_id=1, source_target_pairs={{0,4},{4,8},{8,12},{12,16},{16,20},{20,24},{24,28},{28,0},{1,5},{5... | collective-permute-start | bytes 98312 | tf_op jit(solution)/shard_map/ppermute | solution.py:28
  9.9 5.1 %collective-permute-start.1 = (bf16[4,2,16,128]{3,2,1,0:T(8,128)(2,1)S(1)}, bf16[4,2,16,128]{3,2,1,0:T(8,128)(2,1)S(1)}, u32[]{:S(2)}, u32[]{:S(2)}) collective-permute-start(bf16[4,2,16,128]{3,2,1,0:T(8,128)(2,1)S(1)} %get-tuple-element.18), channel_id=1, source_target_pairs={{0,28},{4,0},{8,4},{12,8},{16,12},{20,16},{24,20},{28,24},{1,29},{... | collective-permute-start | bytes 98312 | tf_op jit(solution)/shard_map/ppermute | solution.py:28
  15.1 4.3 %collective-permute-start.3 = (bf16[8,2,16,128]{3,2,1,0:T(8,128)(2,1)S(1)}, bf16[8,2,16,128]{3,2,1,0:T(8,128)(2,1)S(1)}, u32[]{:S(2)}, u32[]{:S(2)}) collective-permute-start(bf16[8,2,16,128]{3,2,1,0:T(8,128)(2,1)S(1)} %shard_map.69.refs_0_.refs_4_), channel_id=1, source_target_pairs={{0,2},{1,3},{2,0},{3,1},{4,6},{5,7},{6,4},{7,5},{8,10},{9,11},{10,... | collective-permute-start | bytes 196616 | tf_op jit(solution)/shard_map/ppermute | solution.py:23
  17.6 4.9 %collective-permute-start.11 = (bf16[64,864]{1,0:T(8,128)(2,1)S(1)}, bf16[64,864]{1,0:T(8,128)(2,1)S(1)}, u32[]{:S(2)}, u32[]{:S(2)}) collective-permute-start(bf16[64,864]{1,0:T(8,128)(2,1)S(1)} %get-tuple-element.27), channel_id=1, source_target_pairs={{0,4},{4,0},{8,12},{12,8},{16,20},{20,16},{24,28},{28,24},{1,5},{5... | collective-permute-start | bytes 331784 | tf_op jit(solution)/shard_map/ppermute | solution.py:23
  18.9 1.3 %collective-permute-start.2 = (bf16[8,2,16,128]{3,2,1,0:T(8,128)(2,1)S(1)}, bf16[8,2,16,128]{3,2,1,0:T(8,128)(2,1)S(1)}, u32[]{:S(2)}, u32[]{:S(2)}) collective-permute-start(bf16[8,2,16,128]{3,2,1,0:T(8,128)(2,1)S(1)} %shard_map.69.refs_0_.refs_4_), channel_id=1, source_target_pairs={{0,1},{1,0},{2,3},{3,2},{4,5},{5,4},{6,7},{7,6},{8,9},{9,8},{10,11... | collective-permute-start | bytes 196616 | tf_op jit(solution)/shard_map/ppermute | solution.py:23
  19.4 1.3 %collective-permute-start.4 = (bf16[8,2,16,128]{3,2,1,0:T(8,128)(2,1)S(1)}, bf16[8,2,16,128]{3,2,1,0:T(8,128)(2,1)S(1)}, u32[]{:S(2)}, u32[]{:S(2)}) collective-permute-start(bf16[8,2,16,128]{3,2,1,0:T(8,128)(2,1)S(1)} %collective-permute-done.3.refs_2_.refs_6_), channel_id=1, source_target_pairs={{0,1},{1,0},{2,3},{3,2},{4,5},{5,4},{6,7},{7,6},{8,9},{9,8},{10,11... | collective-permute-start | bytes 196616 | tf_op jit(solution)/shard_map/ppermute | solution.py:23
  22.6 8.9 %collective-permute-start.12 = (bf16[32,864]{1,0:T(8,128)(2,1)S(1)}, bf16[32,864]{1,0:T(8,128)(2,1)S(1)}, u32[]{:S(2)}, u32[]{:S(2)}) collective-permute-start(bf16[32,864]{1,0:T(8,128)(2,1)S(1)} %get-tuple-element.29), channel_id=1, source_target_pairs={{0,8},{4,12},{8,0},{12,4},{16,24},{20,28},{24,16},{28,20},{1,9},{5... | collective-permute-start | bytes 165896 | tf_op jit(solution)/shard_map/ppermute | solution.py:23
  29.5 5.1 %collective-permute-start.8 = (bf16[1,4,8,512]{3,2,1,0:T(8,128)(2,1)S(1)}, bf16[1,4,8,512]{3,2,1,0:T(8,128)(2,1)S(1)}, u32[]{:S(2)}, u32[]{:S(2)}) collective-permute-start(bf16[1,4,8,512]{3,2,1,0:T(8,128)(2,1)S(1)} %get-tuple-element.23), channel_id=1, source_target_pairs={{0,1},{1,0},{2,3},{3,2},{4,5},{5,4},{6,7},{7,6},{8,9},{9,8},{10,11... | collective-permute-start | bytes 98312 | tf_op jit(solution)/shard_map/ppermute | solution.py:23
  29.6 5.0 %collective-permute-start.9 = (bf16[1,4,8,512]{3,2,1,0:T(8,128)(2,1)S(1)}, bf16[1,4,8,512]{3,2,1,0:T(8,128)(2,1)S(1)}, u32[]{:S(2)}, u32[]{:S(2)}) collective-permute-start(bf16[1,4,8,512]{3,2,1,0:T(8,128)(2,1)S(1)} %get-tuple-element.24), channel_id=1, source_target_pairs={{0,2},{1,3},{2,0},{3,1},{4,6},{5,7},{6,4},{7,5},{8,10},{9,11},{10,... | collective-permute-start | bytes 98312 | tf_op jit(solution)/shard_map/ppermute | solution.py:23
  30.2 4.4 %collective-permute-start.10 = (bf16[1,4,8,512]{3,2,1,0:T(8,128)(2,1)S(1)}, bf16[1,4,8,512]{3,2,1,0:T(8,128)(2,1)S(1)}, u32[]{:S(2)}, u32[]{:S(2)}) collective-permute-start(bf16[1,4,8,512]{3,2,1,0:T(8,128)(2,1)S(1)} %get-tuple-element.25), channel_id=1, source_target_pairs={{0,3},{1,2},{2,1},{3,0},{4,7},{5,6},{6,5},{7,4},{8,11},{9,10},{10,... | collective-permute-start | bytes 98312 | tf_op jit(solution)/shard_map/ppermute | solution.py:23
  31.5 5.5 %collective-permute-start.13 = (bf16[16,864]{1,0:T(8,128)(2,1)S(1)}, bf16[16,864]{1,0:T(8,128)(2,1)S(1)}, u32[]{:S(2)}, u32[]{:S(2)}) collective-permute-start(bf16[16,864]{1,0:T(8,128)(2,1)S(1)} %get-tuple-element.31), channel_id=1, source_target_pairs={{0,16},{4,20},{8,24},{12,28},{16,0},{20,4},{24,8},{28,12},{1,17},{... | collective-permute-start | bytes 82952 | tf_op jit(solution)/shard_map/ppermute | solution.py:23

commit v3 on v2

--- a/solution.py
+++ b/solution.py
@@ -115,8 +115,11 @@
         refs[n + 4 : 2 * n + 4],
         refs[2 * n + 4 :],
     )
-    load = pltpu.make_async_copy(half_ref, held, arrived)
-    load.start()
+    loads = [
+        pltpu.make_async_copy(half_ref.at[p], held.at[p], arrived.at[p]) for p in range(3)
+    ]
+    for load in loads:
+        load.start()
     halo = rims[0].shape[0] // 2 - 1
     nx, rows, half_z, ch = inner_ref.shape[1:]
     nx = nx - 2
@@ -170,8 +173,8 @@
         padded[2, 1 : half_y + 1, i] = jnp.where(level == 0, 0.0, pltpu.roll(plane, 1, 1))
     cells = half_y * half_x * half_z
     total = None
-    load.wait()
     for p in range(3):
+        loads[p].wait()
         windows = [
             padded[r, 2 - q : 2 - q + half_y, 2 - p : 2 - p + half_x]
             .reshape(cells, width)
@@ -483,7 +486,7 @@
             pltpu.VMEM((3, half_y + 2, half_x + 2, half_z, width), F32),
             pltpu.VMEM((n,) + chunk, F32),
             pltpu.VMEM(filters_half.shape, BF16),
-            pltpu.SemaphoreType.DMA,
+            pltpu.SemaphoreType.DMA((3,)),
         ],
         (*rims, inner, full, up, filters_half),
         far=1,

time: 38.1 us -> 37.7 us (0.990)
  no operation moved by 1% of the time
where the time goes in v3:
time: 37.7 us; the launch traced here: 37.5 us
  starting transfers between devices  16.6 us (44%)
  waiting for transfers between devices  10.3 us (27%)
  Pallas kernels  9.99 us (26%)
  between operations  0.71 us (2%)
    ppermute x12, starting transfers between devices, swap(): return lax.ppermute(value, axis, [(i, i ^ k) for i in range(n)])  11.8 us
    pallas_call x10, Pallas kernels, call(): pl.pallas_call(kernel, out_shape=[pltpu.VMEM(v.shape, v.dtype) if placed...  8.76 us
    ppermute x12, waiting for transfers between devices, swap(): return lax.ppermute(value, axis, [(i, i ^ k) for i in range(n)])  8.2 us
    ppermute x2, starting transfers between devices, shift(): return lax.ppermute(value, axis, [(i, (i + step) % n) for i in range(n)])  4.81 us
    ppermute x2, waiting for transfers between devices, shift(): return lax.ppermute(value, axis, [(i, (i + step) % n) for i in range(n)])  2.06 us
    pallas_call x1, Pallas kernels, fetch(): pl.pallas_call(fetch_kernel, out_shape=[pltpu.VMEM(shape, BF16) for shape...  1.23 us
  transfers between devices with their start and end apart: 14, of which 7 were waited for; matrix products, arithmetic and copies ran while one was open for 0% of the time, Pallas kernels for 22%

profile of v3, /device:TPU:0, one launch (start us, length us, event | category | flops | bytes accessed | tf_op | source)
XLA Modules:
  0.0 37.5 jit_solution(11500909200490998810)
XLA Ops:
  0.6 1.0 %shard_map.68 = (bf16[16,2,16,128]{3,2,1,0:T(8,128)(2,1)S(1)}, bf16[4,2,16,128]{3,2,1,0:T(8,128)(2,1)S(1)}, bf16[4,2,16,128]{3,2,1,0:T(8,128)(2,1)S(1)}) custom-call(bf16[8,2,16,128]{3,2,1,0:T(8,128)(2,1)} %grad_ref.1, bf16[8,2,16,128]{3,2,1,0:T(8,128)(2,1)} %feat_ref.1), custom_call_target="tpu_custom_call" | custom-call | tf_op jit(solution)/shard_map/pallas_call | solution.py:398
  1.6 3.0 %collective-permute-start.6 = (bf16[16,2,16,128]{3,2,1,0:T(8,128)(2,1)S(1)}, bf16[16,2,16,128]{3,2,1,0:T(8,128)(2,1)S(1)}, u32[]{:S(2)}, u32[]{:S(2)}) collective-permute-start(bf16[16,2,16,128]{3,2,1,0:T(8,128)(2,1)S(1)} %get-tuple-element.19.refs_0_), channel_id=1, source_target_pairs={{0,2},{1,3},{2,0},{3,1},{4,6},{5,7},{6,4},{7,5},{8,10},{9,11},{10,... | collective-permute-start | bytes 393224 | tf_op jit(solution)/shard_map/ppermute | solution.py:23
  4.7 0.0 collective-permute-start.5
  4.7 3.5 %collective-permute-done.6.refs_2_ = bf16[16,2,16,128]{3,2,1,0:T(8,128)(2,1)S(1)} collective-permute-done((bf16[16,2,16,128]{3,2,1,0:T(8,128)(2,1)S(1)}, bf16[16,2,16,128]{3,2,1,0:T(8,128)(2,1)S(1)}, u32[]{:S(2)}, u32[]{:S(2)}) %collective-permute-start.6) | collective-permute-done | bytes 131104 | tf_op jit(solution)/shard_map/ppermute | solution.py:23
  8.2 0.0 collective-permute-start.7
  8.2 1.8 %collective-permute-start = (bf16[4,2,16,128]{3,2,1,0:T(8,128)(2,1)S(1)}, bf16[4,2,16,128]{3,2,1,0:T(8,128)(2,1)S(1)}, u32[]{:S(2)}, u32[]{:S(2)}) collective-permute-start(bf16[4,2,16,128]{3,2,1,0:T(8,128)(2,1)S(1)} %get-tuple-element.17), channel_id=1, source_target_pairs={{0,4},{4,8},{8,12},{12,16},{16,20},{20,24},{24,28},{28,0},{1,5},{5... | collective-permute-start | bytes 98312 | tf_op jit(solution)/shard_map/ppermute | solution.py:28
  9.9 3.0 %collective-permute-start.1 = (bf16[4,2,16,128]{3,2,1,0:T(8,128)(2,1)S(1)}, bf16[4,2,16,128]{3,2,1,0:T(8,128)(2,1)S(1)}, u32[]{:S(2)}, u32[]{:S(2)}) collective-permute-start(bf16[4,2,16,128]{3,2,1,0:T(8,128)(2,1)S(1)} %get-tuple-element.18), channel_id=1, source_target_pairs={{0,28},{4,0},{8,4},{12,8},{16,12},{20,16},{24,20},{28,24},{1,29},{... | collective-permute-start | bytes 98312 | tf_op jit(solution)/shard_map/ppermute | solution.py:28
  13.0 2.1 %collective-permute-done.refs_0_ = bf16[4,2,16,128]{3,2,1,0:T(8,128)(2,1)S(1)} collective-permute-done((bf16[4,2,16,128]{3,2,1,0:T(8,128)(2,1)S(1)}, bf16[4,2,16,128]{3,2,1,0:T(8,128)(2,1)S(1)}, u32[]{:S(2)}, u32[]{:S(2)}) %collective-permute-start) | collective-permute-done | bytes 32800 | tf_op jit(solution)/shard_map/ppermute | solution.py:28
  15.0 0.0 collective-permute-done.1.refs_1_
  15.1 1.6 %collective-permute-start.3 = (bf16[8,2,16,128]{3,2,1,0:T(8,128)(2,1)S(1)}, bf16[8,2,16,128]{3,2,1,0:T(8,128)(2,1)S(1)}, u32[]{:S(2)}, u32[]{:S(2)}) collective-permute-start(bf16[8,2,16,128]{3,2,1,0:T(8,128)(2,1)S(1)} %shard_map.69.refs_0_.refs_4_), channel_id=1, source_target_pairs={{0,2},{1,3},{2,0},{3,1},{4,6},{5,7},{6,4},{7,5},{8,10},{9,11},{10,... | collective-permute-start | bytes 196616 | tf_op jit(solution)/shard_map/ppermute | solution.py:23
  16.6 0.0 collective-permute-done.5.refs_1_
  16.6 0.0 collective-permute-done.7.refs_3_
  16.6 1.0 %shard_map.74 = (f32[64,864]{1,0:T(8,128)S(1)}, bf16[64,864]{1,0:T(8,128)(2,1)S(1)}) custom-call(bf16[16,2,16,128]{3,2,1,0:T(8,128)(2,1)S(1)} %get-tuple-element.19.refs_0_, bf16[16,2,16,128]{3,2,1,0:T(8,128)(2,1)S(1)} %collective-permute-done.5.refs_1_, bf16[16,2,16,128]{3,2,1,0:T(8,128)(2,1)S(1)} %collective-permute-done.6.refs_2_, ...), custom_call_target="tpu_custom_call" | custom-call | tf_op jit(solution)/shard_map/pallas_call | solution.py:398
  17.6 1.3 %collective-permute-start.11 = (bf16[64,864]{1,0:T(8,128)(2,1)S(1)}, bf16[64,864]{1,0:T(8,128)(2,1)S(1)}, u32[]{:S(2)}, u32[]{:S(2)}) collective-permute-start(bf16[64,864]{1,0:T(8,128)(2,1)S(1)} %get-tuple-element.27), channel_id=1, source_target_pairs={{0,4},{4,0},{8,12},{12,8},{16,20},{20,16},{24,28},{28,24},{1,5},{5... | collective-permute-start | bytes 331784 | tf_op jit(solution)/shard_map/ppermute | solution.py:23
  18.9 0.0 collective-permute-start.2
  18.9 0.5 %collective-permute-done.3.refs_2_.refs_6_ = bf16[8,2,16,128]{3,2,1,0:T(8,128)(2,1)S(1)} collective-permute-done((bf16[8,2,16,128]{3,2,1,0:T(8,128)(2,1)S(1)}, bf16[8,2,16,128]{3,2,1,0:T(8,128)(2,1)S(1)}, u32[]{:S(2)}, u32[]{:S(2)}) %collective-permute-start.3) | collective-permute-done | bytes 65568 | tf_op jit(solution)/shard_map/ppermute | solution.py:23
  19.4 0.0 collective-permute-start.4
  19.4 0.7 %collective-permute-done.2.refs_1_.refs_5_ = bf16[8,2,16,128]{3,2,1,0:T(8,128)(2,1)S(1)} collective-permute-done((bf16[8,2,16,128]{3,2,1,0:T(8,128)(2,1)S(1)}, bf16[8,2,16,128]{3,2,1,0:T(8,128)(2,1)S(1)}, u32[]{:S(2)}, u32[]{:S(2)}) %collective-permute-start.2) | collective-permute-done | bytes 65568 | tf_op jit(solution)/shard_map/ppermute | solution.py:23
  20.2 0.5 %collective-permute-done.4.refs_3_.refs_7_ = bf16[8,2,16,128]{3,2,1,0:T(8,128)(2,1)S(1)} collective-permute-done((bf16[8,2,16,128]{3,2,1,0:T(8,128)(2,1)S(1)}, bf16[8,2,16,128]{3,2,1,0:T(8,128)(2,1)S(1)}, u32[]{:S(2)}, u32[]{:S(2)}) %collective-permute-start.4) | collective-permute-done | bytes 65568 | tf_op jit(solution)/shard_map/ppermute | solution.py:23
  20.6 0.6 %shard_map.75.refs_2_ = f32[2,64,288]{2,1,0:T(8,128)S(1)} custom-call(bf16[16,2,16,128]{3,2,1,0:T(8,128)(2,1)S(1)} %get-tuple-element.19.refs_0_, bf16[16,2,16,128]{3,2,1,0:T(8,128)(2,1)S(1)} %collective-permute-done.5.refs_1_, bf16[16,2,16,128]{3,2,1,0:T(8,128)(2,1)S(1)} %collective-permute-done.6.refs_2_, ...), custom_call_target="tpu_custom_call" | custom-call | tf_op jit(solution)/shard_map/pallas_call | solution.py:398
  21.3 1.2 %collective-permute-done.11.refs_1_ = bf16[64,864]{1,0:T(8,128)(2,1)S(1)} collective-permute-done((bf16[64,864]{1,0:T(8,128)(2,1)S(1)}, bf16[64,864]{1,0:T(8,128)(2,1)S(1)}, u32[]{:S(2)}, u32[]{:S(2)}) %collective-permute-start.11) | collective-permute-done | bytes 110624 | tf_op jit(solution)/shard_map/ppermute | solution.py:23
  22.5 0.1 shard_map.76
  22.6 0.8 %collective-permute-start.12 = (bf16[32,864]{1,0:T(8,128)(2,1)S(1)}, bf16[32,864]{1,0:T(8,128)(2,1)S(1)}, u32[]{:S(2)}, u32[]{:S(2)}) collective-permute-start(bf16[32,864]{1,0:T(8,128)(2,1)S(1)} %get-tuple-element.29), channel_id=1, source_target_pairs={{0,8},{4,12},{8,0},{12,4},{16,24},{20,28},{24,16},{28,20},{1,9},{5... | collective-permute-start | bytes 165896 | tf_op jit(solution)/shard_map/ppermute | solution.py:23
  23.4 1.2 %shard_map.70 = (bf16[3,3,3,128,128]{4,3,2,1,0:T(8,128)(2,1)S(1)}, bf16[2,2,2,128,128]{4,3,2,1,0:T(8,128)(2,1)S(1)}) custom-call(bf16[3,3,3,128,128]{4,3,2,1,0:T(8,128)(2,1)} %refs_0_.1, bf16[2,2,2,512,128]{4,3,2,1,0:T(8,128)(2,1)} %refs_1_.1), custom_call_target="tpu_custom_call" | custom-call | tf_op jit(solution)/shard_map/pallas_call | solution.py:410
  24.7 1.6 %shard_map.71.refs_4_ = f32[2,10,8,8,128]{4,3,2,1,0:T(8,128)S(1)} custom-call(bf16[16,2,16,128]{3,2,1,0:T(8,128)(2,1)S(1)} %get-tuple-element.19.refs_0_, bf16[16,2,16,128]{3,2,1,0:T(8,128)(2,1)S(1)} %collective-permute-done.5.refs_1_, bf16[16,2,16,128]{3,2,1,0:T(8,128)(2,1)S(1)} %collective-permute-done.6.refs_2_, ...), custom_call_target="tpu_custom_call" | custom-call | tf_op jit(solution)/shard_map/pallas_call | solution.py:398
  26.2 3.0 %shard_map.72 = (f32[1,4,8,512]{3,2,1,0:T(8,128)S(1)}, bf16[1,4,8,512]{3,2,1,0:T(8,128)(2,1)S(1)}, bf16[1,4,8,512]{3,2,1,0:T(8,128)(2,1)S(1)}, bf16[1,4,8,512]{3,2,1,0:T(8,128)(2,1)S(1)}) custom-call(bf16[8,2,16,128]{3,2,1,0:T(8,128)(2,1)S(1)} %shard_map.69.refs_0_.refs_4_, bf16[8,2,16,128]{3,2,1,0:T(8,128)(2,1)S(1)} %collective-permute-done.2.refs_1_.refs_5_, ...), custom_call_target="tpu_custom_call" | custom-call | tf_op jit(solution)/shard_map/pallas_call | solution.py:398
  29.2 0.1 collective-permute-start.8
  29.3 0.6 %collective-permute-start.9 = (bf16[1,4,8,512]{3,2,1,0:T(8,128)(2,1)S(1)}, bf16[1,4,8,512]{3,2,1,0:T(8,128)(2,1)S(1)}, u32[]{:S(2)}, u32[]{:S(2)}) collective-permute-start(bf16[1,4,8,512]{3,2,1,0:T(8,128)(2,1)S(1)} %get-tuple-element.24), channel_id=1, source_target_pairs={{0,2},{1,3},{2,0},{3,1},{4,6},{5,7},{6,4},{7,5},{8,10},{9,11},{10,... | collective-permute-start | bytes 98312 | tf_op jit(solution)/shard_map/ppermute | solution.py:23
  29.9 1.2 %collective-permute-start.10 = (bf16[1,4,8,512]{3,2,1,0:T(8,128)(2,1)S(1)}, bf16[1,4,8,512]{3,2,1,0:T(8,128)(2,1)S(1)}, u32[]{:S(2)}, u32[]{:S(2)}) collective-permute-start(bf16[1,4,8,512]{3,2,1,0:T(8,128)(2,1)S(1)} %get-tuple-element.25), channel_id=1, source_target_pairs={{0,3},{1,2},{2,1},{3,0},{4,7},{5,6},{6,5},{7,4},{8,11},{9,10},{10,... | collective-permute-start | bytes 98312 | tf_op jit(solution)/shard_map/ppermute | solution.py:23
  31.2 0.0 collective-permute-done.12.refs_1_
  31.2 3.1 %collective-permute-start.13 = (bf16[16,864]{1,0:T(8,128)(2,1)S(1)}, bf16[16,864]{1,0:T(8,128)(2,1)S(1)}, u32[]{:S(2)}, u32[]{:S(2)}) collective-permute-start(bf16[16,864]{1,0:T(8,128)(2,1)S(1)} %get-tuple-element.31), channel_id=1, source_target_pairs={{0,16},{4,20},{8,24},{12,28},{16,0},{20,4},{24,8},{28,12},{1,17},{... | collective-permute-start | bytes 82952 | tf_op jit(solution)/shard_map/ppermute | solution.py:23
  34.3 0.0 collective-permute-done.8.refs_1_
  34.3 0.0 collective-permute-done.9.refs_2_
  34.3 0.0 collective-permute-done.10.refs_3_
  34.3 0.6 %shard_map.73 = bf16[1,4,8,512]{3,2,1,0:T(8,128)(2,1)} custom-call(f32[1,4,8,512]{3,2,1,0:T(8,128)S(1)} %get-tuple-element.22.refs_0_, bf16[1,4,8,512]{3,2,1,0:T(8,128)(2,1)S(1)} %collective-permute-done.8.refs_1_, bf16[1,4,8,512]{3,2,1,0:T(8,128)(2,1)S(1)} %collective-permute-done.9.refs_2_, bf16[1,4,8,512]{3,2,1,0:T(8,128)(2,1)S(1)} %collective-permute-done.10.refs_3_), custom_call_target="tpu_custom_call" | custom-call | tf_op jit(solution)/shard_map/pallas_call | solution.py:398
  35.0 1.8 %collective-permute-done.13.got_ref = bf16[16,864]{1,0:T(8,128)(2,1)S(1)} collective-permute-done((bf16[16,864]{1,0:T(8,128)(2,1)S(1)}, bf16[16,864]{1,0:T(8,128)(2,1)S(1)}, u32[]{:S(2)}, u32[]{:S(2)}) %collective-permute-start.13) | collective-permute-done | bytes 27680 | tf_op jit(solution)/shard_map/ppermute | solution.py:23
  36.7 0.8 %shard_map.78 = f32[3,3,3,16,32]{4,3,2,1,0:T(8,128)} custom-call(f32[16,864]{1,0:T(8,128)S(1)} %get-tuple-element.30.keep_ref, bf16[16,864]{1,0:T(8,128)(2,1)S(1)} %collective-permute-done.13.got_ref), custom_call_target="tpu_custom_call" | custom-call | tf_op jit(solution)/shard_map/pallas_call | solution.py:398
  (2 shorter events, 0.0 us)
Async XLA Ops:
  1.6 6.5 %collective-permute-start.6 = (bf16[16,2,16,128]{3,2,1,0:T(8,128)(2,1)S(1)}, bf16[16,2,16,128]{3,2,1,0:T(8,128)(2,1)S(1)}, u32[]{:S(2)}, u32[]{:S(2)}) collective-permute-start(bf16[16,2,16,128]{3,2,1,0:T(8,128)(2,1)S(1)} %get-tuple-element.19.refs_0_), channel_id=1, source_target_pairs={{0,2},{1,3},{2,0},{3,1},{4,6},{5,7},{6,4},{7,5},{8,10},{9,11},{10,... | collective-permute-start | bytes 393224 | tf_op jit(solution)/shard_map/ppermute | solution.py:23
  4.7 12.0 %collective-permute-start.5 = (bf16[16,2,16,128]{3,2,1,0:T(8,128)(2,1)S(1)}, bf16[16,2,16,128]{3,2,1,0:T(8,128)(2,1)S(1)}, u32[]{:S(2)}, u32[]{:S(2)}) collective-permute-start(bf16[16,2,16,128]{3,2,1,0:T(8,128)(2,1)S(1)} %get-tuple-element.19.refs_0_), channel_id=1, source_target_pairs={{0,1},{1,0},{2,3},{3,2},{4,5},{5,4},{6,7},{7,6},{8,9},{9,8},{10,11... | collective-permute-start | bytes 393224 | tf_op jit(solution)/shard_map/ppermute | solution.py:23
  8.2 8.5 %collective-permute-start.7 = (bf16[16,2,16,128]{3,2,1,0:T(8,128)(2,1)S(1)}, bf16[16,2,16,128]{3,2,1,0:T(8,128)(2,1)S(1)}, u32[]{:S(2)}, u32[]{:S(2)}) collective-permute-start(bf16[16,2,16,128]{3,2,1,0:T(8,128)(2,1)S(1)} %collective-permute-done.6.refs_2_), channel_id=1, source_target_pairs={{0,1},{1,0},{2,3},{3,2},{4,5},{5,4},{6,7},{7,6},{8,9},{9,8},{10,11... | collective-permute-start | bytes 393224 | tf_op jit(solution)/shard_map/ppermute | solution.py:23
  8.2 6.9 %collective-permute-start = (bf16[4,2,16,128]{3,2,1,0:T(8,128)(2,1)S(1)}, bf16[4,2,16,128]{3,2,1,0:T(8,128)(2,1)S(1)}, u32[]{:S(2)}, u32[]{:S(2)}) collective-permute-start(bf16[4,2,16,128]{3,2,1,0:T(8,128)(2,1)S(1)} %get-tuple-element.17), channel_id=1, source_target_pairs={{0,4},{4,8},{8,12},{12,16},{16,20},{20,24},{24,28},{28,0},{1,5},{5... | collective-permute-start | bytes 98312 | tf_op jit(solution)/shard_map/ppermute | solution.py:28
  9.9 5.1 %collective-permute-start.1 = (bf16[4,2,16,128]{3,2,1,0:T(8,128)(2,1)S(1)}, bf16[4,2,16,128]{3,2,1,0:T(8,128)(2,1)S(1)}, u32[]{:S(2)}, u32[]{:S(2)}) collective-permute-start(bf16[4,2,16,128]{3,2,1,0:T(8,128)(2,1)S(1)} %get-tuple-element.18), channel_id=1, source_target_pairs={{0,28},{4,0},{8,4},{12,8},{16,12},{20,16},{24,20},{28,24},{1,29},{... | collective-permute-start | bytes 98312 | tf_op jit(solution)/shard_map/ppermute | solution.py:28
  15.1 4.3 %collective-permute-start.3 = (bf16[8,2,16,128]{3,2,1,0:T(8,128)(2,1)S(1)}, bf16[8,2,16,128]{3,2,1,0:T(8,128)(2,1)S(1)}, u32[]{:S(2)}, u32[]{:S(2)}) collective-permute-start(bf16[8,2,16,128]{3,2,1,0:T(8,128)(2,1)S(1)} %shard_map.69.refs_0_.refs_4_), channel_id=1, source_target_pairs={{0,2},{1,3},{2,0},{3,1},{4,6},{5,7},{6,4},{7,5},{8,10},{9,11},{10,... | collective-permute-start | bytes 196616 | tf_op jit(solution)/shard_map/ppermute | solution.py:23
  17.6 4.9 %collective-permute-start.11 = (bf16[64,864]{1,0:T(8,128)(2,1)S(1)}, bf16[64,864]{1,0:T(8,128)(2,1)S(1)}, u32[]{:S(2)}, u32[]{:S(2)}) collective-permute-start(bf16[64,864]{1,0:T(8,128)(2,1)S(1)} %get-tuple-element.27), channel_id=1, source_target_pairs={{0,4},{4,0},{8,12},{12,8},{16,20},{20,16},{24,28},{28,24},{1,5},{5... | collective-permute-start | bytes 331784 | tf_op jit(solution)/shard_map/ppermute | solution.py:23
  18.9 1.3 %collective-permute-start.2 = (bf16[8,2,16,128]{3,2,1,0:T(8,128)(2,1)S(1)}, bf16[8,2,16,128]{3,2,1,0:T(8,128)(2,1)S(1)}, u32[]{:S(2)}, u32[]{:S(2)}) collective-permute-start(bf16[8,2,16,128]{3,2,1,0:T(8,128)(2,1)S(1)} %shard_map.69.refs_0_.refs_4_), channel_id=1, source_target_pairs={{0,1},{1,0},{2,3},{3,2},{4,5},{5,4},{6,7},{7,6},{8,9},{9,8},{10,11... | collective-permute-start | bytes 196616 | tf_op jit(solution)/shard_map/ppermute | solution.py:23
  19.4 1.3 %collective-permute-start.4 = (bf16[8,2,16,128]{3,2,1,0:T(8,128)(2,1)S(1)}, bf16[8,2,16,128]{3,2,1,0:T(8,128)(2,1)S(1)}, u32[]{:S(2)}, u32[]{:S(2)}) collective-permute-start(bf16[8,2,16,128]{3,2,1,0:T(8,128)(2,1)S(1)} %collective-permute-done.3.refs_2_.refs_6_), channel_id=1, source_target_pairs={{0,1},{1,0},{2,3},{3,2},{4,5},{5,4},{6,7},{7,6},{8,9},{9,8},{10,11... | collective-permute-start | bytes 196616 | tf_op jit(solution)/shard_map/ppermute | solution.py:23
  22.6 8.6 %collective-permute-start.12 = (bf16[32,864]{1,0:T(8,128)(2,1)S(1)}, bf16[32,864]{1,0:T(8,128)(2,1)S(1)}, u32[]{:S(2)}, u32[]{:S(2)}) collective-permute-start(bf16[32,864]{1,0:T(8,128)(2,1)S(1)} %get-tuple-element.29), channel_id=1, source_target_pairs={{0,8},{4,12},{8,0},{12,4},{16,24},{20,28},{24,16},{28,20},{1,9},{5... | collective-permute-start | bytes 165896 | tf_op jit(solution)/shard_map/ppermute | solution.py:23
  29.2 5.1 %collective-permute-start.8 = (bf16[1,4,8,512]{3,2,1,0:T(8,128)(2,1)S(1)}, bf16[1,4,8,512]{3,2,1,0:T(8,128)(2,1)S(1)}, u32[]{:S(2)}, u32[]{:S(2)}) collective-permute-start(bf16[1,4,8,512]{3,2,1,0:T(8,128)(2,1)S(1)} %get-tuple-element.23), channel_id=1, source_target_pairs={{0,1},{1,0},{2,3},{3,2},{4,5},{5,4},{6,7},{7,6},{8,9},{9,8},{10,11... | collective-permute-start | bytes 98312 | tf_op jit(solution)/shard_map/ppermute | solution.py:23
  29.3 5.0 %collective-permute-start.9 = (bf16[1,4,8,512]{3,2,1,0:T(8,128)(2,1)S(1)}, bf16[1,4,8,512]{3,2,1,0:T(8,128)(2,1)S(1)}, u32[]{:S(2)}, u32[]{:S(2)}) collective-permute-start(bf16[1,4,8,512]{3,2,1,0:T(8,128)(2,1)S(1)} %get-tuple-element.24), channel_id=1, source_target_pairs={{0,2},{1,3},{2,0},{3,1},{4,6},{5,7},{6,4},{7,5},{8,10},{9,11},{10,... | collective-permute-start | bytes 98312 | tf_op jit(solution)/shard_map/ppermute | solution.py:23
  29.9 4.4 %collective-permute-start.10 = (bf16[1,4,8,512]{3,2,1,0:T(8,128)(2,1)S(1)}, bf16[1,4,8,512]{3,2,1,0:T(8,128)(2,1)S(1)}, u32[]{:S(2)}, u32[]{:S(2)}) collective-permute-start(bf16[1,4,8,512]{3,2,1,0:T(8,128)(2,1)S(1)} %get-tuple-element.25), channel_id=1, source_target_pairs={{0,3},{1,2},{2,1},{3,0},{4,7},{5,6},{6,5},{7,4},{8,11},{9,10},{10,... | collective-permute-start | bytes 98312 | tf_op jit(solution)/shard_map/ppermute | solution.py:23
  31.2 5.5 %collective-permute-start.13 = (bf16[16,864]{1,0:T(8,128)(2,1)S(1)}, bf16[16,864]{1,0:T(8,128)(2,1)S(1)}, u32[]{:S(2)}, u32[]{:S(2)}) collective-permute-start(bf16[16,864]{1,0:T(8,128)(2,1)S(1)} %get-tuple-element.31), channel_id=1, source_target_pairs={{0,16},{4,20},{8,24},{12,28},{16,0},{20,4},{24,8},{28,12},{1,17},{... | collective-permute-start | bytes 82952 | tf_op jit(solution)/shard_map/ppermute | solution.py:23

commit v4 on v3

--- a/solution.py
+++ b/solution.py
@@ -111,10 +111,7 @@
 
 def main_kernel(n, m, *refs):
     rims, (inner_ref, full_ref, up_ref, half_ref) = refs[:n], refs[n : n + 4]
-    outs, (stage, spread, padded, result, held, arrived) = (
-        refs[n + 4 : 2 * n + 4],
-        refs[2 * n + 4 :],
-    )
+    outs, (stage, spread, padded, result, held, arrived) = refs[n + 4 : n + 6], refs[n + 6 :]
     loads = [
         pltpu.make_async_copy(half_ref.at[p], held.at[p], arrived.at[p]) for p in range(3)
     ]
@@ -191,7 +188,8 @@
             total = product if total is None else total + product
     result[...] = total.reshape(result.shape)
     for k in range(n):
-        outs[k][...] = result[pair(k)].astype(outs[k].dtype)
+        out = outs[k // (n // 2)]
+        out[k % (n // 2)] = result[pair(k)].astype(out.dtype)
 
 
 def chosen_lanes(cells, pick, part, nz):
@@ -385,12 +383,14 @@
                 out_ref[p, q, r] = total[:, at : at + part]
 
 
-def sum_kernel(*refs):
-    inputs, out_ref = refs[:-1], refs[-1]
-    total = inputs[0][...]
-    for ref in inputs[1:]:
-        total = total + ref[...].astype(F32)
-    out_ref[...] = total.astype(BF16)
+def halve_kernel(keep_ref, got_ref, held_ref, send_ref):
+    half = held_ref.shape[0]
+    held_ref[...] = keep_ref[:half] + got_ref[:half].astype(F32)
+    send_ref[...] = (keep_ref[half:] + got_ref[half:].astype(F32)).astype(BF16)
+
+
+def sum_kernel(keep_ref, got_ref, out_ref):
+    out_ref[...] = (keep_ref[0] + got_ref[0].astype(F32)).astype(BF16)
 
 
 def call(kernel, outs, scratch, inputs, placed=True, far=0):
@@ -477,9 +477,9 @@
         (*bricks, full),
     )
     chunk = (half_y // n, half_x, half_z, filters_half.shape[3])
-    chunks = call(
+    own_sum, other = call(
         lambda *refs: main_kernel(n, m, *refs),
-        [shape(chunk, F32)] + [shape(chunk, BF16)] * (n - 1),
+        [shape((n // 2,) + chunk, F32), shape((n // 2,) + chunk, BF16)],
         [
             pltpu.VMEM((2 * HALO * ny, nz, ch), F32),
             pltpu.VMEM((4, HALO, n * ny + 2, nz, ch), BF16),
@@ -491,10 +491,17 @@
         (*rims, inner, full, up, filters_half),
         far=1,
     )
-    parts = [chunks[0]]
-    for k in range(1, n):
-        parts.append(swap(chunks[k], "chan", k))
-    (grad_half,) = call(sum_kernel, [shape(chunk, BF16)], [], parts, False)
+    got_sum = swap(other, "chan", n // 2)
+    for bit in range(1, n.bit_length() - 1):
+        count = own_sum.shape[0] // 2
+        own_sum, other = call(
+            halve_kernel,
+            [shape((count,) + chunk, F32), shape((count,) + chunk, BF16)],
+            [],
+            (own_sum, got_sum),
+        )
+        got_sum = swap(other, "chan", n // 2 ** (bit + 1))
+    (grad_half,) = call(sum_kernel, [shape(chunk, BF16)], [], (own_sum, got_sum), False)
     for bit in range(1, m.bit_length() - 1):
         rows = keep.shape[0] // 2
         keep, send = call(

time: 37.7 us -> 38 us (level)
  waiting for transfers between devices: 10.3 us -> 12.2 us
  starting transfers between devices: 16.6 us -> 14.8 us
    ppermute x12 -> x11, waiting for transfers between devices: 8.2 us -> 10.2 us  [swap(): return lax.ppermute(value, axis, [(i, i ^ k) for i in range(n)])]
    ppermute x12 -> x11, starting transfers between devices: 11.8 us -> 9.97 us  [swap(): return lax.ppermute(value, axis, [(i, i ^ k) for i in range(n)])]
    pallas_call x10 -> x11, Pallas kernels: 8.76 us -> 8.81 us  [call(): pl.pallas_call(kernel, out_shape=[pltpu.VMEM(v.shape, v.dtype) if placed...]
  transfers between devices with their start and end apart: 14 -> 13, of which waited for: 7 -> 6; matrix products, arithmetic and copies ran while one was open for 0% -> 0% of each run, Pallas kernels for 22% -> 22%
where the time goes in v4:
time: 38 us; the launch traced here: 37.8 us
  starting transfers between devices  14.8 us (39%)
  waiting for transfers between devices  12.2 us (32%)
  Pallas kernels  10 us (26%)
  between operations  0.73 us (2%)
    ppermute x11, waiting for transfers between devices, swap(): return lax.ppermute(value, axis, [(i, i ^ k) for i in range(n)])  10.2 us
    ppermute x11, starting transfers between devices, swap(): return lax.ppermute(value, axis, [(i, i ^ k) for i in range(n)])  9.97 us
    pallas_call x11, Pallas kernels, call(): pl.pallas_call(kernel, out_shape=[pltpu.VMEM(v.shape, v.dtype) if placed...  8.81 us
    ppermute x2, starting transfers between devices, shift(): return lax.ppermute(value, axis, [(i, (i + step) % n) for i in range(n)])  4.81 us
    ppermute x2, waiting for transfers between devices, shift(): return lax.ppermute(value, axis, [(i, (i + step) % n) for i in range(n)])  2.06 us
    pallas_call x1, Pallas kernels, fetch(): pl.pallas_call(fetch_kernel, out_shape=[pltpu.VMEM(shape, BF16) for shape...  1.23 us
  transfers between devices with their start and end apart: 13, of which 6 were waited for; matrix products, arithmetic and copies ran while one was open for 0% of the time, Pallas kernels for 22%

profile of v4, /device:TPU:0, one launch (start us, length us, event | category | flops | bytes accessed | tf_op | source)
XLA Modules:
  0.0 37.8 jit_solution(7436993203925744962)
XLA Ops:
  0.6 1.0 %shard_map.68 = (bf16[16,2,16,128]{3,2,1,0:T(8,128)(2,1)S(1)}, bf16[4,2,16,128]{3,2,1,0:T(8,128)(2,1)S(1)}, bf16[4,2,16,128]{3,2,1,0:T(8,128)(2,1)S(1)}) custom-call(bf16[8,2,16,128]{3,2,1,0:T(8,128)(2,1)} %grad_ref.1, bf16[8,2,16,128]{3,2,1,0:T(8,128)(2,1)} %feat_ref.1), custom_call_target="tpu_custom_call" | custom-call | tf_op jit(solution)/shard_map/pallas_call | solution.py:398
  1.6 3.0 %collective-permute-start.6 = (bf16[16,2,16,128]{3,2,1,0:T(8,128)(2,1)S(1)}, bf16[16,2,16,128]{3,2,1,0:T(8,128)(2,1)S(1)}, u32[]{:S(2)}, u32[]{:S(2)}) collective-permute-start(bf16[16,2,16,128]{3,2,1,0:T(8,128)(2,1)S(1)} %get-tuple-element.19.refs_0_), channel_id=1, source_target_pairs={{0,2},{1,3},{2,0},{3,1},{4,6},{5,7},{6,4},{7,5},{8,10},{9,11},{10,... | collective-permute-start | bytes 393224 | tf_op jit(solution)/shard_map/ppermute | solution.py:23
  4.7 0.0 collective-permute-start.5
  4.7 3.5 %collective-permute-done.6.refs_2_ = bf16[16,2,16,128]{3,2,1,0:T(8,128)(2,1)S(1)} collective-permute-done((bf16[16,2,16,128]{3,2,1,0:T(8,128)(2,1)S(1)}, bf16[16,2,16,128]{3,2,1,0:T(8,128)(2,1)S(1)}, u32[]{:S(2)}, u32[]{:S(2)}) %collective-permute-start.6) | collective-permute-done | bytes 131104 | tf_op jit(solution)/shard_map/ppermute | solution.py:23
  8.2 0.0 collective-permute-start.7
  8.2 1.8 %collective-permute-start = (bf16[4,2,16,128]{3,2,1,0:T(8,128)(2,1)S(1)}, bf16[4,2,16,128]{3,2,1,0:T(8,128)(2,1)S(1)}, u32[]{:S(2)}, u32[]{:S(2)}) collective-permute-start(bf16[4,2,16,128]{3,2,1,0:T(8,128)(2,1)S(1)} %get-tuple-element.17), channel_id=1, source_target_pairs={{0,4},{4,8},{8,12},{12,16},{16,20},{20,24},{24,28},{28,0},{1,5},{5... | collective-permute-start | bytes 98312 | tf_op jit(solution)/shard_map/ppermute | solution.py:28
  9.9 3.0 %collective-permute-start.1 = (bf16[4,2,16,128]{3,2,1,0:T(8,128)(2,1)S(1)}, bf16[4,2,16,128]{3,2,1,0:T(8,128)(2,1)S(1)}, u32[]{:S(2)}, u32[]{:S(2)}) collective-permute-start(bf16[4,2,16,128]{3,2,1,0:T(8,128)(2,1)S(1)} %get-tuple-element.18), channel_id=1, source_target_pairs={{0,28},{4,0},{8,4},{12,8},{16,12},{20,16},{24,20},{28,24},{1,29},{... | collective-permute-start | bytes 98312 | tf_op jit(solution)/shard_map/ppermute | solution.py:28
  13.0 2.1 %collective-permute-done.refs_0_ = bf16[4,2,16,128]{3,2,1,0:T(8,128)(2,1)S(1)} collective-permute-done((bf16[4,2,16,128]{3,2,1,0:T(8,128)(2,1)S(1)}, bf16[4,2,16,128]{3,2,1,0:T(8,128)(2,1)S(1)}, u32[]{:S(2)}, u32[]{:S(2)}) %collective-permute-start) | collective-permute-done | bytes 32800 | tf_op jit(solution)/shard_map/ppermute | solution.py:28
  15.0 0.0 collective-permute-done.1.refs_1_
  15.1 1.6 %collective-permute-start.3 = (bf16[8,2,16,128]{3,2,1,0:T(8,128)(2,1)S(1)}, bf16[8,2,16,128]{3,2,1,0:T(8,128)(2,1)S(1)}, u32[]{:S(2)}, u32[]{:S(2)}) collective-permute-start(bf16[8,2,16,128]{3,2,1,0:T(8,128)(2,1)S(1)} %shard_map.69.refs_0_.refs_4_), channel_id=1, source_target_pairs={{0,2},{1,3},{2,0},{3,1},{4,6},{5,7},{6,4},{7,5},{8,10},{9,11},{10,... | collective-permute-start | bytes 196616 | tf_op jit(solution)/shard_map/ppermute | solution.py:23
  16.6 0.0 collective-permute-done.5.refs_1_
  16.6 0.0 collective-permute-done.7.refs_3_
  16.6 1.0 %shard_map.75 = (f32[64,864]{1,0:T(8,128)S(1)}, bf16[64,864]{1,0:T(8,128)(2,1)S(1)}) custom-call(bf16[16,2,16,128]{3,2,1,0:T(8,128)(2,1)S(1)} %get-tuple-element.19.refs_0_, bf16[16,2,16,128]{3,2,1,0:T(8,128)(2,1)S(1)} %collective-permute-done.5.refs_1_, bf16[16,2,16,128]{3,2,1,0:T(8,128)(2,1)S(1)} %collective-permute-done.6.refs_2_, ...), custom_call_target="tpu_custom_call" | custom-call | tf_op jit(solution)/shard_map/pallas_call | solution.py:398
  17.6 1.3 %collective-permute-start.10 = (bf16[64,864]{1,0:T(8,128)(2,1)S(1)}, bf16[64,864]{1,0:T(8,128)(2,1)S(1)}, u32[]{:S(2)}, u32[]{:S(2)}) collective-permute-start(bf16[64,864]{1,0:T(8,128)(2,1)S(1)} %get-tuple-element.27), channel_id=1, source_target_pairs={{0,4},{4,0},{8,12},{12,8},{16,20},{20,16},{24,28},{28,24},{1,5},{5... | collective-permute-start | bytes 331784 | tf_op jit(solution)/shard_map/ppermute | solution.py:23
  18.9 0.0 collective-permute-start.2
  18.9 0.5 %collective-permute-done.3.refs_2_.refs_6_ = bf16[8,2,16,128]{3,2,1,0:T(8,128)(2,1)S(1)} collective-permute-done((bf16[8,2,16,128]{3,2,1,0:T(8,128)(2,1)S(1)}, bf16[8,2,16,128]{3,2,1,0:T(8,128)(2,1)S(1)}, u32[]{:S(2)}, u32[]{:S(2)}) %collective-permute-start.3) | collective-permute-done | bytes 65568 | tf_op jit(solution)/shard_map/ppermute | solution.py:23
  19.4 0.0 collective-permute-start.4
  19.4 1.2 %shard_map.70 = (bf16[3,3,3,128,128]{4,3,2,1,0:T(8,128)(2,1)S(1)}, bf16[2,2,2,128,128]{4,3,2,1,0:T(8,128)(2,1)S(1)}) custom-call(bf16[3,3,3,128,128]{4,3,2,1,0:T(8,128)(2,1)} %refs_0_.1, bf16[2,2,2,512,128]{4,3,2,1,0:T(8,128)(2,1)} %refs_1_.1), custom_call_target="tpu_custom_call" | custom-call | tf_op jit(solution)/shard_map/pallas_call | solution.py:410
  20.7 1.6 %shard_map.71.refs_4_ = f32[2,10,8,8,128]{4,3,2,1,0:T(8,128)S(1)} custom-call(bf16[16,2,16,128]{3,2,1,0:T(8,128)(2,1)S(1)} %get-tuple-element.19.refs_0_, bf16[16,2,16,128]{3,2,1,0:T(8,128)(2,1)S(1)} %collective-permute-done.5.refs_1_, bf16[16,2,16,128]{3,2,1,0:T(8,128)(2,1)S(1)} %collective-permute-done.6.refs_2_, ...), custom_call_target="tpu_custom_call" | custom-call | tf_op jit(solution)/shard_map/pallas_call | solution.py:398
  22.2 0.0 collective-permute-done.2.refs_1_.refs_5_
  22.2 0.0 collective-permute-done.4.refs_3_.refs_7_
  22.3 3.0 %shard_map.72 = (f32[2,1,4,8,512]{4,3,2,1,0:T(8,128)S(1)}, bf16[2,1,4,8,512]{4,3,2,1,0:T(8,128)(2,1)S(1)}) custom-call(bf16[8,2,16,128]{3,2,1,0:T(8,128)(2,1)S(1)} %shard_map.69.refs_0_.refs_4_, bf16[8,2,16,128]{3,2,1,0:T(8,128)(2,1)S(1)} %collective-permute-done.2.refs_1_.refs_5_, bf16[8,2,16,128]{3,2,1,0:T(8,128)(2,1)S(1)} %collective-permute-done.3.refs_2_.refs_6_, ...), custom_call_target="tpu_custom_call" | custom-call | tf_op jit(solution)/shard_map/pallas_call | solution.py:398
  25.3 1.5 %collective-permute-start.8 = (bf16[2,1,4,8,512]{4,3,2,1,0:T(8,128)(2,1)S(1)}, bf16[2,1,4,8,512]{4,3,2,1,0:T(8,128)(2,1)S(1)}, u32[]{:S(2)}, u32[]{:S(2)}) collective-permute-start(bf16[2,1,4,8,512]{4,3,2,1,0:T(8,128)(2,1)S(1)} %get-tuple-element.23), channel_id=1, source_target_pairs={{0,2},{1,3},{2,0},{3,1},{4,6},{5,7},{6,4},{7,5},{8,10},{9,11},{10,... | collective-permute-start | bytes 196616 | tf_op jit(solution)/shard_map/ppermute | solution.py:23
  26.8 0.6 %shard_map.76.refs_2_ = f32[2,64,288]{2,1,0:T(8,128)S(1)} custom-call(bf16[16,2,16,128]{3,2,1,0:T(8,128)(2,1)S(1)} %get-tuple-element.19.refs_0_, bf16[16,2,16,128]{3,2,1,0:T(8,128)(2,1)S(1)} %collective-permute-done.5.refs_1_, bf16[16,2,16,128]{3,2,1,0:T(8,128)(2,1)S(1)} %collective-permute-done.6.refs_2_, ...), custom_call_target="tpu_custom_call" | custom-call | tf_op jit(solution)/shard_map/pallas_call | solution.py:398
  27.5 0.0 collective-permute-done.10.refs_1_
  27.5 0.1 shard_map.77
  27.6 0.7 %collective-permute-start.11 = (bf16[32,864]{1,0:T(8,128)(2,1)S(1)}, bf16[32,864]{1,0:T(8,128)(2,1)S(1)}, u32[]{:S(2)}, u32[]{:S(2)}) collective-permute-start(bf16[32,864]{1,0:T(8,128)(2,1)S(1)} %get-tuple-element.29), channel_id=1, source_target_pairs={{0,8},{4,12},{8,0},{12,4},{16,24},{20,28},{24,16},{28,20},{1,9},{5... | collective-permute-start | bytes 165896 | tf_op jit(solution)/shard_map/ppermute | solution.py:23
  28.3 1.6 %collective-permute-done.8.got_ref = bf16[2,1,4,8,512]{4,3,2,1,0:T(8,128)(2,1)S(1)} collective-permute-done((bf16[2,1,4,8,512]{4,3,2,1,0:T(8,128)(2,1)S(1)}, bf16[2,1,4,8,512]{4,3,2,1,0:T(8,128)(2,1)S(1)}, u32[]{:S(2)}, u32[]{:S(2)}) %collective-permute-start.8) | collective-permute-done | bytes 65568 | tf_op jit(solution)/shard_map/ppermute | solution.py:23
  29.9 0.1 collective-permute-start.9
  29.9 1.9 %collective-permute-done.11.refs_1_ = bf16[32,864]{1,0:T(8,128)(2,1)S(1)} collective-permute-done((bf16[32,864]{1,0:T(8,128)(2,1)S(1)}, bf16[32,864]{1,0:T(8,128)(2,1)S(1)}, u32[]{:S(2)}, u32[]{:S(2)}) %collective-permute-start.11) | collective-permute-done | bytes 55328 | tf_op jit(solution)/shard_map/ppermute | solution.py:23
  31.9 1.7 %collective-permute-start.12 = (bf16[16,864]{1,0:T(8,128)(2,1)S(1)}, bf16[16,864]{1,0:T(8,128)(2,1)S(1)}, u32[]{:S(2)}, u32[]{:S(2)}) collective-permute-start(bf16[16,864]{1,0:T(8,128)(2,1)S(1)} %get-tuple-element.31), channel_id=1, source_target_pairs={{0,16},{4,20},{8,24},{12,28},{16,0},{20,4},{24,8},{28,12},{1,17},{... | collective-permute-start | bytes 82952 | tf_op jit(solution)/shard_map/ppermute | solution.py:23
  33.6 0.0 collective-permute-done.9.got_ref
  33.6 0.6 %shard_map.74 = bf16[1,4,8,512]{3,2,1,0:T(8,128)(2,1)} custom-call(f32[1,1,4,8,512]{4,3,2,1,0:T(8,128)S(1)} %get-tuple-element.24.keep_ref, bf16[1,1,4,8,512]{4,3,2,1,0:T(8,128)(2,1)S(1)} %collective-permute-done.9.got_ref), custom_call_target="tpu_custom_call" | custom-call | tf_op jit(solution)/shard_map/pallas_call | solution.py:398
  34.2 2.8 %collective-permute-done.12.got_ref = bf16[16,864]{1,0:T(8,128)(2,1)S(1)} collective-permute-done((bf16[16,864]{1,0:T(8,128)(2,1)S(1)}, bf16[16,864]{1,0:T(8,128)(2,1)S(1)}, u32[]{:S(2)}, u32[]{:S(2)}) %collective-permute-start.12) | collective-permute-done | bytes 27680 | tf_op jit(solution)/shard_map/ppermute | solution.py:23
  37.0 0.8 %shard_map.79 = f32[3,3,3,16,32]{4,3,2,1,0:T(8,128)} custom-call(f32[16,864]{1,0:T(8,128)S(1)} %get-tuple-element.30.keep_ref, bf16[16,864]{1,0:T(8,128)(2,1)S(1)} %collective-permute-done.12.got_ref), custom_call_target="tpu_custom_call" | custom-call | tf_op jit(solution)/shard_map/pallas_call | solution.py:398
  (3 shorter events, 0.1 us)
Async XLA Ops:
  1.6 6.5 %collective-permute-start.6 = (bf16[16,2,16,128]{3,2,1,0:T(8,128)(2,1)S(1)}, bf16[16,2,16,128]{3,2,1,0:T(8,128)(2,1)S(1)}, u32[]{:S(2)}, u32[]{:S(2)}) collective-permute-start(bf16[16,2,16,128]{3,2,1,0:T(8,128)(2,1)S(1)} %get-tuple-element.19.refs_0_), channel_id=1, source_target_pairs={{0,2},{1,3},{2,0},{3,1},{4,6},{5,7},{6,4},{7,5},{8,10},{9,11},{10,... | collective-permute-start | bytes 393224 | tf_op jit(solution)/shard_map/ppermute | solution.py:23
  4.7 12.0 %collective-permute-start.5 = (bf16[16,2,16,128]{3,2,1,0:T(8,128)(2,1)S(1)}, bf16[16,2,16,128]{3,2,1,0:T(8,128)(2,1)S(1)}, u32[]{:S(2)}, u32[]{:S(2)}) collective-permute-start(bf16[16,2,16,128]{3,2,1,0:T(8,128)(2,1)S(1)} %get-tuple-element.19.refs_0_), channel_id=1, source_target_pairs={{0,1},{1,0},{2,3},{3,2},{4,5},{5,4},{6,7},{7,6},{8,9},{9,8},{10,11... | collective-permute-start | bytes 393224 | tf_op jit(solution)/shard_map/ppermute | solution.py:23
  8.2 8.5 %collective-permute-start.7 = (bf16[16,2,16,128]{3,2,1,0:T(8,128)(2,1)S(1)}, bf16[16,2,16,128]{3,2,1,0:T(8,128)(2,1)S(1)}, u32[]{:S(2)}, u32[]{:S(2)}) collective-permute-start(bf16[16,2,16,128]{3,2,1,0:T(8,128)(2,1)S(1)} %collective-permute-done.6.refs_2_), channel_id=1, source_target_pairs={{0,1},{1,0},{2,3},{3,2},{4,5},{5,4},{6,7},{7,6},{8,9},{9,8},{10,11... | collective-permute-start | bytes 393224 | tf_op jit(solution)/shard_map/ppermute | solution.py:23
  8.2 6.9 %collective-permute-start = (bf16[4,2,16,128]{3,2,1,0:T(8,128)(2,1)S(1)}, bf16[4,2,16,128]{3,2,1,0:T(8,128)(2,1)S(1)}, u32[]{:S(2)}, u32[]{:S(2)}) collective-permute-start(bf16[4,2,16,128]{3,2,1,0:T(8,128)(2,1)S(1)} %get-tuple-element.17), channel_id=1, source_target_pairs={{0,4},{4,8},{8,12},{12,16},{16,20},{20,24},{24,28},{28,0},{1,5},{5... | collective-permute-start | bytes 98312 | tf_op jit(solution)/shard_map/ppermute | solution.py:28
  9.9 5.1 %collective-permute-start.1 = (bf16[4,2,16,128]{3,2,1,0:T(8,128)(2,1)S(1)}, bf16[4,2,16,128]{3,2,1,0:T(8,128)(2,1)S(1)}, u32[]{:S(2)}, u32[]{:S(2)}) collective-permute-start(bf16[4,2,16,128]{3,2,1,0:T(8,128)(2,1)S(1)} %get-tuple-element.18), channel_id=1, source_target_pairs={{0,28},{4,0},{8,4},{12,8},{16,12},{20,16},{24,20},{28,24},{1,29},{... | collective-permute-start | bytes 98312 | tf_op jit(solution)/shard_map/ppermute | solution.py:28
  15.1 4.3 %collective-permute-start.3 = (bf16[8,2,16,128]{3,2,1,0:T(8,128)(2,1)S(1)}, bf16[8,2,16,128]{3,2,1,0:T(8,128)(2,1)S(1)}, u32[]{:S(2)}, u32[]{:S(2)}) collective-permute-start(bf16[8,2,16,128]{3,2,1,0:T(8,128)(2,1)S(1)} %shard_map.69.refs_0_.refs_4_), channel_id=1, source_target_pairs={{0,2},{1,3},{2,0},{3,1},{4,6},{5,7},{6,4},{7,5},{8,10},{9,11},{10,... | collective-permute-start | bytes 196616 | tf_op jit(solution)/shard_map/ppermute | solution.py:23
  17.6 9.8 %collective-permute-start.10 = (bf16[64,864]{1,0:T(8,128)(2,1)S(1)}, bf16[64,864]{1,0:T(8,128)(2,1)S(1)}, u32[]{:S(2)}, u32[]{:S(2)}) collective-permute-start(bf16[64,864]{1,0:T(8,128)(2,1)S(1)} %get-tuple-element.27), channel_id=1, source_target_pairs={{0,4},{4,0},{8,12},{12,8},{16,20},{20,16},{24,28},{28,24},{1,5},{5... | collective-permute-start | bytes 331784 | tf_op jit(solution)/shard_map/ppermute | solution.py:23
  18.9 3.3 %collective-permute-start.2 = (bf16[8,2,16,128]{3,2,1,0:T(8,128)(2,1)S(1)}, bf16[8,2,16,128]{3,2,1,0:T(8,128)(2,1)S(1)}, u32[]{:S(2)}, u32[]{:S(2)}) collective-permute-start(bf16[8,2,16,128]{3,2,1,0:T(8,128)(2,1)S(1)} %shard_map.69.refs_0_.refs_4_), channel_id=1, source_target_pairs={{0,1},{1,0},{2,3},{3,2},{4,5},{5,4},{6,7},{7,6},{8,9},{9,8},{10,11... | collective-permute-start | bytes 196616 | tf_op jit(solution)/shard_map/ppermute | solution.py:23
  19.4 2.9 %collective-permute-start.4 = (bf16[8,2,16,128]{3,2,1,0:T(8,128)(2,1)S(1)}, bf16[8,2,16,128]{3,2,1,0:T(8,128)(2,1)S(1)}, u32[]{:S(2)}, u32[]{:S(2)}) collective-permute-start(bf16[8,2,16,128]{3,2,1,0:T(8,128)(2,1)S(1)} %collective-permute-done.3.refs_2_.refs_6_), channel_id=1, source_target_pairs={{0,1},{1,0},{2,3},{3,2},{4,5},{5,4},{6,7},{7,6},{8,9},{9,8},{10,11... | collective-permute-start | bytes 196616 | tf_op jit(solution)/shard_map/ppermute | solution.py:23
  25.3 4.5 %collective-permute-start.8 = (bf16[2,1,4,8,512]{4,3,2,1,0:T(8,128)(2,1)S(1)}, bf16[2,1,4,8,512]{4,3,2,1,0:T(8,128)(2,1)S(1)}, u32[]{:S(2)}, u32[]{:S(2)}) collective-permute-start(bf16[2,1,4,8,512]{4,3,2,1,0:T(8,128)(2,1)S(1)} %get-tuple-element.23), channel_id=1, source_target_pairs={{0,2},{1,3},{2,0},{3,1},{4,6},{5,7},{6,4},{7,5},{8,10},{9,11},{10,... | collective-permute-start | bytes 196616 | tf_op jit(solution)/shard_map/ppermute | solution.py:23
  27.6 4.2 %collective-permute-start.11 = (bf16[32,864]{1,0:T(8,128)(2,1)S(1)}, bf16[32,864]{1,0:T(8,128)(2,1)S(1)}, u32[]{:S(2)}, u32[]{:S(2)}) collective-permute-start(bf16[32,864]{1,0:T(8,128)(2,1)S(1)} %get-tuple-element.29), channel_id=1, source_target_pairs={{0,8},{4,12},{8,0},{12,4},{16,24},{20,28},{24,16},{28,20},{1,9},{5... | collective-permute-start | bytes 165896 | tf_op jit(solution)/shard_map/ppermute | solution.py:23
  29.9 3.7 %collective-permute-start.9 = (bf16[1,1,4,8,512]{4,3,2,1,0:T(8,128)(2,1)S(1)}, bf16[1,1,4,8,512]{4,3,2,1,0:T(8,128)(2,1)S(1)}, u32[]{:S(2)}, u32[]{:S(2)}) collective-permute-start(bf16[1,1,4,8,512]{4,3,2,1,0:T(8,128)(2,1)S(1)} %get-tuple-element.25), channel_id=1, source_target_pairs={{0,1},{1,0},{2,3},{3,2},{4,5},{5,4},{6,7},{7,6},{8,9},{9,8},{10,11... | collective-permute-start | bytes 98312 | tf_op jit(solution)/shard_map/ppermute | solution.py:23
  31.9 5.1 %collective-permute-start.12 = (bf16[16,864]{1,0:T(8,128)(2,1)S(1)}, bf16[16,864]{1,0:T(8,128)(2,1)S(1)}, u32[]{:S(2)}, u32[]{:S(2)}) collective-permute-start(bf16[16,864]{1,0:T(8,128)(2,1)S(1)} %get-tuple-element.31), channel_id=1, source_target_pairs={{0,16},{4,20},{8,24},{12,28},{16,0},{20,4},{24,8},{28,12},{1,17},{... | collective-permute-start | bytes 82952 | tf_op jit(solution)/shard_map/ppermute | solution.py:23

commit v5 on v3

--- a/solution.py
+++ b/solution.py
@@ -375,14 +375,20 @@
     send_ref[...] = jnp.where(upper, total[:half], total[half:]).astype(BF16)
 
 
-def finish_kernel(keep_ref, got_ref, out_ref):
+def finish_kernel(keep_ref, got_ref, out_ref, held, leaving):
     part = out_ref.shape[4]
-    total = keep_ref[...] + got_ref[...].astype(F32)
+    copies = []
     for p in range(3):
+        at = slice(9 * p * part, 9 * (p + 1) * part)
+        total = keep_ref[:, at] + got_ref[:, at].astype(F32)
         for q in range(3):
             for r in range(3):
-                at = (9 * p + 3 * q + r) * part
-                out_ref[p, q, r] = total[:, at : at + part]
+                lane = (3 * q + r) * part
+                held[p, q, r] = total[:, lane : lane + part]
+        copies.append(pltpu.make_async_copy(held.at[p], out_ref.at[p], leaving.at[p]))
+        copies[-1].start()
+    for copy in copies:
+        copy.wait()
 
 
 def sum_kernel(*refs):
@@ -504,9 +510,15 @@
             (keep, got) if bit > 1 else (keep, got, outer),
         )
         got = swap(send, "grp", 2**bit)
-    (taps_grad,) = call(
-        finish_kernel, [shape((3, 3, 3, ch // m, ch // n), F32)], [], (keep, got), False
-    )
+    final = (3, 3, 3, ch // m, ch // n)
+    taps_grad = pl.pallas_call(
+        finish_kernel,
+        out_shape=shape(final, F32),
+        in_specs=[pl.BlockSpec(memory_space=pltpu.VMEM)] * 2,
+        out_specs=pl.BlockSpec(memory_space=pltpu.HBM),
+        scratch_shapes=[pltpu.VMEM(final, F32), pltpu.SemaphoreType.DMA((3,))],
+        compiler_params=pltpu.CompilerParams(vmem_limit_bytes=LIMIT),
+    )(*[pltpu.with_memory_space_constraint(v, pltpu.VMEM) for v in (keep, got)])
     return (grad_half, taps_grad)
 
 

time: 37.7 us -> 37.7 us (level)
    pallas_call x10 -> x9, Pallas kernels: 8.76 us -> 7.96 us  [call(): pl.pallas_call(kernel, out_shape=[pltpu.VMEM(v.shape, v.dtype) if placed...]
    pallas_call x0 -> x1, Pallas kernels: none -> 0.79 us  [work(): pl.pallas_call(finish_kernel, out_shape=shape(final, F32), in_specs=[pl.B...]
where the time goes in v5:
time: 37.7 us; the launch traced here: 37.5 us
  starting transfers between devices  16.6 us (44%)
  waiting for transfers between devices  10.3 us (27%)
  Pallas kernels  9.98 us (26%)
  between operations  0.71 us (2%)
    ppermute x12, starting transfers between devices, swap(): return lax.ppermute(value, axis, [(i, i ^ k) for i in range(n)])  11.8 us
    ppermute x12, waiting for transfers between devices, swap(): return lax.ppermute(value, axis, [(i, i ^ k) for i in range(n)])  8.2 us
    pallas_call x9, Pallas kernels, call(): pl.pallas_call(kernel, out_shape=[pltpu.VMEM(v.shape, v.dtype) if placed...  7.96 us
    ppermute x2, starting transfers between devices, shift(): return lax.ppermute(value, axis, [(i, (i + step) % n) for i in range(n)])  4.81 us
    ppermute x2, waiting for transfers between devices, shift(): return lax.ppermute(value, axis, [(i, (i + step) % n) for i in range(n)])  2.06 us
    pallas_call x1, Pallas kernels, fetch(): pl.pallas_call(fetch_kernel, out_shape=[pltpu.VMEM(shape, BF16) for shape...  1.23 us
    pallas_call x1, Pallas kernels, work(): pl.pallas_call(finish_kernel, out_shape=shape(final, F32), in_specs=[pl.B...  0.79 us
  transfers between devices with their start and end apart: 14, of which 7 were waited for; matrix products, arithmetic and copies ran while one was open for 0% of the time, Pallas kernels for 22%

profile of v5, /device:TPU:0, one launch (start us, length us, event | category | flops | bytes accessed | tf_op | source)
XLA Modules:
  0.0 37.5 jit_solution(9586625918472750560)
XLA Ops:
  0.6 1.0 %shard_map.68 = (bf16[16,2,16,128]{3,2,1,0:T(8,128)(2,1)S(1)}, bf16[4,2,16,128]{3,2,1,0:T(8,128)(2,1)S(1)}, bf16[4,2,16,128]{3,2,1,0:T(8,128)(2,1)S(1)}) custom-call(bf16[8,2,16,128]{3,2,1,0:T(8,128)(2,1)} %grad_ref.1, bf16[8,2,16,128]{3,2,1,0:T(8,128)(2,1)} %feat_ref.1), custom_call_target="tpu_custom_call" | custom-call | tf_op jit(solution)/shard_map/pallas_call | solution.py:404
  1.6 3.0 %collective-permute-start.6 = (bf16[16,2,16,128]{3,2,1,0:T(8,128)(2,1)S(1)}, bf16[16,2,16,128]{3,2,1,0:T(8,128)(2,1)S(1)}, u32[]{:S(2)}, u32[]{:S(2)}) collective-permute-start(bf16[16,2,16,128]{3,2,1,0:T(8,128)(2,1)S(1)} %get-tuple-element.19.refs_0_), channel_id=1, source_target_pairs={{0,2},{1,3},{2,0},{3,1},{4,6},{5,7},{6,4},{7,5},{8,10},{9,11},{10,... | collective-permute-start | bytes 393224 | tf_op jit(solution)/shard_map/ppermute | solution.py:23
  4.7 0.0 collective-permute-start.5
  4.7 3.5 %collective-permute-done.6.refs_2_ = bf16[16,2,16,128]{3,2,1,0:T(8,128)(2,1)S(1)} collective-permute-done((bf16[16,2,16,128]{3,2,1,0:T(8,128)(2,1)S(1)}, bf16[16,2,16,128]{3,2,1,0:T(8,128)(2,1)S(1)}, u32[]{:S(2)}, u32[]{:S(2)}) %collective-permute-start.6) | collective-permute-done | bytes 131104 | tf_op jit(solution)/shard_map/ppermute | solution.py:23
  8.2 0.0 collective-permute-start.7
  8.2 1.8 %collective-permute-start = (bf16[4,2,16,128]{3,2,1,0:T(8,128)(2,1)S(1)}, bf16[4,2,16,128]{3,2,1,0:T(8,128)(2,1)S(1)}, u32[]{:S(2)}, u32[]{:S(2)}) collective-permute-start(bf16[4,2,16,128]{3,2,1,0:T(8,128)(2,1)S(1)} %get-tuple-element.17), channel_id=1, source_target_pairs={{0,4},{4,8},{8,12},{12,16},{16,20},{20,24},{24,28},{28,0},{1,5},{5... | collective-permute-start | bytes 98312 | tf_op jit(solution)/shard_map/ppermute | solution.py:28
  9.9 3.0 %collective-permute-start.1 = (bf16[4,2,16,128]{3,2,1,0:T(8,128)(2,1)S(1)}, bf16[4,2,16,128]{3,2,1,0:T(8,128)(2,1)S(1)}, u32[]{:S(2)}, u32[]{:S(2)}) collective-permute-start(bf16[4,2,16,128]{3,2,1,0:T(8,128)(2,1)S(1)} %get-tuple-element.18), channel_id=1, source_target_pairs={{0,28},{4,0},{8,4},{12,8},{16,12},{20,16},{24,20},{28,24},{1,29},{... | collective-permute-start | bytes 98312 | tf_op jit(solution)/shard_map/ppermute | solution.py:28
  13.0 2.1 %collective-permute-done.refs_0_ = bf16[4,2,16,128]{3,2,1,0:T(8,128)(2,1)S(1)} collective-permute-done((bf16[4,2,16,128]{3,2,1,0:T(8,128)(2,1)S(1)}, bf16[4,2,16,128]{3,2,1,0:T(8,128)(2,1)S(1)}, u32[]{:S(2)}, u32[]{:S(2)}) %collective-permute-start) | collective-permute-done | bytes 32800 | tf_op jit(solution)/shard_map/ppermute | solution.py:28
  15.0 0.0 collective-permute-done.1.refs_1_
  15.1 1.6 %collective-permute-start.3 = (bf16[8,2,16,128]{3,2,1,0:T(8,128)(2,1)S(1)}, bf16[8,2,16,128]{3,2,1,0:T(8,128)(2,1)S(1)}, u32[]{:S(2)}, u32[]{:S(2)}) collective-permute-start(bf16[8,2,16,128]{3,2,1,0:T(8,128)(2,1)S(1)} %shard_map.69.refs_0_.refs_4_), channel_id=1, source_target_pairs={{0,2},{1,3},{2,0},{3,1},{4,6},{5,7},{6,4},{7,5},{8,10},{9,11},{10,... | collective-permute-start | bytes 196616 | tf_op jit(solution)/shard_map/ppermute | solution.py:23
  16.6 0.0 collective-permute-done.5.refs_1_
  16.6 0.0 collective-permute-done.7.refs_3_
  16.6 1.0 %shard_map.74 = (f32[64,864]{1,0:T(8,128)S(1)}, bf16[64,864]{1,0:T(8,128)(2,1)S(1)}) custom-call(bf16[16,2,16,128]{3,2,1,0:T(8,128)(2,1)S(1)} %get-tuple-element.19.refs_0_, bf16[16,2,16,128]{3,2,1,0:T(8,128)(2,1)S(1)} %collective-permute-done.5.refs_1_, bf16[16,2,16,128]{3,2,1,0:T(8,128)(2,1)S(1)} %collective-permute-done.6.refs_2_, ...), custom_call_target="tpu_custom_call" | custom-call | tf_op jit(solution)/shard_map/pallas_call | solution.py:404
  17.6 1.3 %collective-permute-start.11 = (bf16[64,864]{1,0:T(8,128)(2,1)S(1)}, bf16[64,864]{1,0:T(8,128)(2,1)S(1)}, u32[]{:S(2)}, u32[]{:S(2)}) collective-permute-start(bf16[64,864]{1,0:T(8,128)(2,1)S(1)} %get-tuple-element.27), channel_id=1, source_target_pairs={{0,4},{4,0},{8,12},{12,8},{16,20},{20,16},{24,28},{28,24},{1,5},{5... | collective-permute-start | bytes 331784 | tf_op jit(solution)/shard_map/ppermute | solution.py:23
  18.9 0.0 collective-permute-start.2
  18.9 0.5 %collective-permute-done.3.refs_2_.refs_6_ = bf16[8,2,16,128]{3,2,1,0:T(8,128)(2,1)S(1)} collective-permute-done((bf16[8,2,16,128]{3,2,1,0:T(8,128)(2,1)S(1)}, bf16[8,2,16,128]{3,2,1,0:T(8,128)(2,1)S(1)}, u32[]{:S(2)}, u32[]{:S(2)}) %collective-permute-start.3) | collective-permute-done | bytes 65568 | tf_op jit(solution)/shard_map/ppermute | solution.py:23
  19.4 0.0 collective-permute-start.4
  19.4 0.7 %collective-permute-done.2.refs_1_.refs_5_ = bf16[8,2,16,128]{3,2,1,0:T(8,128)(2,1)S(1)} collective-permute-done((bf16[8,2,16,128]{3,2,1,0:T(8,128)(2,1)S(1)}, bf16[8,2,16,128]{3,2,1,0:T(8,128)(2,1)S(1)}, u32[]{:S(2)}, u32[]{:S(2)}) %collective-permute-start.2) | collective-permute-done | bytes 65568 | tf_op jit(solution)/shard_map/ppermute | solution.py:23
  20.2 0.5 %collective-permute-done.4.refs_3_.refs_7_ = bf16[8,2,16,128]{3,2,1,0:T(8,128)(2,1)S(1)} collective-permute-done((bf16[8,2,16,128]{3,2,1,0:T(8,128)(2,1)S(1)}, bf16[8,2,16,128]{3,2,1,0:T(8,128)(2,1)S(1)}, u32[]{:S(2)}, u32[]{:S(2)}) %collective-permute-start.4) | collective-permute-done | bytes 65568 | tf_op jit(solution)/shard_map/ppermute | solution.py:23
  20.6 0.6 %shard_map.75.refs_2_ = f32[2,64,288]{2,1,0:T(8,128)S(1)} custom-call(bf16[16,2,16,128]{3,2,1,0:T(8,128)(2,1)S(1)} %get-tuple-element.19.refs_0_, bf16[16,2,16,128]{3,2,1,0:T(8,128)(2,1)S(1)} %collective-permute-done.5.refs_1_, bf16[16,2,16,128]{3,2,1,0:T(8,128)(2,1)S(1)} %collective-permute-done.6.refs_2_, ...), custom_call_target="tpu_custom_call" | custom-call | tf_op jit(solution)/shard_map/pallas_call | solution.py:404
  21.3 1.2 %collective-permute-done.11.refs_1_ = bf16[64,864]{1,0:T(8,128)(2,1)S(1)} collective-permute-done((bf16[64,864]{1,0:T(8,128)(2,1)S(1)}, bf16[64,864]{1,0:T(8,128)(2,1)S(1)}, u32[]{:S(2)}, u32[]{:S(2)}) %collective-permute-start.11) | collective-permute-done | bytes 110624 | tf_op jit(solution)/shard_map/ppermute | solution.py:23
  22.5 0.1 shard_map.76
  22.6 0.8 %collective-permute-start.12 = (bf16[32,864]{1,0:T(8,128)(2,1)S(1)}, bf16[32,864]{1,0:T(8,128)(2,1)S(1)}, u32[]{:S(2)}, u32[]{:S(2)}) collective-permute-start(bf16[32,864]{1,0:T(8,128)(2,1)S(1)} %get-tuple-element.29), channel_id=1, source_target_pairs={{0,8},{4,12},{8,0},{12,4},{16,24},{20,28},{24,16},{28,20},{1,9},{5... | collective-permute-start | bytes 165896 | tf_op jit(solution)/shard_map/ppermute | solution.py:23
  23.4 1.2 %shard_map.70 = (bf16[3,3,3,128,128]{4,3,2,1,0:T(8,128)(2,1)S(1)}, bf16[2,2,2,128,128]{4,3,2,1,0:T(8,128)(2,1)S(1)}) custom-call(bf16[3,3,3,128,128]{4,3,2,1,0:T(8,128)(2,1)} %refs_0_.1, bf16[2,2,2,512,128]{4,3,2,1,0:T(8,128)(2,1)} %refs_1_.1), custom_call_target="tpu_custom_call" | custom-call | tf_op jit(solution)/shard_map/pallas_call | solution.py:416
  24.7 1.6 %shard_map.71.refs_4_ = f32[2,10,8,8,128]{4,3,2,1,0:T(8,128)S(1)} custom-call(bf16[16,2,16,128]{3,2,1,0:T(8,128)(2,1)S(1)} %get-tuple-element.19.refs_0_, bf16[16,2,16,128]{3,2,1,0:T(8,128)(2,1)S(1)} %collective-permute-done.5.refs_1_, bf16[16,2,16,128]{3,2,1,0:T(8,128)(2,1)S(1)} %collective-permute-done.6.refs_2_, ...), custom_call_target="tpu_custom_call" | custom-call | tf_op jit(solution)/shard_map/pallas_call | solution.py:404
  26.2 3.0 %shard_map.72 = (f32[1,4,8,512]{3,2,1,0:T(8,128)S(1)}, bf16[1,4,8,512]{3,2,1,0:T(8,128)(2,1)S(1)}, bf16[1,4,8,512]{3,2,1,0:T(8,128)(2,1)S(1)}, bf16[1,4,8,512]{3,2,1,0:T(8,128)(2,1)S(1)}) custom-call(bf16[8,2,16,128]{3,2,1,0:T(8,128)(2,1)S(1)} %shard_map.69.refs_0_.refs_4_, bf16[8,2,16,128]{3,2,1,0:T(8,128)(2,1)S(1)} %collective-permute-done.2.refs_1_.refs_5_, ...), custom_call_target="tpu_custom_call" | custom-call | tf_op jit(solution)/shard_map/pallas_call | solution.py:404
  29.2 0.1 collective-permute-start.8
  29.3 0.6 %collective-permute-start.9 = (bf16[1,4,8,512]{3,2,1,0:T(8,128)(2,1)S(1)}, bf16[1,4,8,512]{3,2,1,0:T(8,128)(2,1)S(1)}, u32[]{:S(2)}, u32[]{:S(2)}) collective-permute-start(bf16[1,4,8,512]{3,2,1,0:T(8,128)(2,1)S(1)} %get-tuple-element.24), channel_id=1, source_target_pairs={{0,2},{1,3},{2,0},{3,1},{4,6},{5,7},{6,4},{7,5},{8,10},{9,11},{10,... | collective-permute-start | bytes 98312 | tf_op jit(solution)/shard_map/ppermute | solution.py:23
  29.9 1.2 %collective-permute-start.10 = (bf16[1,4,8,512]{3,2,1,0:T(8,128)(2,1)S(1)}, bf16[1,4,8,512]{3,2,1,0:T(8,128)(2,1)S(1)}, u32[]{:S(2)}, u32[]{:S(2)}) collective-permute-start(bf16[1,4,8,512]{3,2,1,0:T(8,128)(2,1)S(1)} %get-tuple-element.25), channel_id=1, source_target_pairs={{0,3},{1,2},{2,1},{3,0},{4,7},{5,6},{6,5},{7,4},{8,11},{9,10},{10,... | collective-permute-start | bytes 98312 | tf_op jit(solution)/shard_map/ppermute | solution.py:23
  31.2 0.0 collective-permute-done.12.refs_1_
  31.2 3.1 %collective-permute-start.13 = (bf16[16,864]{1,0:T(8,128)(2,1)S(1)}, bf16[16,864]{1,0:T(8,128)(2,1)S(1)}, u32[]{:S(2)}, u32[]{:S(2)}) collective-permute-start(bf16[16,864]{1,0:T(8,128)(2,1)S(1)} %get-tuple-element.31), channel_id=1, source_target_pairs={{0,16},{4,20},{8,24},{12,28},{16,0},{20,4},{24,8},{28,12},{1,17},{... | collective-permute-start | bytes 82952 | tf_op jit(solution)/shard_map/ppermute | solution.py:23
  34.3 0.0 collective-permute-done.8.refs_1_
  34.3 0.0 collective-permute-done.9.refs_2_
  34.3 0.0 collective-permute-done.10.refs_3_
  34.3 0.6 %shard_map.73 = bf16[1,4,8,512]{3,2,1,0:T(8,128)(2,1)} custom-call(f32[1,4,8,512]{3,2,1,0:T(8,128)S(1)} %get-tuple-element.22.refs_0_, bf16[1,4,8,512]{3,2,1,0:T(8,128)(2,1)S(1)} %collective-permute-done.8.refs_1_, bf16[1,4,8,512]{3,2,1,0:T(8,128)(2,1)S(1)} %collective-permute-done.9.refs_2_, bf16[1,4,8,512]{3,2,1,0:T(8,128)(2,1)S(1)} %collective-permute-done.10.refs_3_), custom_call_target="tpu_custom_call" | custom-call | tf_op jit(solution)/shard_map/pallas_call | solution.py:404
  35.0 1.8 %collective-permute-done.13.got_ref = bf16[16,864]{1,0:T(8,128)(2,1)S(1)} collective-permute-done((bf16[16,864]{1,0:T(8,128)(2,1)S(1)}, bf16[16,864]{1,0:T(8,128)(2,1)S(1)}, u32[]{:S(2)}, u32[]{:S(2)}) %collective-permute-start.13) | collective-permute-done | bytes 27680 | tf_op jit(solution)/shard_map/ppermute | solution.py:23
  36.7 0.8 %shard_map.78 = f32[3,3,3,16,32]{4,3,2,1,0:T(8,128)} custom-call(f32[16,864]{1,0:T(8,128)S(1)} %get-tuple-element.30.keep_ref, bf16[16,864]{1,0:T(8,128)(2,1)S(1)} %collective-permute-done.13.got_ref), custom_call_target="tpu_custom_call" | custom-call | tf_op jit(solution)/shard_map/pallas_call | solution.py:514
  (2 shorter events, 0.0 us)
Async XLA Ops:
  1.6 6.5 %collective-permute-start.6 = (bf16[16,2,16,128]{3,2,1,0:T(8,128)(2,1)S(1)}, bf16[16,2,16,128]{3,2,1,0:T(8,128)(2,1)S(1)}, u32[]{:S(2)}, u32[]{:S(2)}) collective-permute-start(bf16[16,2,16,128]{3,2,1,0:T(8,128)(2,1)S(1)} %get-tuple-element.19.refs_0_), channel_id=1, source_target_pairs={{0,2},{1,3},{2,0},{3,1},{4,6},{5,7},{6,4},{7,5},{8,10},{9,11},{10,... | collective-permute-start | bytes 393224 | tf_op jit(solution)/shard_map/ppermute | solution.py:23
  4.7 12.0 %collective-permute-start.5 = (bf16[16,2,16,128]{3,2,1,0:T(8,128)(2,1)S(1)}, bf16[16,2,16,128]{3,2,1,0:T(8,128)(2,1)S(1)}, u32[]{:S(2)}, u32[]{:S(2)}) collective-permute-start(bf16[16,2,16,128]{3,2,1,0:T(8,128)(2,1)S(1)} %get-tuple-element.19.refs_0_), channel_id=1, source_target_pairs={{0,1},{1,0},{2,3},{3,2},{4,5},{5,4},{6,7},{7,6},{8,9},{9,8},{10,11... | collective-permute-start | bytes 393224 | tf_op jit(solution)/shard_map/ppermute | solution.py:23
  8.2 8.5 %collective-permute-start.7 = (bf16[16,2,16,128]{3,2,1,0:T(8,128)(2,1)S(1)}, bf16[16,2,16,128]{3,2,1,0:T(8,128)(2,1)S(1)}, u32[]{:S(2)}, u32[]{:S(2)}) collective-permute-start(bf16[16,2,16,128]{3,2,1,0:T(8,128)(2,1)S(1)} %collective-permute-done.6.refs_2_), channel_id=1, source_target_pairs={{0,1},{1,0},{2,3},{3,2},{4,5},{5,4},{6,7},{7,6},{8,9},{9,8},{10,11... | collective-permute-start | bytes 393224 | tf_op jit(solution)/shard_map/ppermute | solution.py:23
  8.2 6.9 %collective-permute-start = (bf16[4,2,16,128]{3,2,1,0:T(8,128)(2,1)S(1)}, bf16[4,2,16,128]{3,2,1,0:T(8,128)(2,1)S(1)}, u32[]{:S(2)}, u32[]{:S(2)}) collective-permute-start(bf16[4,2,16,128]{3,2,1,0:T(8,128)(2,1)S(1)} %get-tuple-element.17), channel_id=1, source_target_pairs={{0,4},{4,8},{8,12},{12,16},{16,20},{20,24},{24,28},{28,0},{1,5},{5... | collective-permute-start | bytes 98312 | tf_op jit(solution)/shard_map/ppermute | solution.py:28
  9.9 5.1 %collective-permute-start.1 = (bf16[4,2,16,128]{3,2,1,0:T(8,128)(2,1)S(1)}, bf16[4,2,16,128]{3,2,1,0:T(8,128)(2,1)S(1)}, u32[]{:S(2)}, u32[]{:S(2)}) collective-permute-start(bf16[4,2,16,128]{3,2,1,0:T(8,128)(2,1)S(1)} %get-tuple-element.18), channel_id=1, source_target_pairs={{0,28},{4,0},{8,4},{12,8},{16,12},{20,16},{24,20},{28,24},{1,29},{... | collective-permute-start | bytes 98312 | tf_op jit(solution)/shard_map/ppermute | solution.py:28
  15.1 4.3 %collective-permute-start.3 = (bf16[8,2,16,128]{3,2,1,0:T(8,128)(2,1)S(1)}, bf16[8,2,16,128]{3,2,1,0:T(8,128)(2,1)S(1)}, u32[]{:S(2)}, u32[]{:S(2)}) collective-permute-start(bf16[8,2,16,128]{3,2,1,0:T(8,128)(2,1)S(1)} %shard_map.69.refs_0_.refs_4_), channel_id=1, source_target_pairs={{0,2},{1,3},{2,0},{3,1},{4,6},{5,7},{6,4},{7,5},{8,10},{9,11},{10,... | collective-permute-start | bytes 196616 | tf_op jit(solution)/shard_map/ppermute | solution.py:23
  17.6 4.9 %collective-permute-start.11 = (bf16[64,864]{1,0:T(8,128)(2,1)S(1)}, bf16[64,864]{1,0:T(8,128)(2,1)S(1)}, u32[]{:S(2)}, u32[]{:S(2)}) collective-permute-start(bf16[64,864]{1,0:T(8,128)(2,1)S(1)} %get-tuple-element.27), channel_id=1, source_target_pairs={{0,4},{4,0},{8,12},{12,8},{16,20},{20,16},{24,28},{28,24},{1,5},{5... | collective-permute-start | bytes 331784 | tf_op jit(solution)/shard_map/ppermute | solution.py:23
  18.9 1.3 %collective-permute-start.2 = (bf16[8,2,16,128]{3,2,1,0:T(8,128)(2,1)S(1)}, bf16[8,2,16,128]{3,2,1,0:T(8,128)(2,1)S(1)}, u32[]{:S(2)}, u32[]{:S(2)}) collective-permute-start(bf16[8,2,16,128]{3,2,1,0:T(8,128)(2,1)S(1)} %shard_map.69.refs_0_.refs_4_), channel_id=1, source_target_pairs={{0,1},{1,0},{2,3},{3,2},{4,5},{5,4},{6,7},{7,6},{8,9},{9,8},{10,11... | collective-permute-start | bytes 196616 | tf_op jit(solution)/shard_map/ppermute | solution.py:23
  19.4 1.3 %collective-permute-start.4 = (bf16[8,2,16,128]{3,2,1,0:T(8,128)(2,1)S(1)}, bf16[8,2,16,128]{3,2,1,0:T(8,128)(2,1)S(1)}, u32[]{:S(2)}, u32[]{:S(2)}) collective-permute-start(bf16[8,2,16,128]{3,2,1,0:T(8,128)(2,1)S(1)} %collective-permute-done.3.refs_2_.refs_6_), channel_id=1, source_target_pairs={{0,1},{1,0},{2,3},{3,2},{4,5},{5,4},{6,7},{7,6},{8,9},{9,8},{10,11... | collective-permute-start | bytes 196616 | tf_op jit(solution)/shard_map/ppermute | solution.py:23
  22.6 8.6 %collective-permute-start.12 = (bf16[32,864]{1,0:T(8,128)(2,1)S(1)}, bf16[32,864]{1,0:T(8,128)(2,1)S(1)}, u32[]{:S(2)}, u32[]{:S(2)}) collective-permute-start(bf16[32,864]{1,0:T(8,128)(2,1)S(1)} %get-tuple-element.29), channel_id=1, source_target_pairs={{0,8},{4,12},{8,0},{12,4},{16,24},{20,28},{24,16},{28,20},{1,9},{5... | collective-permute-start | bytes 165896 | tf_op jit(solution)/shard_map/ppermute | solution.py:23
  29.2 5.1 %collective-permute-start.8 = (bf16[1,4,8,512]{3,2,1,0:T(8,128)(2,1)S(1)}, bf16[1,4,8,512]{3,2,1,0:T(8,128)(2,1)S(1)}, u32[]{:S(2)}, u32[]{:S(2)}) collective-permute-start(bf16[1,4,8,512]{3,2,1,0:T(8,128)(2,1)S(1)} %get-tuple-element.23), channel_id=1, source_target_pairs={{0,1},{1,0},{2,3},{3,2},{4,5},{5,4},{6,7},{7,6},{8,9},{9,8},{10,11... | collective-permute-start | bytes 98312 | tf_op jit(solution)/shard_map/ppermute | solution.py:23
  29.3 5.0 %collective-permute-start.9 = (bf16[1,4,8,512]{3,2,1,0:T(8,128)(2,1)S(1)}, bf16[1,4,8,512]{3,2,1,0:T(8,128)(2,1)S(1)}, u32[]{:S(2)}, u32[]{:S(2)}) collective-permute-start(bf16[1,4,8,512]{3,2,1,0:T(8,128)(2,1)S(1)} %get-tuple-element.24), channel_id=1, source_target_pairs={{0,2},{1,3},{2,0},{3,1},{4,6},{5,7},{6,4},{7,5},{8,10},{9,11},{10,... | collective-permute-start | bytes 98312 | tf_op jit(solution)/shard_map/ppermute | solution.py:23
  29.9 4.4 %collective-permute-start.10 = (bf16[1,4,8,512]{3,2,1,0:T(8,128)(2,1)S(1)}, bf16[1,4,8,512]{3,2,1,0:T(8,128)(2,1)S(1)}, u32[]{:S(2)}, u32[]{:S(2)}) collective-permute-start(bf16[1,4,8,512]{3,2,1,0:T(8,128)(2,1)S(1)} %get-tuple-element.25), channel_id=1, source_target_pairs={{0,3},{1,2},{2,1},{3,0},{4,7},{5,6},{6,5},{7,4},{8,11},{9,10},{10,... | collective-permute-start | bytes 98312 | tf_op jit(solution)/shard_map/ppermute | solution.py:23
  31.2 5.5 %collective-permute-start.13 = (bf16[16,864]{1,0:T(8,128)(2,1)S(1)}, bf16[16,864]{1,0:T(8,128)(2,1)S(1)}, u32[]{:S(2)}, u32[]{:S(2)}) collective-permute-start(bf16[16,864]{1,0:T(8,128)(2,1)S(1)} %get-tuple-element.31), channel_id=1, source_target_pairs={{0,16},{4,20},{8,24},{12,28},{16,0},{20,4},{24,8},{28,12},{1,17},{... | collective-permute-start | bytes 82952 | tf_op jit(solution)/shard_map/ppermute | solution.py:23
